TPU v7x, 32 devices: a whole 2x2x4 slice. The times are simulated.
32 devices in a mesh: row: 2 (over core), col: 16 (over z, y, x).
Axes of the slice: x: 2, y: 2, z: 4, core: 2. Of those that a mesh axis runs over, the one named last changes fastest.
Arguments:
- node_feats: bfloat16 [256, 25, 128], P(('row', 'col')), may hold values from -6 to 6
- grad_out: bfloat16 [256, 25, 128], P(('row', 'col')), may hold values from -6 to 6
- edge_src: int32 [2, 16, 512], P('row', 'col'), may hold values from 0 to 15
- edge_tgt: int32 [2, 16, 512], P('row', 'col'), may hold values from 0 to 127
- edge_counts: int32 [2, 16], P('row', 'col'), may hold values from 64 to 512, as said below
- wigner: bfloat16 [2, 16, 512, 475], P('row', 'col'), may hold values from -1 to 1, as said below
- w_zero: bfloat16 [1280, 640], replicated, may hold values from -0.15625 to 0.15625
- w_one: bfloat16 [2, 1024, 512], replicated, may hold values from -0.1875 to 0.1875
- w_two: bfloat16 [2, 768, 384], replicated, may hold values from -0.21875 to 0.21875
Outputs:
- grad_nodes: float32 [256, 25, 128], P(('row', 'col'))
Inputs may be any that keep to these rules, and one draw needn't show every extreme that they name: `edge_counts`: slots at or past a tile's count are ignored. In every row of tiles one tile holds exactly 512 edges. `edge_src`: slot values at or past the tile's count are arbitrary but in range. `edge_tgt`: slot values at or past the tile's count are arbitrary but in range. `wigner`: for every degree l, the rows of orders -2..2 (as far as l allows) hold the matching rows of an orthogonal (2l+1) x (2l+1) block in the columns of degree l, column index l*l + l + m; all other entries are zero.
All inputs are finite; a program needn't handle non-finite values.
Results may differ from a plain program's by a relative error of at most 0.015.
Values may be sent and summed in bfloat16 or wider, within the bound.
No kernel may reach another device: no remote copies, remote signals or barrier semaphores. Data moves between devices by JAX's collectives and lax.ppermute only.
A program may use at most 64 MiB of HBM per device.

v0:
```python
import jax
import jax.numpy as jnp
from jax import lax
from jax.sharding import PartitionSpec as P

E_CAP = 512
C = 128
COEF = 25


def so2_apply(edge_in, w_zero, w_one, w_two):
    edge_count = edge_in.shape[0]
    zero_part = jnp.dot(
        edge_in[:, 0:5].reshape(edge_count, -1), w_zero, preferred_element_type=jnp.float32
    )
    outputs = [zero_part.reshape(edge_count, 5, -1)]
    for first_row, row_count, weights in ((5, 4, w_one), (13, 3, w_two)):
        plus_part = edge_in[:, first_row : first_row + row_count].reshape(edge_count, -1)
        minus_part = edge_in[:, first_row + row_count : first_row + 2 * row_count].reshape(
            edge_count, -1
        )
        stacked = jnp.concatenate([plus_part, minus_part], axis=0)
        real_out = jnp.dot(stacked, weights[0], preferred_element_type=jnp.float32)
        imag_out = jnp.dot(stacked, weights[1], preferred_element_type=jnp.float32)
        outputs.append(
            (real_out[:edge_count] - imag_out[edge_count:]).reshape(edge_count, row_count, -1)
        )
        outputs.append(
            (real_out[edge_count:] + imag_out[:edge_count]).reshape(edge_count, row_count, -1)
        )
    return jnp.concatenate(outputs, axis=1)


def so2_transpose(grad_y, w_zero, w_one, w_two):
    edge_count = grad_y.shape[0]
    zero_part = jnp.dot(
        grad_y[:, 0:5].reshape(edge_count, -1), w_zero.T, preferred_element_type=jnp.float32
    )
    outputs = [zero_part.reshape(edge_count, 5, -1)]
    for first_row, row_count, weights in ((5, 4, w_one), (13, 3, w_two)):
        plus_grad = grad_y[:, first_row : first_row + row_count].reshape(edge_count, -1)
        minus_grad = grad_y[:, first_row + row_count : first_row + 2 * row_count].reshape(
            edge_count, -1
        )
        stacked = jnp.concatenate([plus_grad, minus_grad], axis=0)
        real_back = jnp.dot(stacked, weights[0].T, preferred_element_type=jnp.float32)
        imag_back = jnp.dot(stacked, weights[1].T, preferred_element_type=jnp.float32)
        outputs.append(
            (real_back[:edge_count] + imag_back[edge_count:]).reshape(edge_count, row_count, -1)
        )
        outputs.append(
            (real_back[edge_count:] - imag_back[:edge_count]).reshape(edge_count, row_count, -1)
        )
    return jnp.concatenate(outputs, axis=1)


def edge_grads(src_feats, tgt_feats, cotangent, matrix, weights):
    w_zero, w_one, w_two = weights

    def rotate(values):
        return jnp.einsum("ekj,ejc->ekc", matrix, values, preferred_element_type=jnp.float32)

    def unrotate(values):
        return jnp.einsum("ekj,ekc->ejc", matrix, values, preferred_element_type=jnp.float32)

    edge_in = jnp.concatenate([rotate(src_feats), rotate(tgt_feats)], axis=2).astype(jnp.bfloat16)
    rotated_cot = rotate(cotangent).astype(jnp.bfloat16)
    output = so2_apply(edge_in, w_zero, w_one, w_two)
    scalar = output[:, 0]
    gating = jax.nn.sigmoid(scalar)
    gate_slope = gating * (1.0 - gating)
    higher = rotated_cot[:, 1:].astype(jnp.float32)
    gate_grad = jnp.sum(higher * output[:, 1:], axis=1)
    first_cot = rotated_cot[:, 0].astype(jnp.float32)
    scalar_grad = first_cot * (gating + scalar * gate_slope) + gate_grad * gate_slope
    grad_y = jnp.concatenate([scalar_grad[:, None], gating[:, None] * higher], axis=1).astype(
        jnp.bfloat16
    )
    grad_in = so2_transpose(grad_y, w_zero, w_one, w_two).astype(jnp.bfloat16)
    channels = cotangent.shape[2]
    grad_src = unrotate(grad_in[:, :, :channels]).astype(jnp.bfloat16)
    grad_tgt = unrotate(grad_in[:, :, channels:]).astype(jnp.bfloat16)
    return (grad_src, grad_tgt)


def run_edges(
    source_list,
    target_list,
    rotations,
    source_feats,
    target_feats,
    target_cot,
    upper,
    totals,
    weights,
):
    block_size = min(128, E_CAP)
    source_list = jnp.concatenate([source_list, jnp.zeros((block_size,), jnp.int32)])
    target_list = jnp.concatenate([target_list, jnp.zeros((block_size,), jnp.int32)])
    rotations = jnp.concatenate(
        [rotations, jnp.zeros((block_size, rotations.shape[1]), rotations.dtype)]
    )
    target_ids = jnp.arange(target_feats.shape[0], dtype=jnp.int32)
    source_ids = jnp.arange(source_feats.shape[0], dtype=jnp.int32)
    block_count = (upper + block_size - 1) // block_size

    def block_step(block_index, running):
        start_slot = block_index * block_size
        source_rows = lax.dynamic_slice_in_dim(source_list, start_slot, block_size)
        target_rows = lax.dynamic_slice_in_dim(target_list, start_slot, block_size)
        matrix = lax.dynamic_slice_in_dim(rotations, start_slot, block_size, 0).reshape(
            block_size, 19, 25
        )
        in_range = start_slot + jnp.arange(block_size, dtype=jnp.int32) < upper
        grad_src, grad_tgt = edge_grads(
            source_feats[source_rows],
            target_feats[target_rows],
            target_cot[target_rows],
            matrix,
            weights,
        )
        target_hot = ((target_rows[None, :] == target_ids[:, None]) & in_range[None, :]).astype(
            jnp.bfloat16
        )
        source_hot = ((source_rows[None, :] == source_ids[:, None]) & in_range[None, :]).astype(
            jnp.bfloat16
        )
        new_target = running[0] + jnp.dot(
            target_hot, grad_tgt.reshape(block_size, -1), preferred_element_type=jnp.float32
        )
        new_source = running[1] + jnp.dot(
            source_hot, grad_src.reshape(block_size, -1), preferred_element_type=jnp.float32
        )
        return (new_target, new_source)

    return lax.fori_loop(0, block_count, block_step, totals)


def rounded(values):
    narrow = lax.optimization_barrier(values.astype(jnp.bfloat16))
    return narrow.astype(jnp.float32)


def local(node_feats, grad_out, edge_src, edge_tgt, edge_counts, wigner, w_zero, w_one, w_two):
    target_cot, target_feats = (
        lax.all_gather(grad_out, "col", axis=0, tiled=True),
        lax.all_gather(node_feats, "col", axis=0, tiled=True),
    )
    source_feats = lax.all_gather(node_feats, "row", axis=0, tiled=True)
    weights = (w_zero, w_one, w_two)
    own_src = edge_src[0, 0]
    own_tgt = edge_tgt[0, 0]
    own_count = edge_counts[0, 0]
    own_rot = wigner[0, 0]
    empty_target = jnp.zeros((target_feats.shape[0], COEF * C), jnp.float32)
    empty_source = jnp.zeros((source_feats.shape[0], COEF * C), jnp.float32)
    target_sum, source_sum = run_edges(
        own_src,
        own_tgt,
        own_rot,
        source_feats,
        target_feats,
        target_cot,
        own_count,
        (empty_target, empty_source),
        weights,
    )
    own_part = lax.psum_scatter(
        rounded(target_sum).astype(jnp.bfloat16), "col", scatter_dimension=0, tiled=True
    ).astype(jnp.float32)
    cross_part = lax.psum_scatter(
        rounded(source_sum).astype(jnp.bfloat16), "row", scatter_dimension=0, tiled=True
    ).astype(jnp.float32)
    return (own_part + cross_part).reshape(own_part.shape[0], COEF, C)


def solution(mesh):
    placed = (
        P(("row", "col"), None, None),
        P(("row", "col"), None, None),
        P("row", "col", None),
        P("row", "col", None),
        P("row", "col"),
        P("row", "col", None, None),
        P(),
        P(),
        P(),
    )
    return jax.shard_map(
        local, mesh=mesh, in_specs=placed, out_specs=P(("row", "col"), None, None), check_vma=False
    )
```

profile of v0, /device:TPU:0, one launch (start us, length us, event | category | flops | bytes accessed | tf_op | source)
XLA Modules:
  0.0 459.1 jit_solution(18360474345674955324)
XLA Ops:
  7.2 2.3 all_gather.10
  9.5 47.5 %all_gather.11 = bf16[128,25,128]{2,0,1:T(8,128)(2,1)S(1)} all-gather(bf16[8,25,128]{2,0,1:T(8,128)(2,1)} %param.11), channel_id=1, replica_groups=mesh['row'=2,'col'=16] {'col'}, dimensions={0}, use_global_device_ids=true | all-gather | bytes 870400 | tf_op jit(solution)/shard_map/all_gather | solution.py:147
  58.4 40.6 %all_gather.9 = bf16[128,25,128]{2,0,1:T(8,128)(2,1)S(1)} all-gather(bf16[8,25,128]{2,0,1:T(8,128)(2,1)S(1)} %copy-done.18), channel_id=1, replica_groups=mesh['row'=2,'col'=16] {'col'}, dimensions={0}, use_global_device_ids=true | all-gather | bytes 870400 | tf_op jit(solution)/shard_map/all_gather | solution.py:146
  99.1 1.5 copy.203
  100.6 1.6 copy.205
  102.2 1.2 copy.206
  103.4 1.1 concatenate.37
  105.2 1.3 broadcast_in_dim.8
  106.5 108.2 %while.13 = (s32[]{:T(128)}, f32[128,3200]{1,0:T(8,128)}, f32[16,3200]{1,0:T(8,128)}, s32[]{:T(128)}, s32[640]{0:T(1024)S(1)}, /*index=5*/s32[]{:T(128)}, bf16[6...) while((s32[]{:T(128)}, f32[128,3200]{1,0:T(8,128)}, ...), condition=%wide.region_2.3_spmd.clone, body=%wide.region_0.2_spmd.clone.sunk | while | flops 2303878144 | bytes 139214816 | solution.py:136
  109.7 2.0 gather_fusion.2
  113.3 2.0 gather_fusion.1
  117.6 1.2 copy.263
  121.2 1.3 fusion.161
  123.7 1.7 copy.265
  125.4 1.7 copy.266
  128.0 1.1 copy.268
  129.0 1.5 fusion.158
  130.5 1.5 fusion.157
  132.6 2.1 constant_dynamic-update-slice_fusion.22
  139.9 1.1 copy.281
  141.0 1.7 copy.282
  142.7 1.7 copy.283
  146.3 2.9 copy.271
  152.9 1.6 copy.285
  154.5 1.6 copy.284
  157.3 3.2 convolution_add_fusion.4
  163.7 2.0 gather_fusion.2
  167.3 2.0 gather_fusion.1
  171.6 1.2 copy.263
  175.2 1.3 fusion.161
  177.7 1.7 copy.265
  179.4 1.7 copy.266
  182.0 1.1 copy.268
  183.0 1.5 fusion.158
  184.5 1.5 fusion.157
  186.6 2.1 constant_dynamic-update-slice_fusion.22
  193.9 1.1 copy.281
  195.0 1.7 copy.282
  196.7 1.7 copy.283
  200.3 2.9 copy.271
  206.8 1.6 copy.285
  208.5 1.6 copy.284
  211.3 3.2 convolution_add_fusion.4
  214.7 1.6 convert_element_type.39
  216.4 2.5 convert_element_type.37
  221.5 111.8 %all-reduce.10.cloned.1.call-done = bf16[16,3200]{1,0:T(8,128)(2,1)} async-done(((bf16[16,3200]{1,0:T(8,128)(2,1)}), bf16[16,3200]{1,0:T(8,128)(2,1)}) %all-reduce.10.cloned.1.call-update) | async-done | bytes 102416
  333.3 117.5 %all-reduce.8.cloned.1.call-done = bf16[128,3200]{1,0:T(8,128)(2,1)} async-done(((bf16[128,3200]{1,0:T(8,128)(2,1)}), bf16[128,3200]{1,0:T(8,128)(2,1)}) %all-reduce.8.cloned.1.call-update) | async-done | bytes 819216
  450.8 1.5 add_bitcast_fusion
  (230 shorter events, 50.5 us)
Async XLA Ops:
  6.5 51.9 %copy-start.18 = (bf16[8,25,128]{2,0,1:T(8,128)(2,1)S(1)}, bf16[8,25,128]{2,0,1:T(8,128)(2,1)}, u32[]{:S(2)}) copy-start(bf16[8,25,128]{2,0,1:T(8,128)(2,1)} %param.12) | copy-start | bytes 153604
  6.5 326.7 %all-reduce.10.cloned.1.call-start = ((), (), s32[]{:S(2)}) async-start(), calls=%async_computation.1 | async-start | bytes 204800
  100.6 1.6 copy-start.17
  106.5 1.2 copy-start
  106.5 1.5 copy-start.15
  106.5 2.7 copy-start.19
  106.5 2.7 copy-start.21
  117.6 3.6 copy-start.7
  120.5 2.1 copy-start.14
  122.9 6.1 %copy-start.5 = (bf16[2,1024,512]{2,1,0:T(8,128)(2,1)S(1)}, bf16[2,1024,512]{2,1,0:T(8,128)(2,1)}, u32[]{:S(2)}) copy-start(bf16[2,1024,512]{2,1,0:T(8,128)(2,1)} %get-tuple-element.435) | copy-start | bytes 6291460 | tf_op jit(solution)/shard_map/while
  132.6 2.2 copy-start.9
  134.8 1.1 copy-start.4
  136.1 1.4 copy-start.8
  138.4 6.1 %copy-start.6 = (bf16[2,1024,512]{2,1,0:T(8,128)(2,1)S(1)}, bf16[2,1024,512]{2,1,0:T(8,128)(2,1)}, u32[]{:S(2)}) copy-start(bf16[2,1024,512]{2,1,0:T(8,128)(2,1)} %get-tuple-element.435) | copy-start | bytes 6291460 | tf_op jit(solution)/shard_map/while
  146.3 2.9 copy-start.11
  149.8 0.9 copy-start.10
  154.5 1.6 copy-start.2
  154.5 1.6 copy-start.12
  156.1 1.1 copy-start.3
  157.2 3.2 copy-start.13
  157.2 3.2 copy-start.1
  157.2 3.2 copy-start.16
  157.2 3.2 copy-start.20
  157.3 3.2 copy-start.22
  160.5 1.2 copy-start
  160.5 1.5 copy-start.15
  160.5 2.7 copy-start.19
  160.5 2.7 copy-start.21
  171.6 3.6 copy-start.7
  174.4 2.1 copy-start.14
  176.9 6.1 %copy-start.5 = (bf16[2,1024,512]{2,1,0:T(8,128)(2,1)S(1)}, bf16[2,1024,512]{2,1,0:T(8,128)(2,1)}, u32[]{:S(2)}) copy-start(bf16[2,1024,512]{2,1,0:T(8,128)(2,1)} %get-tuple-element.435) | copy-start | bytes 6291460 | tf_op jit(solution)/shard_map/while
  186.6 2.2 copy-start.9
  188.7 1.1 copy-start.4
  190.1 1.4 copy-start.8
  192.3 6.1 %copy-start.6 = (bf16[2,1024,512]{2,1,0:T(8,128)(2,1)S(1)}, bf16[2,1024,512]{2,1,0:T(8,128)(2,1)}, u32[]{:S(2)}) copy-start(bf16[2,1024,512]{2,1,0:T(8,128)(2,1)} %get-tuple-element.435) | copy-start | bytes 6291460 | tf_op jit(solution)/shard_map/while
  200.3 2.9 copy-start.11
  203.8 0.9 copy-start.10
  208.5 1.6 copy-start.2
  208.5 1.6 copy-start.12
  210.1 1.1 copy-start.3
  211.2 3.2 copy-start.13
  211.2 3.2 copy-start.1
  211.2 3.2 copy-start.16
  211.2 3.2 copy-start.20
  211.2 3.2 copy-start.22
  216.3 234.5 %all-reduce.8.cloned.1.call-start = ((), (), s32[]{:S(2)}) async-start(), calls=%async_computation | async-start | bytes 1638400
  216.3 2.5 copy-start.24
  216.3 3.2 copy-start.23
Sparse Core Ops, SparseCore 0:
  216.4 116.8 all-reduce.9
  338.6 112.1 all-reduce.7
where the time goes:
time: 465 us; the launch traced here: 459 us
  waiting for transfers between devices  229 us (49%)
  blocking collectives  90.4 us (19%)
  local copies, waits for them, and re-layouts  76.5 us (16%)
  matrix products  32 us (7%)
  between operations  15.5 us (3%)
  other arithmetic  14 us (3%)
    unnamed x4, waiting for transfers between devices  229 us
    all_gather x1, blocking collectives, local(): lax.all_gather(node_feats, 'col', axis=0, tiled=True)  47.5 us
    all_gather x1, blocking collectives, local(): lax.all_gather(grad_out, 'col', axis=0, tiled=True)  40.6 us
    while x104, local copies, waits for them, and re-layouts  13.9 us
  transfers between devices with their start and end apart: 2, of which 2 were waited for; matrix products, arithmetic and copies ran while one was open for 1% of the time, Pallas kernels for 0%

commit v1 on v0

v1 whole, which is shorter than its diff:
```python
import functools

import jax
import jax.numpy as jnp
from jax import lax
from jax.experimental import pallas as pl
from jax.experimental.pallas import tpu as pltpu
from jax.sharding import PartitionSpec as P

C = 128
COEF = 25
ROWS = 19
GROUP = 8
K_PAD = 20 * GROUP
J_PAD = 26 * GROUP
LANES = 256
UNROLL = 4
F32 = jnp.float32
BF16 = jnp.bfloat16


def iota(shape, axis):
    return lax.broadcasted_iota(jnp.int32, shape, axis)


def expand_kernel(wig_ref, fwd_ref, bwd_ref, flat):
    edges = wig_ref.shape[0]
    width = wig_ref.shape[1]
    flat[:, 384:512] = jnp.zeros((edges, 128), BF16)
    flat[:, 0:width] = wig_ref[...]
    same_edge = (iota((edges, LANES), 0) % GROUP) == (iota((edges, LANES), 1) % GROUP)
    source = iota((512, LANES), 0)
    slot = iota((512, LANES), 1) // GROUP

    def picked(wanted):
        chosen = jnp.where(source == wanted, 1.0, 0.0).astype(BF16)
        spread = jnp.dot(flat[...], chosen, preferred_element_type=F32)
        return jnp.where(same_edge, spread, 0.0).reshape(edges // GROUP, GROUP, LANES)

    def fwd_step(pair, unused):
        parts = []
        for odd in range(2):
            k = pair * 2 + odd
            wanted = jnp.where((slot < COEF) & (k < ROWS), k * COEF + slot, -1)
            parts.append(picked(wanted))
        start = pl.multiple_of(pair * 16, 16)
        fwd_ref[:, pl.ds(start, 16), :] = jnp.concatenate(parts, axis=1).astype(BF16)
        return unused

    def bwd_step(pair, unused):
        parts = []
        for odd in range(2):
            j = pair * 2 + odd
            wanted = jnp.where((slot < ROWS) & (j < COEF), slot * COEF + j, -1)
            parts.append(picked(wanted))
        start = pl.multiple_of(pair * 16, 16)
        bwd_ref[:, pl.ds(start, 16), :] = jnp.concatenate(parts, axis=1).astype(BF16)
        return unused

    lax.fori_loop(0, K_PAD // 16, fwd_step, 0)
    lax.fori_loop(0, J_PAD // 16, bwd_step, 0)


def gather_atoms(ids_ref, feats_ref, table, gathered):
    blocks = feats_ref.shape[0]
    edges = ids_ref.shape[0]
    for j in range(COEF):
        column = jnp.concatenate([feats_ref[b, j].astype(F32) for b in range(blocks)], axis=0)
        table[:, j * C : (j + 1) * C] = column.astype(BF16)
    atoms = blocks * 8
    hot = jnp.where(ids_ref[...] == iota((edges, atoms), 1), 1.0, 0.0).astype(BF16)
    for j in range(0, COEF, 5):
        gathered[:, j * C : (j + 5) * C] = jnp.dot(
            hot, table[:, j * C : (j + 5) * C], preferred_element_type=F32
        )


def rotate_group(rot_ref, gathered, g):
    start = pl.multiple_of(g * GROUP, GROUP)
    rows = [gathered[pl.ds(start, GROUP), j * C : (j + 1) * C] for j in range(COEF)]
    rows.append(jnp.zeros((LANES - COEF * GROUP, C), F32))
    right = jnp.concatenate(rows, axis=0).astype(BF16)
    return jnp.dot(rot_ref[g], right, preferred_element_type=F32)


def pair_row(first, second, k):
    return jnp.concatenate([first[k * 8 : k * 8 + 8], second[k * 8 : k * 8 + 8]], axis=0)


def forward_kernel(has_prev, *refs):
    ids_ref, feats_ref, rot_ref, w0_ref, w1_ref, w2_ref = refs[:6]
    refs = refs[6:]
    if has_prev:
        prev, refs = refs[:3], refs[3:]
    outs = refs[:3]
    table, gathered, l0, l1, l2 = refs[3:]
    edges = ids_ref.shape[0]
    gather_atoms(ids_ref, feats_ref, table, gathered)

    def step(i, unused):
        for u in range(0, UNROLL, 2):
            g = i * UNROLL + u
            first = rotate_group(rot_ref, gathered, g)
            second = rotate_group(rot_ref, gathered, g + 1)
            top = pl.ds(pl.multiple_of(g * GROUP, 16), 16)
            low = pl.ds(pl.multiple_of(g * GROUP + edges, 16), 16)
            for k in range(5):
                l0[top, k * C : (k + 1) * C] = pair_row(first, second, k).astype(BF16)
            for left, base, count in ((l1, 5, 4), (l2, 13, 3)):
                half = count * C
                for n in range(count):
                    p = pair_row(first, second, base + n)
                    q = pair_row(first, second, base + count + n)
                    here = slice(n * C, (n + 1) * C)
                    there = slice(half + n * C, half + (n + 1) * C)
                    left[top, here] = p.astype(BF16)
                    left[top, there] = (-q).astype(BF16)
                    left[low, here] = q.astype(BF16)
                    left[low, there] = p.astype(BF16)
        return unused

    lax.fori_loop(0, edges // (GROUP * UNROLL), step, 0)
    for n, (left, w_ref) in enumerate(((l0, w0_ref), (l1, w1_ref), (l2, w2_ref))):
        width = w_ref.shape[-1]
        weight = w_ref[...].reshape(-1, width)
        value = jnp.dot(left[...], weight, preferred_element_type=F32)
        if has_prev:
            value = value + prev[n][...]
        outs[n][...] = value


def y_slices(edges, start):
    out = []
    for k in range(5):
        out.append((0, start, k))
    for base, count in ((1, 4), (2, 3)):
        for sign in range(2):
            for n in range(count):
                out.append((base, start + sign * edges, n))
    return out


def back_half(lefts, w_refs, rot_ref, grad_in, edge_grad):
    edges = lefts[0].shape[0]
    dims = (((1,), (1,)), ((), ()))
    for n in range(3):
        w_ref = w_refs[n]
        width = w_ref.shape[-1]
        if n == 0:
            weight = w_ref[...].reshape(-1, width)
            grad_in[0][...] = lax.dot_general(
                lefts[0][...], weight, dims, preferred_element_type=F32
            )
        else:
            real = w_ref[0].reshape(-1, width)
            imag = w_ref[1].reshape(-1, width)
            grad_in[n][...] = lax.dot_general(
                lefts[n][:, :width], real, dims, preferred_element_type=F32
            ) + lax.dot_general(lefts[n][:, width:], imag, dims, preferred_element_type=F32)

    def one(g):
        start = pl.multiple_of(g * GROUP, GROUP)
        rows = []
        for which, row, n in y_slices(edges, start):
            rows.append(
                grad_in[which][pl.ds(pl.multiple_of(row, GROUP), GROUP), n * C : (n + 1) * C]
            )
        rows.append(jnp.zeros((LANES - ROWS * GROUP, C), F32))
        right = jnp.concatenate(rows, axis=0).astype(BF16)
        return jnp.dot(rot_ref[g], right, preferred_element_type=F32)

    def step(i, unused):
        for u in range(0, UNROLL, 2):
            g = i * UNROLL + u
            first, second = one(g), one(g + 1)
            top = pl.ds(pl.multiple_of(g * GROUP, 16), 16)
            for j in range(COEF):
                edge_grad[top, j * C : (j + 1) * C] = pair_row(first, second, j).astype(BF16)
        return unused

    lax.fori_loop(0, edges // (GROUP * UNROLL), step, 0)


def scatter_atoms(ids_row_ref, count_ref, edge_grad, out_ref):
    blocks = out_ref.shape[0]
    atoms = blocks * 8
    edges = edge_grad.shape[0]
    valid = iota((atoms, edges), 1) < count_ref[0]
    hot = jnp.where((ids_row_ref[...] == iota((atoms, edges), 0)) & valid, 1.0, 0.0).astype(BF16)
    for j in range(COEF):
        total = jnp.dot(hot, edge_grad[:, j * C : (j + 1) * C], preferred_element_type=F32)
        for b in range(blocks):
            out_ref[b, j] = total[b * 8 : b * 8 + 8].astype(out_ref.dtype)


def target_back_kernel(*refs):
    ids_ref, row_ref, count_ref, cot_ref, fwd_ref, bwd_ref = refs[:6]
    w_refs, ys, lefts = refs[6:9], refs[9:12], refs[12:15]
    out_ref = refs[15]
    table, gathered, g0, g1, g2, edge_grad = refs[16:]
    edges = ids_ref.shape[0]
    gather_atoms(ids_ref, cot_ref, table, gathered)

    def step(i, unused):
        for u in range(0, UNROLL, 2):
            g = i * UNROLL + u
            first = rotate_group(fwd_ref, gathered, g)
            second = rotate_group(fwd_ref, gathered, g + 1)
            start = g * GROUP
            top = pl.ds(pl.multiple_of(start, 16), 16)
            low = pl.ds(pl.multiple_of(start + edges, 16), 16)
            cots = [pair_row(first, second, k).astype(BF16).astype(F32) for k in range(ROWS)]
            where = y_slices(edges, start)

            def y_at(k):
                which, row, n = where[k]
                return ys[which][pl.ds(pl.multiple_of(row, 16), 16), n * C : (n + 1) * C]

            y0 = y_at(0)
            gating = jax.nn.sigmoid(y0)
            slope = gating * (1.0 - gating)
            total = cots[1] * y_at(1)
            for k in range(2, ROWS):
                total = total + cots[k] * y_at(k)
            scalar = cots[0] * (gating + y0 * slope) + total * slope
            grads = [scalar] + [gating * cots[k] for k in range(1, ROWS)]
            for k in range(5):
                lefts[0][top, k * C : (k + 1) * C] = grads[k].astype(BF16)
            for n, base, count in ((1, 5, 4), (2, 13, 3)):
                left = lefts[n]
                half = count * C
                for m in range(count):
                    a = grads[base + m]
                    b = grads[base + count + m]
                    here = slice(m * C, (m + 1) * C)
                    there = slice(half + m * C, half + (m + 1) * C)
                    left[top, here] = a.astype(BF16)
                    left[top, there] = b.astype(BF16)
                    left[low, here] = b.astype(BF16)
                    left[low, there] = (-a).astype(BF16)
        return unused

    lax.fori_loop(0, edges // (GROUP * UNROLL), step, 0)
    back_half(lefts, w_refs, bwd_ref, (g0, g1, g2), edge_grad)
    scatter_atoms(row_ref, count_ref, edge_grad, out_ref)


def source_back_kernel(*refs):
    row_ref, count_ref, bwd_ref = refs[:3]
    w_refs, lefts, out_ref = refs[3:6], refs[6:9], refs[9]
    g0, g1, g2, edge_grad = refs[10:]
    back_half(lefts, w_refs, bwd_ref, (g0, g1, g2), edge_grad)
    scatter_atoms(row_ref, count_ref, edge_grad, out_ref)


VMEM_LIMIT = 56 * 1024 * 1024


def whole(shape):
    return pl.BlockSpec(shape, lambda i: (0,) * len(shape))


def half_specs(half):
    return [
        pl.BlockSpec((5, 1, C, 5 * C), lambda i: (0, half, 0, 0)),
        pl.BlockSpec((2, 4, 1, C, 4 * C), lambda i: (0, 0, half, 0, 0)),
        pl.BlockSpec((2, 3, 1, C, 3 * C), lambda i: (0, 0, half, 0, 0)),
    ]


def call(kernel, args, specs, outs, scratch, flops, aliases=None):
    moved = sum(a.size * a.dtype.itemsize for a in args) + sum(
        o.size * o.dtype.itemsize for o in outs
    )
    return pl.pallas_call(
        kernel,
        grid=(1,),
        in_specs=specs,
        out_specs=[whole(o.shape) for o in outs],
        out_shape=outs,
        scratch_shapes=scratch,
        input_output_aliases=aliases or {},
        compiler_params=pltpu.CompilerParams(vmem_limit_bytes=VMEM_LIMIT),
        cost_estimate=pl.CostEstimate(flops=flops, bytes_accessed=moved, transcendentals=0),
    )(*args)


def expand(wig):
    edges = wig.shape[0]
    groups = edges // GROUP
    outs = [
        jax.ShapeDtypeStruct((groups, K_PAD, LANES), BF16),
        jax.ShapeDtypeStruct((groups, J_PAD, LANES), BF16),
    ]
    return call(
        expand_kernel,
        [wig],
        [whole(wig.shape)],
        outs,
        [pltpu.VMEM((edges, 512), BF16)],
        2 * 46 * edges * 512 * 256,
    )


def y_shapes(edges):
    return [
        jax.ShapeDtypeStruct((edges, 5 * C), F32),
        jax.ShapeDtypeStruct((2 * edges, 4 * C), F32),
        jax.ShapeDtypeStruct((2 * edges, 3 * C), F32),
    ]


def left_shapes(edges):
    return [(edges, 5 * C), (2 * edges, 8 * C), (2 * edges, 6 * C)]


def forward(half, ids, feats, rot, weights, prev):
    edges = ids.shape[0]
    atoms = feats.shape[0] * 8
    args = [ids, feats, rot, *weights]
    specs = [whole(ids.shape), whole(feats.shape), whole(rot.shape), *half_specs(half)]
    outs = y_shapes(edges)
    aliases = None
    if prev is not None:
        aliases = {len(args) + n: n for n in range(3)}
        args += prev
        specs += [whole(o.shape) for o in outs]
    scratch = [pltpu.VMEM((atoms, COEF * C), BF16), pltpu.VMEM((edges, COEF * C), F32)]
    scratch += [pltpu.VMEM(s, BF16) for s in left_shapes(edges)]
    kernel = functools.partial(forward_kernel, prev is not None)
    return call(kernel, args, specs, outs, scratch, 2 * edges * 65536 * 64, aliases)


def target_back(ids, row, count, cot, fwd, bwd, weights, ys):
    edges = ids.shape[0]
    blocks = cot.shape[0]
    args = [ids, row, count, cot, fwd, bwd, *weights, *ys]
    specs = [whole(ids.shape), whole(row.shape), pl.BlockSpec(memory_space=pltpu.SMEM)]
    specs += [whole(cot.shape), whole(fwd.shape), whole(bwd.shape), *half_specs(1)]
    specs += [whole(y.shape) for y in ys]
    outs = [jax.ShapeDtypeStruct(s, BF16) for s in left_shapes(edges)]
    outs.append(jax.ShapeDtypeStruct((blocks, COEF, 8, C), BF16))
    scratch = [pltpu.VMEM((blocks * 8, COEF * C), BF16), pltpu.VMEM((edges, COEF * C), F32)]
    scratch += [pltpu.VMEM(o.shape, F32) for o in y_shapes(edges)]
    scratch.append(pltpu.VMEM((edges, COEF * C), BF16))
    return call(target_back_kernel, args, specs, outs, scratch, 2 * edges * 65536 * 95)


def source_back(row, count, bwd, weights, lefts, blocks):
    edges = lefts[0].shape[0]
    args = [row, count, bwd, *weights, *lefts]
    specs = [whole(row.shape), pl.BlockSpec(memory_space=pltpu.SMEM), whole(bwd.shape)]
    specs += half_specs(0) + [whole(v.shape) for v in lefts]
    outs = [jax.ShapeDtypeStruct((blocks, COEF, 8, C), BF16)]
    scratch = [pltpu.VMEM(o.shape, F32) for o in y_shapes(edges)]
    scratch.append(pltpu.VMEM((edges, COEF * C), BF16))
    return call(source_back_kernel, args, specs, outs, scratch, 2 * edges * 65536 * 70)[0]


def spread(block, axis):
    size = lax.axis_size(axis)
    return lax.all_to_all(jnp.broadcast_to(block[None], (size, *block.shape)), axis, 0, 0)


def local(node_feats, grad_out, edge_src, edge_tgt, edge_counts, wigner, w_zero, w_one, w_two):
    feats = node_feats.transpose(1, 0, 2)
    cot = grad_out.transpose(1, 0, 2)
    source_feats = lax.all_gather(feats, "row", axis=0)
    target_feats = spread(feats, "col")
    target_cot = spread(cot, "col")
    weights = (
        w_zero.reshape(5, 2, C, 5 * C),
        w_one.reshape(2, 4, 2, C, 4 * C),
        w_two.reshape(2, 3, 2, C, 3 * C),
    )
    count = edge_counts.reshape(1)
    edges = edge_src.shape[-1]
    src_col, tgt_col = edge_src.reshape(edges, 1), edge_tgt.reshape(edges, 1)
    src_row, tgt_row = edge_src.reshape(1, edges), edge_tgt.reshape(1, edges)
    fwd, bwd = expand(wigner[0, 0])
    ys = forward(0, src_col, source_feats, fwd, weights, None)
    ys = forward(1, tgt_col, target_feats, fwd, weights, list(ys))
    *lefts, tile_tgt = target_back(
        tgt_col, tgt_row, count, target_cot, fwd, bwd, weights, list(ys)
    )
    tile_src = source_back(src_row, count, bwd, weights, lefts, source_feats.shape[0])
    own = lax.all_to_all(tile_tgt, "col", 0, 0).astype(F32).sum(0)
    cross = lax.all_to_all(tile_src, "row", 0, 0).astype(F32).sum(0)
    return (own + cross).transpose(1, 0, 2)


def solution(mesh):
    placed = (
        P(("row", "col"), None, None),
        P(("row", "col"), None, None),
        P("row", "col", None),
        P("row", "col", None),
        P("row", "col"),
        P("row", "col", None, None),
        P(),
        P(),
        P(),
    )
    return jax.shard_map(
        local, mesh=mesh, in_specs=placed, out_specs=P(("row", "col"), None, None), check_vma=False
    )
```

time: 465 us -> 152 us (0.33); the launches traced: 459 us -> 152 us
  waiting for transfers between devices: 229 us -> 20.6 us
  Pallas kernels: 0 us -> 76.5 us
  local copies, waits for them, and re-layouts: 76.5 us -> 5.67 us
  blocking collectives: 90.4 us -> 36.9 us
  matrix products: 32 us -> 0 us
  between operations: 15.5 us -> 0.71 us
  other arithmetic: 14 us -> 0.78 us
  starting transfers between devices: 0.04 us -> 10.6 us
    unnamed x4 -> x0, waiting for transfers between devices: 229 us -> none
    all_gather x3 -> x1, blocking collectives: 90.4 us -> 2.01 us  [local(): source_feats = lax.all_gather(feats, 'row', axis=0)]
    pallas_call x0 -> x5, Pallas kernels: none -> 76.5 us  [call(): pl.pallas_call(kernel, grid=(1,), in_specs=specs, out_specs=[whole(o.shap...]
    all_to_all x0 -> x2, blocking collectives: none -> 34.9 us  [the longest x1 30.2 us: spread(): lax.all_to_all(jnp.broadcast_to(block[None], (size, *block.shape)), axis,...]
    dot_general x34 -> x0, matrix products: 32 us -> none  [the longest x2 6.31 us: block_step(): jnp.dot(target_hot, grad_tgt.reshape(block_size, -1), preferred_element_t...]
    all_to_all x0 -> x2, waiting for transfers between devices: none -> 20.6 us  [the longest x1 20.6 us: local(): own = lax.all_to_all(tile_tgt, 'col', 0, 0).astype(F32).sum(0)]
    while x104 -> x0, local copies, waits for them, and re-layouts: 13.9 us -> none
    reshape x20 -> x2, local copies, waits for them, and re-layouts: 13.3 us -> 1.72 us  [local(): src_col, tgt_col = (edge_src.reshape(edges, 1), edge_tgt.reshape(edges, 1))]
  transfers between devices with their start and end apart: 2 -> 2, of which waited for: 2 -> 1; matrix products, arithmetic and copies ran while one was open for 1% -> 2% of each run, Pallas kernels for 0% -> 27%
where the time goes in v1:
time: 152 us
  Pallas kernels  76.5 us (50%)
  blocking collectives  36.9 us (24%)
  waiting for transfers between devices  20.6 us (14%)
  starting transfers between devices  10.6 us (7%)
  local copies, waits for them, and re-layouts  5.67 us (4%)
    pallas_call x5, Pallas kernels, call(): pl.pallas_call(kernel, grid=(1,), in_specs=specs, out_specs=[whole(o.shap...  76.5 us
    all_to_all x1, blocking collectives, spread(): lax.all_to_all(jnp.broadcast_to(block[None], (size, *block.shape)), axis,...  30.2 us
    all_to_all x1, waiting for transfers between devices, local(): own = lax.all_to_all(tile_tgt, 'col', 0, 0).astype(F32).sum(0)  20.6 us
    all_to_all x1, starting transfers between devices, local(): own = lax.all_to_all(tile_tgt, 'col', 0, 0).astype(F32).sum(0)  6.87 us
    all_to_all x1, blocking collectives, local(): cross = lax.all_to_all(tile_src, 'row', 0, 0).astype(F32).sum(0)  4.77 us
    all_to_all x1, starting transfers between devices, spread(): lax.all_to_all(jnp.broadcast_to(block[None], (size, *block.shape)), axis,...  3.75 us
  transfers between devices with their start and end apart: 2, of which 1 were waited for; matrix products, arithmetic and copies ran while one was open for 2% of the time, Pallas kernels for 27%

profile of v1, /device:TPU:0, one launch (start us, length us, event | category | flops | bytes accessed | tf_op | source)
XLA Modules:
  0.0 151.8 jit_solution(7469370979639901139)
XLA Ops:
  0.0 0.0 copy-start.3
  0.0 0.9 broadcast_in_dim.7
  0.9 30.2 %all_to_all.20.refs_1_ = bf16[16,25,8,128]{3,2,1,0:T(8,128)(2,1)} all-to-all(bf16[16,25,8,128]{3,2,1,0:T(8,128)(2,1)S(1)} %broadcast_in_dim.7), channel_id=1, replica_groups=mesh['row'=2,'col'=16] {'col'}, dimensions={0} | all-to-all | bytes 1638400 | tf_op jit(solution)/shard_map/all_to_all | solution.py:362
  31.1 0.0 copy-start.1
  31.1 0.0 copy-done.3
  31.1 0.0 copy-start.5
  31.1 1.0 broadcast_in_dim.6
  32.1 0.0 copy-start.4
  32.1 0.0 copy-start.2
  32.1 3.7 %all-to-all-start = ((bf16[16,25,8,128]{3,2,1,0:T(8,128)(2,1)}), bf16[16,25,8,128]{3,2,1,0:T(8,128)(2,1)S(1)}, u32[]{:S(2)}, u32[]{:S(2)}) async-start(bf16[16,25,8,128]{3,2,1,0:T(8,128)(2,1)} %broadcast_in_dim.6), calls=%async_computation | async-start | bytes 1638400 | tf_op jit(solution)/shard_map/all_to_all | solution.py:362
  35.9 0.0 copy-done.1
  35.9 1.1 copy.18
  36.9 0.0 copy-done.5
  36.9 0.9 copy.19.refs_0_
  37.8 0.0 copy-done.4
  37.8 0.9 copy.21.refs_0_
  39.3 0.0 copy-done.2
  39.3 2.0 %all-gather = bf16[50,8,128]{2,1,0:T(8,128)(2,1)} all-gather(bf16[25,8,128]{2,1,0:T(8,128)(2,1)S(1)} %bitcast.30), channel_id=2, replica_groups=mesh['row'=2,'col'=16] {'row'}, dimensions={0}, use_global_device_ids=true | all-gather | bytes 153600 | tf_op jit(solution)/shard_map/all_gather | solution.py:368
  41.3 15.4 %shard_map.91 = (bf16[64,160,256]{2,1,0:T(8,128)(2,1)}, bf16[64,208,256]{2,1,0:T(8,128)(2,1)}) custom-call(bf16[512,475]{1,0:T(8,128)(2,1)} %bitcast.28), custom_call_target="tpu_custom_call" | custom-call | flops 6174015488 | bytes 12545024 | tf_op jit(solution)/shard_map/pallas_call | solution.py:275
  56.7 12.3 %shard_map.92 = (f32[512,640]{1,0:T(8,128)}, f32[1024,512]{1,0:T(8,128)}, f32[1024,384]{1,0:T(8,128)}) custom-call(s32[512,1]{1,0:T(8,128)} %copy.19.refs_0_, bf16[2,25,8,128]{3,2,1,0:T(8,128)(2,1)} %bitcast.31, bf16[64,160,256]{2,1,0:T(8,128)(2,1)} %get-tuple-element.17.refs_2_.refs_4_, bf16[5,2,128,640]{3,2,1,0:T(8,128)(2,1)} %bitcast.20, ...), custom_call_target="tpu_custom_call" | custom-call | flops 4294967296 | bytes 15243264 | tf_op jit(solution)/shard_map/pallas_call | solution.py:275
  69.0 14.0 %shard_map.93 = (f32[512,640]{1,0:T(8,128)}, f32[1024,512]{1,0:T(8,128)}, f32[1024,384]{1,0:T(8,128)}) custom-call(s32[512,1]{1,0:T(8,128)} %copy.21.refs_0_, bf16[16,25,8,128]{3,2,1,0:T(8,128)(2,1)} %all_to_all.20.refs_1_, bf16[64,160,256]{2,1,0:T(8,128)(2,1)} %get-tuple-element.17.refs_2_.refs_4_, ...), custom_call_target="tpu_custom_call", output_to_operand_aliasing={{0}: (6, {}), {1}: (7, {}), {2}: (8, {})} | custom-call | flops 4294967296 | bytes 20940800 | tf_op jit(solution)/shard_map/pallas_call | solution.py:275
  83.1 0.0 all-to-all-done.refs_3_
  83.1 0.0 copy-start
  83.1 0.9 copy-done
  84.0 21.6 %shard_map.94 = (bf16[512,640]{1,0:T(8,128)(2,1)}, bf16[1024,1024]{1,0:T(8,128)(2,1)}, bf16[1024,768]{1,0:T(8,128)(2,1)}, bf16[16,25,8,128]{3,2,1,0:T(8,128)(2,1)}) custom-call(s32[512,1]{1,0:T(8,128)} %copy.21.refs_0_, s32[1,512]{1,0:T(1,128)} %bitcast.33, s32[1]{0:T(128)} %bitcast.14.refs_2_, bf16[16,25,8,128]{3,2,1,0:T(8,128)(2,1)} %copy-done, ...), custom_call_target="tpu_custom_call" | custom-call | flops 6375342080 | bytes 27922436 | tf_op jit(solution)/shard_map/pallas_call | solution.py:275
  105.6 13.2 %shard_map.95 = bf16[2,25,8,128]{3,2,1,0:T(8,128)(2,1)} custom-call(s32[1,512]{1,0:T(1,128)} %bitcast.35, s32[1]{0:T(128)} %bitcast.15.refs_1_, bf16[64,208,256]{2,1,0:T(8,128)(2,1)} %get-tuple-element.18.refs_5_.refs_2_, bf16[5,2,128,640]{3,2,1,0:T(8,128)(2,1)} %bitcast.23, bf16[2,4,2,128,512]{4,3,2,1,0:T(8,128)(2,1)} %bitcast.19, ...), custom_call_target="tpu_custom_call" | custom-call | flops 4697620480 | bytes 16160772 | tf_op jit(solution)/shard_map/pallas_call | solution.py:275
  118.8 4.8 %all_to_all.21 = bf16[2,25,8,128]{3,2,1,0:T(8,128)(2,1)S(1)} all-to-all(bf16[2,25,8,128]{3,2,1,0:T(8,128)(2,1)} %shard_map.95), channel_id=1, replica_groups=mesh['row'=2,'col'=16] {'row'}, dimensions={0} | all-to-all | bytes 204800 | tf_op jit(solution)/shard_map/all_to_all | solution.py:388
  123.6 6.9 %all-to-all-start.2 = ((bf16[16,25,8,128]{3,2,1,0:T(8,128)(2,1)}), bf16[16,25,8,128]{3,2,1,0:T(8,128)(2,1)S(1)}, u32[]{:S(2)}, u32[]{:S(2)}) async-start(bf16[16,25,8,128]{3,2,1,0:T(8,128)(2,1)} %get-tuple-element.25), calls=%async_computation.2 | async-start | bytes 1638400 | tf_op jit(solution)/shard_map/all_to_all | solution.py:387
  130.5 20.6 %all-to-all-done.2 = bf16[16,25,8,128]{3,2,1,0:T(8,128)(2,1)S(1)} async-done(((bf16[16,25,8,128]{3,2,1,0:T(8,128)(2,1)}), bf16[16,25,8,128]{3,2,1,0:T(8,128)(2,1)S(1)}, u32[]{:S(2)}, u32[]{:S(2)}) %all-to-all-start.2) | async-done | bytes 819232 | tf_op jit(solution)/shard_map/all_to_all | solution.py:387
  151.0 0.1 convert_reduce_fusion
  151.1 0.7 add_bitcast_fusion
  (1 shorter events, 0.0 us)
Async XLA Ops:
  0.0 31.1 %copy-start.3 = (bf16[8,25,128]{2,0,1:T(8,128)(2,1)S(1)}, bf16[8,25,128]{2,0,1:T(8,128)(2,1)}, u32[]{:S(2)}) copy-start(bf16[8,25,128]{2,0,1:T(8,128)(2,1)} %param.10) | copy-start | bytes 153604
  31.1 4.8 %copy-start.1 = (bf16[1,1,512,475]{2,3,1,0:T(8,128)(2,1)S(1)}, bf16[1,1,512,475]{2,3,1,0:T(8,128)(2,1)}, u32[]{:S(2)}) copy-start(bf16[1,1,512,475]{2,3,1,0:T(8,128)(2,1)} %param.14) | copy-start | bytes 1459204
  31.1 5.8 %copy-start.5 = (s32[1,1,512]{2,1,0:T(1,128)S(1)}, s32[1,1,512]{2,1,0:T(1,128)}, u32[]{:S(2)}) copy-start(s32[1,1,512]{2,1,0:T(1,128)} %param.11) | copy-start | bytes 6148
  32.1 5.7 %copy-start.4 = (s32[1,1,512]{2,1,0:T(1,128)S(1)}, s32[1,1,512]{2,1,0:T(1,128)}, u32[]{:S(2)}) copy-start(s32[1,1,512]{2,1,0:T(1,128)} %param.12) | copy-start | bytes 6148
  32.1 7.2 %copy-start.2 = (bf16[8,25,128]{2,0,1:T(8,128)(2,1)S(1)}, bf16[8,25,128]{2,0,1:T(8,128)(2,1)}, u32[]{:S(2)}) copy-start(bf16[8,25,128]{2,0,1:T(8,128)(2,1)} %param.9) | copy-start | bytes 153604
  32.1 51.0 %all-to-all-start = ((bf16[16,25,8,128]{3,2,1,0:T(8,128)(2,1)}), bf16[16,25,8,128]{3,2,1,0:T(8,128)(2,1)S(1)}, u32[]{:S(2)}, u32[]{:S(2)}) async-start(bf16[16,25,8,128]{3,2,1,0:T(8,128)(2,1)} %broadcast_in_dim.6), calls=%async_computation | async-start | bytes 1638400 | tf_op jit(solution)/shard_map/all_to_all | solution.py:362
  83.1 0.9 copy-start
  123.6 27.5 %all-to-all-start.2 = ((bf16[16,25,8,128]{3,2,1,0:T(8,128)(2,1)}), bf16[16,25,8,128]{3,2,1,0:T(8,128)(2,1)S(1)}, u32[]{:S(2)}, u32[]{:S(2)}) async-start(bf16[16,25,8,128]{3,2,1,0:T(8,128)(2,1)} %get-tuple-element.25), calls=%async_computation.2 | async-start | bytes 1638400 | tf_op jit(solution)/shard_map/all_to_all | solution.py:387

commit v2 on v1

v2 whole, which is shorter than its diff:
```python
import functools

import jax
import jax.numpy as jnp
from jax import lax
from jax.experimental import pallas as pl
from jax.experimental.pallas import tpu as pltpu
from jax.sharding import PartitionSpec as P


C = 128
COEF = 25
ROWS = 19
GROUP = 8
K_PAD = 20 * GROUP
J_PAD = 26 * GROUP
LANES = 256
CHUNK = 256
UNROLL = 4
F32 = jnp.float32
BF16 = jnp.bfloat16
MIB = 1024 * 1024
NT = (((1,), (1,)), ((), ()))


def iota(shape, axis):
    return lax.broadcasted_iota(jnp.int32, shape, axis)


def expand_kernel(wig_ref, fwd_ref, bwd_ref, flat):
    edges = wig_ref.shape[0]
    width = wig_ref.shape[1]
    flat[:, 384:512] = jnp.zeros((edges, 128), BF16)
    flat[:, 0:width] = wig_ref[...]
    same_edge = (iota((edges, LANES), 0) % GROUP) == (iota((edges, LANES), 1) % GROUP)
    source = iota((512, LANES), 0)
    slot = iota((512, LANES), 1) // GROUP

    def picked(wanted):
        chosen = jnp.where(source == wanted, 1.0, 0.0).astype(BF16)
        spread = jnp.dot(flat[...], chosen, preferred_element_type=F32)
        return jnp.where(same_edge, spread, 0.0).reshape(edges // GROUP, GROUP, LANES)

    def fwd_step(pair, unused):
        parts = []
        for odd in range(2):
            k = pair * 2 + odd
            wanted = jnp.where((slot < COEF) & (k < ROWS), k * COEF + slot, -1)
            parts.append(picked(wanted))
        start = pl.multiple_of(pair * 16, 16)
        fwd_ref[:, pl.ds(start, 16), :] = jnp.concatenate(parts, axis=1).astype(BF16)
        return unused

    def bwd_step(pair, unused):
        parts = []
        for odd in range(2):
            j = pair * 2 + odd
            wanted = jnp.where((slot < ROWS) & (j < COEF), slot * COEF + j, -1)
            parts.append(picked(wanted))
        start = pl.multiple_of(pair * 16, 16)
        bwd_ref[:, pl.ds(start, 16), :] = jnp.concatenate(parts, axis=1).astype(BF16)
        return unused

    lax.fori_loop(0, K_PAD // 16, fwd_step, 0)
    lax.fori_loop(0, J_PAD // 16, bwd_step, 0)


def aligned(value, by):
    return pl.multiple_of(value, by)


def fill_table(blocks, table, kinds):
    width = kinds * C
    for j in range(COEF):
        for kind in range(kinds):
            column = jnp.concatenate([block(kind, j).astype(F32) for block in blocks], axis=0)
            start = j * width + kind * C
            table[:, start : start + C] = column.astype(BF16)


def source_hot(ids_ref, chunk, atoms):
    ids = ids_ref[:, pl.ds(aligned(chunk * CHUNK, CHUNK), CHUNK)]
    place = ids ^ (lax.axis_index("row") * 8)
    return place == iota((atoms, CHUNK), 0)


def target_hot(ids_ref, chunk, atoms, inner):
    ids = ids_ref[:, pl.ds(aligned(chunk * CHUNK, CHUNK), CHUNK)]
    place = ids ^ (lax.axis_index("col") * 8)
    block = place // 8
    outer = atoms // (8 * inner)
    place = ((block % inner) * outer + block // inner) * 8 + place % 8
    return place == iota((atoms, CHUNK), 0)


def gather_atoms(hot, table, gathered):
    hot = jnp.where(hot, 1.0, 0.0).T.astype(BF16)
    step = gathered.shape[1] // 5
    for n in range(5):
        gathered[:, n * step : (n + 1) * step] = jnp.dot(
            hot, table[:, n * step : (n + 1) * step], preferred_element_type=F32
        )


def rotate_group(rot_ref, g, gathered, local_g):
    width = gathered.shape[1] // COEF
    start = aligned(local_g * GROUP, GROUP)
    rows = [gathered[pl.ds(start, GROUP), j * width : (j + 1) * width] for j in range(COEF)]
    rows.append(jnp.zeros((LANES - COEF * GROUP, width), F32))
    right = jnp.concatenate(rows, axis=0).astype(BF16)
    return jnp.dot(rot_ref[g], right, preferred_element_type=F32)


def pair_row(first, second, k, kind=0):
    lanes = slice(kind * C, (kind + 1) * C)
    return jnp.concatenate([first[k * 8 : k * 8 + 8, lanes], second[k * 8 : k * 8 + 8, lanes]], 0)


def store_forward(value, lefts, top, low):
    for k in range(5):
        lefts[0][top, k * C : (k + 1) * C] = value(k).astype(BF16)
    for left, base, count in ((lefts[1], 5, 4), (lefts[2], 13, 3)):
        for n in range(count):
            p, q = value(base + n), value(base + count + n)
            here = slice(n * C, (n + 1) * C)
            there = slice((count + n) * C, (count + n + 1) * C)
            left[top, here] = p.astype(BF16)
            left[top, there] = (-q).astype(BF16)
            left[low, here] = q.astype(BF16)
            left[low, there] = p.astype(BF16)


def half_weight(w_ref, n, half):
    width = w_ref.shape[-1]
    if n == 0:
        return w_ref[:, half].reshape(-1, width)
    return w_ref[:, :, half].reshape(-1, width)


def source_forward_kernel(*refs):
    ids_ref, feats_ref, rot_ref = refs[:3]
    w_refs, outs = refs[3:6], refs[6:9]
    table, gathered, lefts = refs[9], refs[10], refs[11:]
    edges = ids_ref.shape[1]
    blocks = [lambda kind, j, b=b: feats_ref[b, j] for b in range(feats_ref.shape[0])]
    fill_table(blocks, table, 1)

    def chunk_step(chunk, unused):
        gather_atoms(source_hot(ids_ref, chunk, table.shape[0]), table, gathered)

        def step(i, unused):
            for u in range(0, UNROLL, 2):
                g = i * UNROLL + u
                pair = [
                    rotate_group(rot_ref, chunk * (CHUNK // GROUP) + g + n, gathered, g + n)
                    for n in range(2)
                ]
                top = pl.ds(aligned(g * GROUP, 16), 16)
                low = pl.ds(aligned(g * GROUP + CHUNK, 16), 16)
                store_forward(lambda k: pair_row(*pair, k), lefts, top, low)
            return unused

        lax.fori_loop(0, CHUNK // (GROUP * UNROLL), step, 0)
        for n in range(3):
            rows = lefts[n].shape[0]
            outs[n][pl.ds(aligned(chunk * rows, rows), rows), :] = jnp.dot(
                lefts[n][...], half_weight(w_refs[n], n, 0), preferred_element_type=F32
            )
        return unused

    lax.fori_loop(0, edges // CHUNK, chunk_step, 0)


def y_slices(start):
    out = [(0, start, k) for k in range(5)]
    for which, count in ((1, 4), (2, 3)):
        for sign in range(2):
            out += [(which, start + sign * CHUNK, n) for n in range(count)]
    return out


def back_half(half, chunk, lefts, w_refs, rot_ref, grad_in, edge_grad):
    for n in range(3):
        width = w_refs[n].shape[-1]
        rows = grad_in[n].shape[0]
        here = pl.ds(aligned(chunk * rows, rows), rows)
        if n == 0:
            weight = w_refs[n][:, half].reshape(-1, width)
            grad_in[n][...] = lax.dot_general(
                lefts[n][here, :], weight, NT, preferred_element_type=F32
            )
        else:
            real = w_refs[n][0, :, half].reshape(-1, width)
            imag = w_refs[n][1, :, half].reshape(-1, width)
            grad_in[n][...] = lax.dot_general(
                lefts[n][here, :width], real, NT, preferred_element_type=F32
            ) + lax.dot_general(lefts[n][here, width:], imag, NT, preferred_element_type=F32)

    def one(g):
        rows = []
        for which, row, n in y_slices(g * GROUP):
            rows.append(grad_in[which][pl.ds(aligned(row, GROUP), GROUP), n * C : (n + 1) * C])
        rows.append(jnp.zeros((LANES - ROWS * GROUP, C), F32))
        right = jnp.concatenate(rows, axis=0).astype(BF16)
        return jnp.dot(
            rot_ref[chunk * (CHUNK // GROUP) + g], right, preferred_element_type=F32
        )

    def step(i, unused):
        for u in range(0, UNROLL, 2):
            g = i * UNROLL + u
            first, second = one(g), one(g + 1)
            top = pl.ds(aligned(g * GROUP, 16), 16)
            for j in range(COEF):
                edge_grad[top, j * C : (j + 1) * C] = pair_row(first, second, j).astype(BF16)
        return unused

    lax.fori_loop(0, CHUNK // (GROUP * UNROLL), step, 0)


def scatter_atoms(hot, count_ref, chunk, edge_grad, total):
    valid = chunk * CHUNK + iota(hot.shape, 1) < count_ref[0, 0]
    hot = jnp.where(hot & valid, 1.0, 0.0).astype(BF16)
    step = total.shape[1] // 5
    for n in range(5):
        here = slice(n * step, (n + 1) * step)
        total[:, here] += jnp.dot(hot, edge_grad[:, here], preferred_element_type=F32)


def write_blocks(total, out_ref):
    for j in range(COEF):
        for b in range(out_ref.shape[0]):
            out_ref[b, j] = total[b * 8 : b * 8 + 8, j * C : (j + 1) * C].astype(out_ref.dtype)


def target_kernel(count_pieces, *refs):
    ids_ref, count_ref, fwd_ref, bwd_ref = refs[:4]
    w_refs, sources = refs[4:7], refs[7:10]
    pieces = refs[10 : 10 + count_pieces]
    refs = refs[10 + count_pieces :]
    lefts, out_ref = refs[:3], refs[3]
    table, gathered = refs[4], refs[5]
    forward_lefts, cots, ys, grad_in = refs[6:9], refs[9], refs[10:13], refs[13:16]
    edge_grad, total = refs[16], refs[17]
    edges = ids_ref.shape[1]
    blocks = []
    for piece in pieces:
        for b in range(piece.shape[0]):
            blocks.append(lambda kind, j, piece=piece, b=b: piece[b, kind, j])
    fill_table(blocks, table, 2)
    total[...] = jnp.zeros_like(total)

    def chunk_step(chunk, unused):
        hot = target_hot(ids_ref, chunk, table.shape[0], count_pieces)
        gather_atoms(hot, table, gathered)

        def turn(i, unused):
            for u in range(0, UNROLL, 2):
                g = i * UNROLL + u
                pair = [
                    rotate_group(fwd_ref, chunk * (CHUNK // GROUP) + g + n, gathered, g + n)
                    for n in range(2)
                ]
                top = pl.ds(aligned(g * GROUP, 16), 16)
                low = pl.ds(aligned(g * GROUP + CHUNK, 16), 16)
                store_forward(lambda k: pair_row(*pair, k), forward_lefts, top, low)
                for k in range(ROWS):
                    cots[top, k * C : (k + 1) * C] = pair_row(*pair, k, 1).astype(BF16)
            return unused

        lax.fori_loop(0, CHUNK // (GROUP * UNROLL), turn, 0)
        for n in range(3):
            rows = forward_lefts[n].shape[0]
            ys[n][...] = sources[n][pl.ds(aligned(chunk * rows, rows), rows), :] + jnp.dot(
                forward_lefts[n][...], half_weight(w_refs[n], n, 1), preferred_element_type=F32
            )

        def gate(i, unused):
            start = aligned(i * 16, 16)
            top = pl.ds(start, 16)
            cot = [cots[top, k * C : (k + 1) * C].astype(F32) for k in range(ROWS)]
            where = y_slices(start)

            def y_at(k):
                which, row, n = where[k]
                return ys[which][pl.ds(aligned(row, 16), 16), n * C : (n + 1) * C]

            y0 = y_at(0)
            gating = jax.nn.sigmoid(y0)
            slope = gating * (1.0 - gating)
            dotted = cot[1] * y_at(1)
            for k in range(2, ROWS):
                dotted = dotted + cot[k] * y_at(k)
            grads = [cot[0] * (gating + y0 * slope) + dotted * slope]
            grads += [gating * cot[k] for k in range(1, ROWS)]
            zero_row = aligned(chunk * CHUNK + start, 16)
            top_row = aligned(chunk * 2 * CHUNK + start, 16)
            low_row = aligned(chunk * 2 * CHUNK + CHUNK + start, 16)
            store_backward(grads, lefts, zero_row, top_row, low_row)
            return unused

        lax.fori_loop(0, CHUNK // 16, gate, 0)
        back_half(1, chunk, lefts, w_refs, bwd_ref, grad_in, edge_grad)
        hot = target_hot(ids_ref, chunk, table.shape[0], count_pieces)
        scatter_atoms(hot, count_ref, chunk, edge_grad, total)
        return unused

    lax.fori_loop(0, edges // CHUNK, chunk_step, 0)
    write_blocks(total, out_ref)


def store_backward(value, lefts, zero_row, top_row, low_row):
    for k in range(5):
        lefts[0][pl.ds(zero_row, 16), k * C : (k + 1) * C] = value[k].astype(BF16)
    top, low = pl.ds(top_row, 16), pl.ds(low_row, 16)
    for left, base, count in ((lefts[1], 5, 4), (lefts[2], 13, 3)):
        for n in range(count):
            a, b = value[base + n], value[base + count + n]
            here = slice(n * C, (n + 1) * C)
            there = slice((count + n) * C, (count + n + 1) * C)
            left[top, here] = a.astype(BF16)
            left[top, there] = b.astype(BF16)
            left[low, here] = b.astype(BF16)
            left[low, there] = (-a).astype(BF16)


def source_back_kernel(*refs):
    ids_ref, count_ref, bwd_ref = refs[:3]
    w_refs, lefts, out_ref = refs[3:6], refs[6:9], refs[9]
    grad_in, edge_grad, total = refs[10:13], refs[13], refs[14]
    total[...] = jnp.zeros_like(total)

    def chunk_step(chunk, unused):
        back_half(0, chunk, lefts, w_refs, bwd_ref, grad_in, edge_grad)
        scatter_atoms(source_hot(ids_ref, chunk, total.shape[0]), count_ref, chunk, edge_grad, total)
        return unused

    lax.fori_loop(0, lefts[0].shape[0] // CHUNK, chunk_step, 0)
    write_blocks(total, out_ref)


IN_VMEM = pl.BlockSpec(memory_space=pltpu.VMEM)
IN_SMEM = pl.BlockSpec(memory_space=pltpu.SMEM)


def call(kernel, args, outs, scratch, limit, flops, scalar=None):
    moved = sum(a.size * a.dtype.itemsize for a in (*args, *outs))
    return pl.pallas_call(
        kernel,
        in_specs=[IN_SMEM if n == scalar else IN_VMEM for n in range(len(args))],
        out_specs=[IN_VMEM] * len(outs),
        out_shape=outs,
        scratch_shapes=[pltpu.VMEM(s, d) for s, d in scratch],
        compiler_params=pltpu.CompilerParams(vmem_limit_bytes=limit * MIB),
        cost_estimate=pl.CostEstimate(flops=flops, bytes_accessed=moved, transcendentals=0),
    )(*args)


def arrays(shapes, dtype):
    return [jax.ShapeDtypeStruct(s, dtype) for s in shapes]


def y_shapes(edges):
    return [(edges, 5 * C), (2 * edges, 4 * C), (2 * edges, 3 * C)]


def left_shapes(edges):
    return [(edges, 5 * C), (2 * edges, 8 * C), (2 * edges, 6 * C)]


def typed(shapes, dtype):
    return [(s, dtype) for s in shapes]


PUSH = 2 * 65536


def expand(wig):
    edges = wig.shape[0]
    groups = edges // GROUP
    outs = arrays([(groups, K_PAD, LANES), (groups, J_PAD, LANES)], BF16)
    scratch = [((edges, 512), BF16)]
    return call(expand_kernel, [wig], outs, scratch, 12, PUSH * edges * 92)


def source_forward(ids, feats, rot, weights):
    edges = ids.shape[1]
    scratch = [((feats.shape[0] * 8, COEF * C), BF16), ((CHUNK, COEF * C), F32)]
    scratch += typed(left_shapes(CHUNK), BF16)
    return call(
        source_forward_kernel,
        [ids, feats, rot, *weights],
        arrays(y_shapes(edges), F32),
        scratch,
        12,
        PUSH * edges * 64,
    )


def target_work(ids, count, fwd, bwd, weights, sources, pieces):
    edges = ids.shape[1]
    blocks = sum(p.shape[0] for p in pieces)
    outs = arrays(left_shapes(edges), BF16) + arrays([(blocks, COEF, 8, C)], BF16)
    scratch = [((blocks * 8, 2 * COEF * C), BF16), ((CHUNK, 2 * COEF * C), F32)]
    scratch += typed(left_shapes(CHUNK), BF16) + [((CHUNK, ROWS * C), BF16)]
    scratch += typed(y_shapes(CHUNK), F32) * 2
    scratch += [((CHUNK, COEF * C), BF16), ((blocks * 8, COEF * C), F32)]
    return call(
        functools.partial(target_kernel, len(pieces)),
        [ids, count, fwd, bwd, *weights, *sources, *pieces],
        outs,
        scratch,
        21 + blocks // 4,
        PUSH * edges * 160,
        1,
    )


def source_back(ids, count, bwd, weights, lefts, blocks):
    scratch = typed(y_shapes(CHUNK), F32)
    scratch += [((CHUNK, COEF * C), BF16), ((blocks * 8, COEF * C), F32)]
    return call(
        source_back_kernel,
        [ids, count, bwd, *weights, *lefts],
        arrays([(blocks, COEF, 8, C)], BF16),
        scratch,
        12,
        PUSH * lefts[0].shape[0] * 70,
        1,
    )[0]


def exchange(value, axis, distance):
    size = lax.axis_size(axis)
    return lax.ppermute(value, axis, [(i, i ^ distance) for i in range(size)])


def step(node_feats, grad_out, edge_src, edge_tgt, count, wigner, w_zero, w_one, w_two):
    rows, cols = lax.axis_size("row"), lax.axis_size("col")
    inner = 4
    outer = cols // inner
    feats = node_feats.transpose(1, 0, 2)
    own = jnp.stack([feats, grad_out.transpose(1, 0, 2)])
    source_feats = [feats] + [exchange(feats, "row", d) for d in range(1, rows)]
    source_feats = jnp.stack(source_feats)
    line = [own]
    for d in range(1, outer):
        line.append(exchange(own, "col", inner * d))
    line = jnp.stack(line)
    pieces = [line]
    for d in range(1, inner):
        pieces.append(exchange(line, "col", d))

    weights = (
        w_zero.reshape(5, 2, C, 5 * C),
        w_one.reshape(2, 4, 2, C, 4 * C),
        w_two.reshape(2, 3, 2, C, 3 * C),
    )
    edges = edge_src.shape[-1]
    src, tgt = edge_src.reshape(1, edges), edge_tgt.reshape(1, edges)
    fwd, bwd = expand(wigner[0, 0])
    sources = source_forward(src, source_feats, fwd, weights)
    *lefts, tile_tgt = target_work(tgt, count, fwd, bwd, weights, sources, pieces)
    tile_src = source_back(src, count, bwd, weights, lefts, rows)

    parts = tile_tgt.reshape(inner, outer, COEF, 8, C)
    summed = parts[0].astype(F32)
    for d in range(1, inner):
        got = exchange(parts[d], "col", d)
        summed = summed + got.astype(F32)
    sent = summed.astype(BF16)
    result = summed[0]
    for d in range(1, outer):
        got = exchange(sent[d], "col", inner * d)
        result = result + got.astype(F32)
    result = result + tile_src[0].astype(F32)
    for d in range(1, rows):
        result = result + exchange(tile_src[d], "row", d).astype(F32)
    return result.transpose(1, 0, 2)


def solution(mesh):
    placed = (
        P(("row", "col"), None, None),
        P(("row", "col"), None, None),
        P("row", "col", None),
        P("row", "col", None),
        P("row", "col"),
        P("row", "col", None, None),
        P(),
        P(),
        P(),
    )
    return jax.shard_map(
        step, mesh=mesh, in_specs=placed, out_specs=P(("row", "col"), None, None), check_vma=False
    )
```

time: 152 us -> 82.3 us (0.54)
  blocking collectives: 36.9 us -> 0 us
  Pallas kernels: 76.5 us -> 46.5 us
  starting transfers between devices: 10.6 us -> 19.2 us
  waiting for transfers between devices: 20.6 us -> 12.5 us
  local copies, waits for them, and re-layouts: 5.67 us -> 1.32 us
    all_to_all x2 -> x0, blocking collectives: 34.9 us -> none  [the longest x1 30.2 us: spread(): lax.all_to_all(jnp.broadcast_to(block[None], (size, *block.shape)), axis,...]
    pallas_call x5 -> x4, Pallas kernels: 76.5 us -> 46.5 us  [call(): pl.pallas_call(kernel, in_specs=[IN_SMEM if n == scalar else IN_VMEM for...]
    all_to_all x2 -> x0, waiting for transfers between devices: 20.6 us -> none  [the longest x1 20.6 us: local(): own = lax.all_to_all(tile_tgt, 'col', 0, 0).astype(F32).sum(0)]
    ppermute x0 -> x14, starting transfers between devices: none -> 19.2 us  [exchange(): return lax.ppermute(value, axis, [(i, i ^ distance) for i in range(size)])]
    ppermute x0 -> x14, waiting for transfers between devices: none -> 12.5 us  [exchange(): return lax.ppermute(value, axis, [(i, i ^ distance) for i in range(size)])]
    all_to_all x2 -> x0, starting transfers between devices: 10.6 us -> none  [the longest x1 6.87 us: local(): own = lax.all_to_all(tile_tgt, 'col', 0, 0).astype(F32).sum(0)]
    all_gather x1 -> x0, blocking collectives: 2.01 us -> none  [local(): source_feats = lax.all_gather(feats, 'row', axis=0)]
    broadcast_in_dim x2 -> x0, local copies, waits for them, and re-layouts: 1.93 us -> none  [spread(): jnp.broadcast_to(block[None], (size, *block.shape))]
  transfers between devices with their start and end apart: 2 -> 14, of which waited for: 1 -> 6; matrix products, arithmetic and copies ran while one was open for 2% -> 2% of each run, Pallas kernels for 27% -> 33%
where the time goes in v2:
time: 82.3 us; the launch traced here: 82.1 us
  Pallas kernels  46.5 us (57%)
  starting transfers between devices  19.2 us (23%)
  waiting for transfers between devices  12.5 us (15%)
  other arithmetic  1.71 us (2%)
  local copies, waits for them, and re-layouts  1.32 us (2%)
  between operations  0.83 us (1%)
    pallas_call x4, Pallas kernels, call(): pl.pallas_call(kernel, in_specs=[IN_SMEM if n == scalar else IN_VMEM for...  46.5 us
    ppermute x14, starting transfers between devices, exchange(): return lax.ppermute(value, axis, [(i, i ^ distance) for i in range(size)])  19.2 us
    ppermute x14, waiting for transfers between devices, exchange(): return lax.ppermute(value, axis, [(i, i ^ distance) for i in range(size)])  12.5 us
  transfers between devices with their start and end apart: 14, of which 6 were waited for; matrix products, arithmetic and copies ran while one was open for 2% of the time, Pallas kernels for 33%

profile of v2, /device:TPU:0, one launch (start us, length us, event | category | flops | bytes accessed | tf_op | source)
XLA Modules:
  0.0 82.1 jit_solution(1512973104768298613)
XLA Ops:
  0.0 0.5 collective-permute-start
  0.5 1.1 %collective-permute-done = bf16[25,8,128]{2,1,0:T(8,128)(2,1)S(1)} collective-permute-done((bf16[25,8,128]{2,1,0:T(8,128)(2,1)}, bf16[25,8,128]{2,1,0:T(8,128)(2,1)S(1)}, u32[]{:S(2)}, u32[]{:S(2)}) %collective-permute-start) | collective-permute-done | bytes 51232 | tf_op jit(solution)/shard_map/ppermute | solution.py:435
  1.6 0.8 %fusion.6 = (bf16[1,2,25,8,128]{4,3,2,1,0:T(8,128)(2,1)S(1)}, bf16[2,25,8,128]{3,2,1,0:T(8,128)(2,1)S(1)}, bf16[2,25,8,128]{3,2,1,0:T(8,128)(2,1)S(1)}) fusion(bf16[1,25,8,128]{3,2,1,0:T(8,128)(2,1)} %bitcast.63, bf16[1,25,8,128]{3,2,1,0:T(8,128)(2,1)} %bitcast.65, bf16[1,25,8,128]{3,2,1,0:T(8,128)(2,1)S(1)} %bitcast.66), kind=kLoop, calls=%fused_computation.16 | loop fusion | flops 102400 | bytes 460800 | tf_op jit(solution)/shard_map/stack | solution.py:449
  2.4 4.0 %collective-permute-start.2 = (bf16[2,25,8,128]{3,2,1,0:T(8,128)(2,1)S(1)}, bf16[2,25,8,128]{3,2,1,0:T(8,128)(2,1)S(1)}, u32[]{:S(2)}, u32[]{:S(2)}) collective-permute-start(bf16[2,25,8,128]{3,2,1,0:T(8,128)(2,1)S(1)} %get-tuple-element.32), channel_id=1, source_target_pairs={{0,8},{1,9},{2,10},{3,11},{4,12},{5,13},{6,14},{7,15},{8,0},{9,1},... | collective-permute-start | bytes 307208 | tf_op jit(solution)/shard_map/ppermute | solution.py:435
  6.4 1.6 %collective-permute-start.1 = (bf16[2,25,8,128]{3,2,1,0:T(8,128)(2,1)S(1)}, bf16[2,25,8,128]{3,2,1,0:T(8,128)(2,1)S(1)}, u32[]{:S(2)}, u32[]{:S(2)}) collective-permute-start(bf16[2,25,8,128]{3,2,1,0:T(8,128)(2,1)S(1)} %get-tuple-element.32), channel_id=1, source_target_pairs={{0,4},{1,5},{2,6},{3,7},{4,0},{5,1},{6,2},{7,3},{8,12},{9,13},{10,... | collective-permute-start | bytes 307208 | tf_op jit(solution)/shard_map/ppermute | solution.py:435
  8.0 0.0 collective-permute-start.3
  8.0 1.2 %copy.10 = bf16[1,1,512,475]{3,2,1,0:T(8,128)(2,1)S(1)} copy(bf16[1,1,512,475]{2,3,1,0:T(8,128)(2,1)} %param.14) | data formatting | bytes 972800 | tf_op args[5]
  9.3 3.3 %collective-permute-done.2 = bf16[2,25,8,128]{3,2,1,0:T(8,128)(2,1)S(1)} collective-permute-done((bf16[2,25,8,128]{3,2,1,0:T(8,128)(2,1)S(1)}, bf16[2,25,8,128]{3,2,1,0:T(8,128)(2,1)S(1)}, u32[]{:S(2)}, u32[]{:S(2)}) %collective-permute-start.2) | collective-permute-done | bytes 102432 | tf_op jit(solution)/shard_map/ppermute | solution.py:435
  12.6 0.0 collective-permute-done.1
  12.6 2.6 %collective-permute-done.3 = bf16[2,25,8,128]{3,2,1,0:T(8,128)(2,1)S(1)} collective-permute-done((bf16[2,25,8,128]{3,2,1,0:T(8,128)(2,1)S(1)}, bf16[2,25,8,128]{3,2,1,0:T(8,128)(2,1)S(1)}, u32[]{:S(2)}, u32[]{:S(2)}) %collective-permute-start.3) | collective-permute-done | bytes 102432 | tf_op jit(solution)/shard_map/ppermute | solution.py:435
  15.2 0.1 pad_maximum_fusion.refs_10_
  15.3 2.5 %collective-permute-start.6 = (bf16[4,2,25,8,128]{4,3,2,1,0:T(8,128)(2,1)S(1)}, bf16[4,2,25,8,128]{4,3,2,1,0:T(8,128)(2,1)S(1)}, u32[]{:S(2)}, u32[]{:S(2)}) collective-permute-start(bf16[4,2,25,8,128]{4,3,2,1,0:T(8,128)(2,1)S(1)} %pad_maximum_fusion.refs_10_), channel_id=1, source_target_pairs={{0,3},{1,2},{2,1},{3,0},{4,7},{5,6},{6,5},{7,4},{8,11},{9,10},{10,... | collective-permute-start | bytes 1228808 | tf_op jit(solution)/shard_map/ppermute | solution.py:435
  17.8 0.5 collective-permute-start.5
  18.3 0.5 collective-permute-start.4
  18.8 0.0 copy-start
  18.8 0.0 copy-start.1
  18.9 0.0 copy-start.2
  18.9 0.0 copy-start.4
  18.9 10.4 %shard_map.91 = (bf16[64,160,256]{2,1,0:T(8,128)(2,1)S(1)}, bf16[64,208,256]{2,1,0:T(8,128)(2,1)S(1)}) custom-call(bf16[512,475]{1,0:T(8,128)(2,1)S(1)} %bitcast.47), custom_call_target="tpu_custom_call" | custom-call | flops 6174015488 | bytes 12545024 | tf_op jit(solution)/shard_map/pallas_call | solution.py:348
  29.9 0.0 copy-done
  29.9 0.0 copy-done.1
  29.9 0.0 copy-done.2
  30.0 0.0 copy-done.4
  30.0 0.0 copy-start.3
  30.0 8.3 %shard_map.92 = (f32[512,640]{1,0:T(8,128)S(1)}, f32[1024,512]{1,0:T(8,128)S(1)}, f32[1024,384]{1,0:T(8,128)S(1)}) custom-call(s32[1,512]{1,0:T(1,128)S(1)} %bitcast.58, bf16[2,25,8,128]{3,2,1,0:T(8,128)(2,1)S(1)} %get-tuple-element.33.refs_1_, bf16[64,160,256]{2,1,0:T(8,128)(2,1)S(1)} %get-tuple-element.14.refs_2_, bf16[5,2,128,640]{3,2,1,0:T(8,128)(2,1)S(1)} %bitcast.51, ...), custom_call_target="tpu_custom_call" | custom-call | flops 4294967296 | bytes 15243264 | tf_op jit(solution)/shard_map/pallas_call | solution.py:348
  38.3 0.0 collective-permute-done.6.refs_13_
  38.3 0.0 collective-permute-done.5.refs_12_
  38.3 0.0 collective-permute-done.4.refs_11_
  38.4 0.0 copy-done.3
  38.4 19.6 %shard_map.93 = (bf16[512,640]{1,0:T(8,128)(2,1)S(1)}, bf16[1024,1024]{1,0:T(8,128)(2,1)S(1)}, bf16[1024,768]{1,0:T(8,128)(2,1)S(1)}, bf16[16,25,8,128]{3,2,1,0:T(8,128)(2,1)S(1)}) custom-call(s32[1,512]{1,0:T(1,128)S(1)} %bitcast.57, s32[1,1]{1,0:T(1,128)S(6)} %copy.11.refs_1_, bf16[64,160,256]{2,1,0:T(8,128)(2,1)S(1)} %get-tuple-element.14.refs_2_, ...), custom_call_target="tpu_custom_call" | custom-call | flops 10737418240 | bytes 28739588 | tf_op jit(solution)/shard_map/pallas_call | solution.py:348
  58.1 1.6 %collective-permute-start.7 = (bf16[4,25,8,128]{3,2,1,0:T(8,128)(2,1)S(1)}, bf16[4,25,8,128]{3,2,1,0:T(8,128)(2,1)S(1)}, u32[]{:S(2)}, u32[]{:S(2)}) collective-permute-start(bf16[4,25,8,128]{3,2,1,0:T(8,128)(2,1)S(1)} %get-tuple-element.25), channel_id=1, source_target_pairs={{0,1},{1,0},{2,3},{3,2},{4,5},{5,4},{6,7},{7,6},{8,9},{9,8},{10,11... | collective-permute-start | bytes 614408 | tf_op jit(solution)/shard_map/ppermute | solution.py:435
  59.6 1.5 %collective-permute-start.9 = (bf16[4,25,8,128]{3,2,1,0:T(8,128)(2,1)S(1)}, bf16[4,25,8,128]{3,2,1,0:T(8,128)(2,1)S(1)}, u32[]{:S(2)}, u32[]{:S(2)}) collective-permute-start(bf16[4,25,8,128]{3,2,1,0:T(8,128)(2,1)S(1)} %get-tuple-element.26), channel_id=1, source_target_pairs={{0,3},{1,2},{2,1},{3,0},{4,7},{5,6},{6,5},{7,4},{8,11},{9,10},{10,... | collective-permute-start | bytes 614408 | tf_op jit(solution)/shard_map/ppermute | solution.py:435
  61.1 0.5 collective-permute-start.8
  61.6 8.1 %shard_map.94 = bf16[2,25,8,128]{3,2,1,0:T(8,128)(2,1)S(1)} custom-call(s32[1,512]{1,0:T(1,128)S(1)} %bitcast.59, s32[1,1]{1,0:T(1,128)S(6)} %copy.11.refs_1_, bf16[64,208,256]{2,1,0:T(8,128)(2,1)S(1)} %get-tuple-element.15.refs_3_.refs_2_, bf16[5,2,128,640]{3,2,1,0:T(8,128)(2,1)S(1)} %bitcast.53, bf16[2,4,2,128,512]{4,3,2,1,0:T(8,128)(2,1)S(1)} %bitcast.50, ...), custom_call_target="tpu_custom_call" | custom-call | flops 4697620480 | bytes 16160772 | tf_op jit(solution)/shard_map/pallas_call | solution.py:348
  69.7 0.1 collective-permute-start.13
  69.8 0.0 collective-permute-done.7
  69.8 0.0 collective-permute-done.9
  69.8 0.5 collective-permute-done.8
  70.3 0.1 fusion.7
  70.4 2.7 %collective-permute-start.10 = (bf16[25,8,128]{2,1,0:T(8,128)(2,1)S(1)}, bf16[25,8,128]{2,1,0:T(8,128)(2,1)S(1)}, u32[]{:S(2)}, u32[]{:S(2)}) collective-permute-start(bf16[25,8,128]{2,1,0:T(8,128)(2,1)S(1)} %get-tuple-element.28), channel_id=1, source_target_pairs={{0,4},{1,5},{2,6},{3,7},{4,0},{5,1},{6,2},{7,3},{8,12},{9,13},{10,... | collective-permute-start | bytes 153608 | tf_op jit(solution)/shard_map/ppermute | solution.py:435
  73.1 3.3 %collective-permute-start.12 = (bf16[25,8,128]{2,1,0:T(8,128)(2,1)S(1)}, bf16[25,8,128]{2,1,0:T(8,128)(2,1)S(1)}, u32[]{:S(2)}, u32[]{:S(2)}) collective-permute-start(bf16[25,8,128]{2,1,0:T(8,128)(2,1)S(1)} %get-tuple-element.29), channel_id=1, source_target_pairs={{0,12},{1,13},{2,14},{3,15},{4,8},{5,9},{6,10},{7,11},{8,4},{9,5},... | collective-permute-start | bytes 153608 | tf_op jit(solution)/shard_map/ppermute | solution.py:435
  76.4 0.0 collective-permute-start.11
  76.4 0.0 collective-permute-done.13
  76.4 0.0 collective-permute-done.10
  76.4 2.7 %collective-permute-done.12 = bf16[25,8,128]{2,1,0:T(8,128)(2,1)S(1)} collective-permute-done((bf16[25,8,128]{2,1,0:T(8,128)(2,1)S(1)}, bf16[25,8,128]{2,1,0:T(8,128)(2,1)S(1)}, u32[]{:S(2)}, u32[]{:S(2)}) %collective-permute-start.12) | collective-permute-done | bytes 51232 | tf_op jit(solution)/shard_map/ppermute | solution.py:435
  79.1 2.3 %collective-permute-done.11 = bf16[25,8,128]{2,1,0:T(8,128)(2,1)S(1)} collective-permute-done((bf16[25,8,128]{2,1,0:T(8,128)(2,1)S(1)}, bf16[25,8,128]{2,1,0:T(8,128)(2,1)S(1)}, u32[]{:S(2)}, u32[]{:S(2)}) %collective-permute-start.11) | collective-permute-done | bytes 51232 | tf_op jit(solution)/shard_map/ppermute | solution.py:435
  81.4 0.7 fusion.5
  (3 shorter events, 0.1 us)
Async XLA Ops:
  0.0 1.6 %collective-permute-start = (bf16[25,8,128]{2,1,0:T(8,128)(2,1)}, bf16[25,8,128]{2,1,0:T(8,128)(2,1)S(1)}, u32[]{:S(2)}, u32[]{:S(2)}) collective-permute-start(bf16[25,8,128]{2,1,0:T(8,128)(2,1)} %bitcast.64), channel_id=1, source_target_pairs={{0,16},{16,0},{1,17},{17,1},{2,18},{18,2},{3,19},{19,3},{4,20},{20... | collective-permute-start | bytes 153608 | tf_op jit(solution)/shard_map/ppermute | solution.py:435
  2.4 10.1 %collective-permute-start.2 = (bf16[2,25,8,128]{3,2,1,0:T(8,128)(2,1)S(1)}, bf16[2,25,8,128]{3,2,1,0:T(8,128)(2,1)S(1)}, u32[]{:S(2)}, u32[]{:S(2)}) collective-permute-start(bf16[2,25,8,128]{3,2,1,0:T(8,128)(2,1)S(1)} %get-tuple-element.32), channel_id=1, source_target_pairs={{0,8},{1,9},{2,10},{3,11},{4,12},{5,13},{6,14},{7,15},{8,0},{9,1},... | collective-permute-start | bytes 307208 | tf_op jit(solution)/shard_map/ppermute | solution.py:435
  6.4 6.2 %collective-permute-start.1 = (bf16[2,25,8,128]{3,2,1,0:T(8,128)(2,1)S(1)}, bf16[2,25,8,128]{3,2,1,0:T(8,128)(2,1)S(1)}, u32[]{:S(2)}, u32[]{:S(2)}) collective-permute-start(bf16[2,25,8,128]{3,2,1,0:T(8,128)(2,1)S(1)} %get-tuple-element.32), channel_id=1, source_target_pairs={{0,4},{1,5},{2,6},{3,7},{4,0},{5,1},{6,2},{7,3},{8,12},{9,13},{10,... | collective-permute-start | bytes 307208 | tf_op jit(solution)/shard_map/ppermute | solution.py:435
  8.0 7.2 %collective-permute-start.3 = (bf16[2,25,8,128]{3,2,1,0:T(8,128)(2,1)S(1)}, bf16[2,25,8,128]{3,2,1,0:T(8,128)(2,1)S(1)}, u32[]{:S(2)}, u32[]{:S(2)}) collective-permute-start(bf16[2,25,8,128]{3,2,1,0:T(8,128)(2,1)S(1)} %get-tuple-element.32), channel_id=1, source_target_pairs={{0,12},{1,13},{2,14},{3,15},{4,8},{5,9},{6,10},{7,11},{8,4},{9,5},... | collective-permute-start | bytes 307208 | tf_op jit(solution)/shard_map/ppermute | solution.py:435
  15.3 23.0 %collective-permute-start.6 = (bf16[4,2,25,8,128]{4,3,2,1,0:T(8,128)(2,1)S(1)}, bf16[4,2,25,8,128]{4,3,2,1,0:T(8,128)(2,1)S(1)}, u32[]{:S(2)}, u32[]{:S(2)}) collective-permute-start(bf16[4,2,25,8,128]{4,3,2,1,0:T(8,128)(2,1)S(1)} %pad_maximum_fusion.refs_10_), channel_id=1, source_target_pairs={{0,3},{1,2},{2,1},{3,0},{4,7},{5,6},{6,5},{7,4},{8,11},{9,10},{10,... | collective-permute-start | bytes 1228808 | tf_op jit(solution)/shard_map/ppermute | solution.py:435
  17.8 20.5 %collective-permute-start.5 = (bf16[4,2,25,8,128]{4,3,2,1,0:T(8,128)(2,1)S(1)}, bf16[4,2,25,8,128]{4,3,2,1,0:T(8,128)(2,1)S(1)}, u32[]{:S(2)}, u32[]{:S(2)}) collective-permute-start(bf16[4,2,25,8,128]{4,3,2,1,0:T(8,128)(2,1)S(1)} %pad_maximum_fusion.refs_10_), channel_id=1, source_target_pairs={{0,2},{1,3},{2,0},{3,1},{4,6},{5,7},{6,4},{7,5},{8,10},{9,11},{10,... | collective-permute-start | bytes 1228808 | tf_op jit(solution)/shard_map/ppermute | solution.py:435
  18.3 20.0 %collective-permute-start.4 = (bf16[4,2,25,8,128]{4,3,2,1,0:T(8,128)(2,1)S(1)}, bf16[4,2,25,8,128]{4,3,2,1,0:T(8,128)(2,1)S(1)}, u32[]{:S(2)}, u32[]{:S(2)}) collective-permute-start(bf16[4,2,25,8,128]{4,3,2,1,0:T(8,128)(2,1)S(1)} %pad_maximum_fusion.refs_10_), channel_id=1, source_target_pairs={{0,1},{1,0},{2,3},{3,2},{4,5},{5,4},{6,7},{7,6},{8,9},{9,8},{10,11... | collective-permute-start | bytes 1228808 | tf_op jit(solution)/shard_map/ppermute | solution.py:435
  18.8 11.1 %copy-start = (bf16[2,1024,512]{2,1,0:T(8,128)(2,1)S(1)}, bf16[2,1024,512]{2,1,0:T(8,128)(2,1)}, u32[]{:S(2)}) copy-start(bf16[2,1024,512]{2,1,0:T(8,128)(2,1)} %param.16) | copy-start | bytes 6291460
  18.8 11.1 %copy-start.1 = (bf16[1280,640]{1,0:T(8,128)(2,1)S(1)}, bf16[1280,640]{1,0:T(8,128)(2,1)}, u32[]{:S(2)}) copy-start(bf16[1280,640]{1,0:T(8,128)(2,1)} %param.15) | copy-start | bytes 4915204
  18.9 11.1 %copy-start.2 = (bf16[2,768,384]{2,1,0:T(8,128)(2,1)S(1)}, bf16[2,768,384]{2,1,0:T(8,128)(2,1)}, u32[]{:S(2)}) copy-start(bf16[2,768,384]{2,1,0:T(8,128)(2,1)} %param.17) | copy-start | bytes 3538948
  18.9 11.1 %copy-start.4 = (s32[1,1,512]{2,1,0:T(1,128)S(1)}, s32[1,1,512]{2,1,0:T(1,128)}, u32[]{:S(2)}) copy-start(s32[1,1,512]{2,1,0:T(1,128)} %param.11) | copy-start | bytes 6148
  30.0 8.4 %copy-start.3 = (s32[1,1,512]{2,1,0:T(1,128)S(1)}, s32[1,1,512]{2,1,0:T(1,128)}, u32[]{:S(2)}) copy-start(s32[1,1,512]{2,1,0:T(1,128)} %param.12) | copy-start | bytes 6148
  58.1 11.8 %collective-permute-start.7 = (bf16[4,25,8,128]{3,2,1,0:T(8,128)(2,1)S(1)}, bf16[4,25,8,128]{3,2,1,0:T(8,128)(2,1)S(1)}, u32[]{:S(2)}, u32[]{:S(2)}) collective-permute-start(bf16[4,25,8,128]{3,2,1,0:T(8,128)(2,1)S(1)} %get-tuple-element.25), channel_id=1, source_target_pairs={{0,1},{1,0},{2,3},{3,2},{4,5},{5,4},{6,7},{7,6},{8,9},{9,8},{10,11... | collective-permute-start | bytes 614408 | tf_op jit(solution)/shard_map/ppermute | solution.py:435
  59.6 10.2 %collective-permute-start.9 = (bf16[4,25,8,128]{3,2,1,0:T(8,128)(2,1)S(1)}, bf16[4,25,8,128]{3,2,1,0:T(8,128)(2,1)S(1)}, u32[]{:S(2)}, u32[]{:S(2)}) collective-permute-start(bf16[4,25,8,128]{3,2,1,0:T(8,128)(2,1)S(1)} %get-tuple-element.26), channel_id=1, source_target_pairs={{0,3},{1,2},{2,1},{3,0},{4,7},{5,6},{6,5},{7,4},{8,11},{9,10},{10,... | collective-permute-start | bytes 614408 | tf_op jit(solution)/shard_map/ppermute | solution.py:435
  61.1 9.2 %collective-permute-start.8 = (bf16[4,25,8,128]{3,2,1,0:T(8,128)(2,1)S(1)}, bf16[4,25,8,128]{3,2,1,0:T(8,128)(2,1)S(1)}, u32[]{:S(2)}, u32[]{:S(2)}) collective-permute-start(bf16[4,25,8,128]{3,2,1,0:T(8,128)(2,1)S(1)} %get-tuple-element.27), channel_id=1, source_target_pairs={{0,2},{1,3},{2,0},{3,1},{4,6},{5,7},{6,4},{7,5},{8,10},{9,11},{10,... | collective-permute-start | bytes 614408 | tf_op jit(solution)/shard_map/ppermute | solution.py:435
  69.7 6.7 %collective-permute-start.13 = (bf16[25,8,128]{2,1,0:T(8,128)(2,1)S(1)}, bf16[25,8,128]{2,1,0:T(8,128)(2,1)S(1)}, u32[]{:S(2)}, u32[]{:S(2)}) collective-permute-start(bf16[25,8,128]{2,1,0:T(8,128)(2,1)S(1)} %slice_bitcast_fusion.1), channel_id=1, source_target_pairs={{0,16},{16,0},{1,17},{17,1},{2,18},{18,2},{3,19},{19,3},{4,20},{20... | collective-permute-start | bytes 153608 | tf_op jit(solution)/shard_map/ppermute | solution.py:435
  70.4 6.0 %collective-permute-start.10 = (bf16[25,8,128]{2,1,0:T(8,128)(2,1)S(1)}, bf16[25,8,128]{2,1,0:T(8,128)(2,1)S(1)}, u32[]{:S(2)}, u32[]{:S(2)}) collective-permute-start(bf16[25,8,128]{2,1,0:T(8,128)(2,1)S(1)} %get-tuple-element.28), channel_id=1, source_target_pairs={{0,4},{1,5},{2,6},{3,7},{4,0},{5,1},{6,2},{7,3},{8,12},{9,13},{10,... | collective-permute-start | bytes 153608 | tf_op jit(solution)/shard_map/ppermute | solution.py:435
  73.1 6.1 %collective-permute-start.12 = (bf16[25,8,128]{2,1,0:T(8,128)(2,1)S(1)}, bf16[25,8,128]{2,1,0:T(8,128)(2,1)S(1)}, u32[]{:S(2)}, u32[]{:S(2)}) collective-permute-start(bf16[25,8,128]{2,1,0:T(8,128)(2,1)S(1)} %get-tuple-element.29), channel_id=1, source_target_pairs={{0,12},{1,13},{2,14},{3,15},{4,8},{5,9},{6,10},{7,11},{8,4},{9,5},... | collective-permute-start | bytes 153608 | tf_op jit(solution)/shard_map/ppermute | solution.py:435
  76.4 5.0 %collective-permute-start.11 = (bf16[25,8,128]{2,1,0:T(8,128)(2,1)S(1)}, bf16[25,8,128]{2,1,0:T(8,128)(2,1)S(1)}, u32[]{:S(2)}, u32[]{:S(2)}) collective-permute-start(bf16[25,8,128]{2,1,0:T(8,128)(2,1)S(1)} %get-tuple-element.30), channel_id=1, source_target_pairs={{0,8},{1,9},{2,10},{3,11},{4,12},{5,13},{6,14},{7,15},{8,0},{9,1},... | collective-permute-start | bytes 153608 | tf_op jit(solution)/shard_map/ppermute | solution.py:435

commit v3 on v2

--- a/solution.py
+++ b/solution.py
@@ -14,9 +14,10 @@
 GROUP = 8
 K_PAD = 20 * GROUP
 J_PAD = 26 * GROUP
+SLOTS = (0, 1, 2, 3, 4, -1, 5, 6, 7, 8, 9, 10, 11, 12, 13, 14, 15, -1, 16, 17, 18, -1)
 LANES = 256
+INNER = 4
 CHUNK = 256
-UNROLL = 4
 F32 = jnp.float32
 BF16 = jnp.bfloat16
 MIB = 1024 * 1024
@@ -27,41 +28,54 @@
     return lax.broadcasted_iota(jnp.int32, shape, axis)
 
 
-def expand_kernel(wig_ref, fwd_ref, bwd_ref, flat):
-    edges = wig_ref.shape[0]
-    width = wig_ref.shape[1]
-    flat[:, 384:512] = jnp.zeros((edges, 128), BF16)
-    flat[:, 0:width] = wig_ref[...]
+def flatten(wig_ref, flat):
+    flat[:, 384:512] = jnp.zeros((wig_ref.shape[0], 128), BF16)
+    flat[:, 0 : wig_ref.shape[1]] = wig_ref[...]
+
+
+def picked(operand, wanted):
+    edges, depth = operand.shape
     same_edge = (iota((edges, LANES), 0) % GROUP) == (iota((edges, LANES), 1) % GROUP)
-    source = iota((512, LANES), 0)
-    slot = iota((512, LANES), 1) // GROUP
-
-    def picked(wanted):
-        chosen = jnp.where(source == wanted, 1.0, 0.0).astype(BF16)
-        spread = jnp.dot(flat[...], chosen, preferred_element_type=F32)
-        return jnp.where(same_edge, spread, 0.0).reshape(edges // GROUP, GROUP, LANES)
+    chosen = jnp.where(iota((depth, LANES), 0) == wanted, 1.0, 0.0).astype(BF16)
+    spread = jnp.dot(operand, chosen, preferred_element_type=F32)
+    return jnp.where(same_edge, spread, 0.0).reshape(edges // GROUP, GROUP, LANES)
+
+
+def expand_fwd_kernel(wig_ref, fwd_ref, flat):
+    flatten(wig_ref, flat)
+    slot = iota((256, LANES), 1) // GROUP
 
     def fwd_step(pair, unused):
         parts = []
         for odd in range(2):
             k = pair * 2 + odd
-            wanted = jnp.where((slot < COEF) & (k < ROWS), k * COEF + slot, -1)
-            parts.append(picked(wanted))
-        start = pl.multiple_of(pair * 16, 16)
+            base = jnp.minimum(k * COEF // 128, 2) * 128
+            wanted = jnp.where((slot < COEF) & (k < ROWS), k * COEF + slot - base, -1)
+            parts.append(picked(flat[:, pl.ds(aligned(base, 128), 256)], wanted))
+        start = aligned(pair * 16, 16)
         fwd_ref[:, pl.ds(start, 16), :] = jnp.concatenate(parts, axis=1).astype(BF16)
         return unused
+
+    lax.fori_loop(0, K_PAD // 16, fwd_step, 0)
+
+
+def expand_bwd_kernel(wig_ref, bwd_ref, flat):
+    flatten(wig_ref, flat)
+    slot = iota((1, LANES), 1) // GROUP
+    row_of = jnp.full(slot.shape, -1, jnp.int32)
+    for n, k in enumerate(SLOTS):
+        row_of = jnp.where(slot == n, k, row_of)
 
     def bwd_step(pair, unused):
         parts = []
         for odd in range(2):
             j = pair * 2 + odd
-            wanted = jnp.where((slot < ROWS) & (j < COEF), slot * COEF + j, -1)
-            parts.append(picked(wanted))
-        start = pl.multiple_of(pair * 16, 16)
+            wanted = jnp.where((row_of >= 0) & (j < COEF), row_of * COEF + j, -1)
+            parts.append(picked(flat[...], wanted))
+        start = aligned(pair * 16, 16)
         bwd_ref[:, pl.ds(start, 16), :] = jnp.concatenate(parts, axis=1).astype(BF16)
         return unused
 
-    lax.fori_loop(0, K_PAD // 16, fwd_step, 0)
     lax.fori_loop(0, J_PAD // 16, bwd_step, 0)
 
 
@@ -84,31 +98,44 @@
     return place == iota((atoms, CHUNK), 0)
 
 
-def target_hot(ids_ref, chunk, atoms, inner):
+def target_hot(ids_ref, chunk, atoms):
     ids = ids_ref[:, pl.ds(aligned(chunk * CHUNK, CHUNK), CHUNK)]
     place = ids ^ (lax.axis_index("col") * 8)
     block = place // 8
-    outer = atoms // (8 * inner)
-    place = ((block % inner) * outer + block // inner) * 8 + place % 8
+    outer = atoms // (8 * INNER)
+    place = ((block % INNER) * outer + block // INNER) * 8 + place % 8
     return place == iota((atoms, CHUNK), 0)
 
 
-def gather_atoms(hot, table, gathered):
+def store_pair(packed, slot, first, second):
+    groups = packed.shape[0]
+    first = first.reshape(groups, GROUP, -1)
+    second = second.reshape(groups, GROUP, -1)
+    rows = slice(slot * GROUP, slot * GROUP + 2 * GROUP)
+    packed[:, rows, :] = jnp.concatenate([first, second], axis=1).astype(BF16)
+
+
+def clear_rows(packed, slots):
+    groups, rows, width = packed.shape
+    for g in range(groups):
+        packed[g, slots * GROUP :, :] = jnp.zeros((rows - slots * GROUP, width), packed.dtype)
+
+
+def gather_atoms(hot, table, packed):
     hot = jnp.where(hot, 1.0, 0.0).T.astype(BF16)
-    step = gathered.shape[1] // 5
-    for n in range(5):
-        gathered[:, n * step : (n + 1) * step] = jnp.dot(
-            hot, table[:, n * step : (n + 1) * step], preferred_element_type=F32
+    width = packed.shape[2]
+    for j in range(0, COEF, 2):
+        count = min(2, COEF - j)
+        value = jnp.dot(
+            hot, table[:, j * width : (j + count) * width], preferred_element_type=F32
         )
-
-
-def rotate_group(rot_ref, g, gathered, local_g):
-    width = gathered.shape[1] // COEF
-    start = aligned(local_g * GROUP, GROUP)
-    rows = [gathered[pl.ds(start, GROUP), j * width : (j + 1) * width] for j in range(COEF)]
-    rows.append(jnp.zeros((LANES - COEF * GROUP, width), F32))
-    right = jnp.concatenate(rows, axis=0).astype(BF16)
-    return jnp.dot(rot_ref[g], right, preferred_element_type=F32)
+        first = value[:, :width]
+        second = value[:, width:] if count == 2 else jnp.zeros_like(first)
+        store_pair(packed, j, first, second)
+
+
+def rotate_group(rot_ref, g, packed, local_g):
+    return jnp.dot(rot_ref[g], packed[local_g], preferred_element_type=F32)
 
 
 def pair_row(first, second, k, kind=0):
@@ -140,27 +167,20 @@
 def source_forward_kernel(*refs):
     ids_ref, feats_ref, rot_ref = refs[:3]
     w_refs, outs = refs[3:6], refs[6:9]
-    table, gathered, lefts = refs[9], refs[10], refs[11:]
+    table, packed, lefts = refs[9], refs[10], refs[11:]
     edges = ids_ref.shape[1]
     blocks = [lambda kind, j, b=b: feats_ref[b, j] for b in range(feats_ref.shape[0])]
     fill_table(blocks, table, 1)
+    clear_rows(packed, COEF + 1)
 
     def chunk_step(chunk, unused):
-        gather_atoms(source_hot(ids_ref, chunk, table.shape[0]), table, gathered)
-
-        def step(i, unused):
-            for u in range(0, UNROLL, 2):
-                g = i * UNROLL + u
-                pair = [
-                    rotate_group(rot_ref, chunk * (CHUNK // GROUP) + g + n, gathered, g + n)
-                    for n in range(2)
-                ]
-                top = pl.ds(aligned(g * GROUP, 16), 16)
-                low = pl.ds(aligned(g * GROUP + CHUNK, 16), 16)
-                store_forward(lambda k: pair_row(*pair, k), lefts, top, low)
-            return unused
-
-        lax.fori_loop(0, CHUNK // (GROUP * UNROLL), step, 0)
+        gather_atoms(source_hot(ids_ref, chunk, table.shape[0]), table, packed)
+
+        for g in range(0, CHUNK // GROUP, 2):
+            at = chunk * (CHUNK // GROUP) + g
+            pair = [rotate_group(rot_ref, at + n, packed, g + n) for n in range(2)]
+            top, low = slice(g * 8, g * 8 + 16), slice(CHUNK + g * 8, CHUNK + g * 8 + 16)
+            store_forward(lambda k: pair_row(*pair, k), lefts, top, low)
         for n in range(3):
             rows = lefts[n].shape[0]
             outs[n][pl.ds(aligned(chunk * rows, rows), rows), :] = jnp.dot(
@@ -179,43 +199,33 @@
     return out
 
 
-def back_half(half, chunk, lefts, w_refs, rot_ref, grad_in, edge_grad):
-    for n in range(3):
+def back_half(half, chunk, lefts, w_refs, rot_ref, packed, edge_grad):
+    for n, count, slot in ((0, 5, 0), (1, 4, 6), (2, 3, 14)):
         width = w_refs[n].shape[-1]
-        rows = grad_in[n].shape[0]
+        rows = CHUNK if n == 0 else 2 * CHUNK
         here = pl.ds(aligned(chunk * rows, rows), rows)
-        if n == 0:
-            weight = w_refs[n][:, half].reshape(-1, width)
-            grad_in[n][...] = lax.dot_general(
-                lefts[n][here, :], weight, NT, preferred_element_type=F32
-            )
-        else:
-            real = w_refs[n][0, :, half].reshape(-1, width)
-            imag = w_refs[n][1, :, half].reshape(-1, width)
-            grad_in[n][...] = lax.dot_general(
-                lefts[n][here, :width], real, NT, preferred_element_type=F32
-            ) + lax.dot_general(lefts[n][here, width:], imag, NT, preferred_element_type=F32)
-
-    def one(g):
-        rows = []
-        for which, row, n in y_slices(g * GROUP):
-            rows.append(grad_in[which][pl.ds(aligned(row, GROUP), GROUP), n * C : (n + 1) * C])
-        rows.append(jnp.zeros((LANES - ROWS * GROUP, C), F32))
-        right = jnp.concatenate(rows, axis=0).astype(BF16)
-        return jnp.dot(
-            rot_ref[chunk * (CHUNK // GROUP) + g], right, preferred_element_type=F32
-        )
-
-    def step(i, unused):
-        for u in range(0, UNROLL, 2):
-            g = i * UNROLL + u
-            first, second = one(g), one(g + 1)
-            top = pl.ds(aligned(g * GROUP, 16), 16)
-            for j in range(COEF):
-                edge_grad[top, j * C : (j + 1) * C] = pair_row(first, second, j).astype(BF16)
-        return unused
-
-    lax.fori_loop(0, CHUNK // (GROUP * UNROLL), step, 0)
+        for k in range(0, count, 2):
+            until = min(k + 2, count)
+            if n == 0:
+                weight = w_refs[n][k:until, half].reshape(-1, width)
+                value = lax.dot_general(lefts[n][here, :], weight, NT, preferred_element_type=F32)
+            else:
+                real = w_refs[n][0, k:until, half].reshape(-1, width)
+                imag = w_refs[n][1, k:until, half].reshape(-1, width)
+                value = lax.dot_general(
+                    lefts[n][here, :width], real, NT, preferred_element_type=F32
+                ) + lax.dot_general(lefts[n][here, width:], imag, NT, preferred_element_type=F32)
+            for sign in range(rows // CHUNK):
+                part = value[sign * CHUNK : (sign + 1) * CHUNK]
+                first = part[:, :C]
+                second = part[:, C:] if until - k == 2 else jnp.zeros_like(first)
+                store_pair(packed, slot + sign * (count + 1) // 2 * 2 + k, first, second)
+
+    at = chunk * (CHUNK // GROUP)
+    for g in range(0, CHUNK // GROUP, 2):
+        pair = [rotate_group(rot_ref, at + g + n, packed, g + n) for n in range(2)]
+        for j in range(COEF):
+            edge_grad[g * 8 : g * 8 + 16, j * C : (j + 1) * C] = pair_row(*pair, j).astype(BF16)
 
 
 def scatter_atoms(hot, count_ref, chunk, edge_grad, total):
@@ -239,36 +249,30 @@
     pieces = refs[10 : 10 + count_pieces]
     refs = refs[10 + count_pieces :]
     lefts, out_ref = refs[:3], refs[3]
-    table, gathered = refs[4], refs[5]
-    forward_lefts, cots, ys, grad_in = refs[6:9], refs[9], refs[10:13], refs[13:16]
-    edge_grad, total = refs[16], refs[17]
+    table, packed = refs[4], refs[5]
+    forward_lefts, cots, ys, packed_back = refs[6:9], refs[9], refs[10:13], refs[13]
+    edge_grad, total = refs[14], refs[15]
     edges = ids_ref.shape[1]
     blocks = []
     for piece in pieces:
         for b in range(piece.shape[0]):
             blocks.append(lambda kind, j, piece=piece, b=b: piece[b, kind, j])
     fill_table(blocks, table, 2)
+    clear_rows(packed, COEF + 1)
+    clear_rows(packed_back, len(SLOTS))
     total[...] = jnp.zeros_like(total)
 
     def chunk_step(chunk, unused):
-        hot = target_hot(ids_ref, chunk, table.shape[0], count_pieces)
-        gather_atoms(hot, table, gathered)
-
-        def turn(i, unused):
-            for u in range(0, UNROLL, 2):
-                g = i * UNROLL + u
-                pair = [
-                    rotate_group(fwd_ref, chunk * (CHUNK // GROUP) + g + n, gathered, g + n)
-                    for n in range(2)
-                ]
-                top = pl.ds(aligned(g * GROUP, 16), 16)
-                low = pl.ds(aligned(g * GROUP + CHUNK, 16), 16)
-                store_forward(lambda k: pair_row(*pair, k), forward_lefts, top, low)
-                for k in range(ROWS):
-                    cots[top, k * C : (k + 1) * C] = pair_row(*pair, k, 1).astype(BF16)
-            return unused
-
-        lax.fori_loop(0, CHUNK // (GROUP * UNROLL), turn, 0)
+        hot = target_hot(ids_ref, chunk, table.shape[0])
+        gather_atoms(hot, table, packed)
+
+        for g in range(0, CHUNK // GROUP, 2):
+            at = chunk * (CHUNK // GROUP) + g
+            pair = [rotate_group(fwd_ref, at + n, packed, g + n) for n in range(2)]
+            top, low = slice(g * 8, g * 8 + 16), slice(CHUNK + g * 8, CHUNK + g * 8 + 16)
+            store_forward(lambda k: pair_row(*pair, k), forward_lefts, top, low)
+            for k in range(ROWS):
+                cots[top, k * C : (k + 1) * C] = pair_row(*pair, k, 1).astype(BF16)
         for n in range(3):
             rows = forward_lefts[n].shape[0]
             ys[n][...] = sources[n][pl.ds(aligned(chunk * rows, rows), rows), :] + jnp.dot(
@@ -299,9 +303,9 @@
             store_backward(grads, lefts, zero_row, top_row, low_row)
             return unused
 
-        lax.fori_loop(0, CHUNK // 16, gate, 0)
-        back_half(1, chunk, lefts, w_refs, bwd_ref, grad_in, edge_grad)
-        hot = target_hot(ids_ref, chunk, table.shape[0], count_pieces)
+        lax.fori_loop(0, CHUNK // 16, gate, 0, unroll=4)
+        back_half(1, chunk, lefts, w_refs, bwd_ref, packed_back, edge_grad)
+        hot = target_hot(ids_ref, chunk, table.shape[0])
         scatter_atoms(hot, count_ref, chunk, edge_grad, total)
         return unused
 
@@ -327,11 +331,12 @@
 def source_back_kernel(*refs):
     ids_ref, count_ref, bwd_ref = refs[:3]
     w_refs, lefts, out_ref = refs[3:6], refs[6:9], refs[9]
-    grad_in, edge_grad, total = refs[10:13], refs[13], refs[14]
+    packed, edge_grad, total = refs[10:]
+    clear_rows(packed, len(SLOTS))
     total[...] = jnp.zeros_like(total)
 
     def chunk_step(chunk, unused):
-        back_half(0, chunk, lefts, w_refs, bwd_ref, grad_in, edge_grad)
+        back_half(0, chunk, lefts, w_refs, bwd_ref, packed, edge_grad)
         scatter_atoms(source_hot(ids_ref, chunk, total.shape[0]), count_ref, chunk, edge_grad, total)
         return unused
 
@@ -372,20 +377,22 @@
     return [(s, dtype) for s in shapes]
 
 
+def packed_shape(kinds):
+    return (CHUNK // GROUP, LANES, kinds * C)
+
+
 PUSH = 2 * 65536
 
 
-def expand(wig):
+def expand(kernel, rows, wig):
     edges = wig.shape[0]
-    groups = edges // GROUP
-    outs = arrays([(groups, K_PAD, LANES), (groups, J_PAD, LANES)], BF16)
-    scratch = [((edges, 512), BF16)]
-    return call(expand_kernel, [wig], outs, scratch, 12, PUSH * edges * 92)
+    outs = arrays([(edges // GROUP, rows, LANES)], BF16)
+    return call(kernel, [wig], outs, [((edges, 512), BF16)], 6, PUSH * edges * 40)[0]
 
 
 def source_forward(ids, feats, rot, weights):
     edges = ids.shape[1]
-    scratch = [((feats.shape[0] * 8, COEF * C), BF16), ((CHUNK, COEF * C), F32)]
+    scratch = [((feats.shape[0] * 8, COEF * C), BF16), (packed_shape(1), BF16)]
     scratch += typed(left_shapes(CHUNK), BF16)
     return call(
         source_forward_kernel,
@@ -401,9 +408,9 @@
     edges = ids.shape[1]
     blocks = sum(p.shape[0] for p in pieces)
     outs = arrays(left_shapes(edges), BF16) + arrays([(blocks, COEF, 8, C)], BF16)
-    scratch = [((blocks * 8, 2 * COEF * C), BF16), ((CHUNK, 2 * COEF * C), F32)]
+    scratch = [((blocks * 8, 2 * COEF * C), BF16), (packed_shape(2), BF16)]
     scratch += typed(left_shapes(CHUNK), BF16) + [((CHUNK, ROWS * C), BF16)]
-    scratch += typed(y_shapes(CHUNK), F32) * 2
+    scratch += typed(y_shapes(CHUNK), F32) + [(packed_shape(1), BF16)]
     scratch += [((CHUNK, COEF * C), BF16), ((blocks * 8, COEF * C), F32)]
     return call(
         functools.partial(target_kernel, len(pieces)),
@@ -417,7 +424,7 @@
 
 
 def source_back(ids, count, bwd, weights, lefts, blocks):
-    scratch = typed(y_shapes(CHUNK), F32)
+    scratch = [(packed_shape(1), BF16)]
     scratch += [((CHUNK, COEF * C), BF16), ((blocks * 8, COEF * C), F32)]
     return call(
         source_back_kernel,
@@ -437,19 +444,20 @@
 
 def step(node_feats, grad_out, edge_src, edge_tgt, count, wigner, w_zero, w_one, w_two):
     rows, cols = lax.axis_size("row"), lax.axis_size("col")
-    inner = 4
-    outer = cols // inner
+    inner, outer = INNER, cols // INNER
     feats = node_feats.transpose(1, 0, 2)
     own = jnp.stack([feats, grad_out.transpose(1, 0, 2)])
-    source_feats = [feats] + [exchange(feats, "row", d) for d in range(1, rows)]
-    source_feats = jnp.stack(source_feats)
     line = [own]
     for d in range(1, outer):
         line.append(exchange(own, "col", inner * d))
     line = jnp.stack(line)
-    pieces = [line]
-    for d in range(1, inner):
-        pieces.append(exchange(line, "col", d))
+    source_feats = [feats] + [exchange(feats, "row", d) for d in range(1, rows)]
+    source_feats = jnp.stack(source_feats)
+    first = exchange(line, "col", 1)
+    second = exchange(line, "col", 2)
+    far_first = exchange(first[: outer // 2], "col", 2)
+    far_second = exchange(second[outer // 2 :], "col", 1)
+    pieces = [line, first, second, far_first, far_second]
 
     weights = (
         w_zero.reshape(5, 2, C, 5 * C),
@@ -458,7 +466,8 @@
     )
     edges = edge_src.shape[-1]
     src, tgt = edge_src.reshape(1, edges), edge_tgt.reshape(1, edges)
-    fwd, bwd = expand(wigner[0, 0])
+    fwd = expand(expand_fwd_kernel, K_PAD, wigner[0, 0])
+    bwd = expand(expand_bwd_kernel, J_PAD, wigner[0, 0])
     sources = source_forward(src, source_feats, fwd, weights)
     *lefts, tile_tgt = target_work(tgt, count, fwd, bwd, weights, sources, pieces)
     tile_src = source_back(src, count, bwd, weights, lefts, rows)

time: 82.3 us -> 73 us (0.89)
  Pallas kernels: 46.5 us -> 35.3 us
  starting transfers between devices: 19.2 us -> 20.3 us
    pallas_call x4 -> x5, Pallas kernels: 46.5 us -> 35.3 us  [call(): pl.pallas_call(kernel, in_specs=[IN_SMEM if n == scalar else IN_VMEM for...]
    ppermute x14 -> x15, starting transfers between devices: 19.2 us -> 20.3 us  [exchange(): return lax.ppermute(value, axis, [(i, i ^ distance) for i in range(size)])]
    ppermute x14 -> x15, waiting for transfers between devices: 12.5 us -> 13.3 us  [exchange(): return lax.ppermute(value, axis, [(i, i ^ distance) for i in range(size)])]
  transfers between devices with their start and end apart: 14 -> 15, of which waited for: 6 -> 7; matrix products, arithmetic and copies ran while one was open for 2% -> 2% of each run, Pallas kernels for 33% -> 28%
where the time goes in v3:
time: 73 us; the launch traced here: 72.8 us
  Pallas kernels  35.3 us (48%)
  starting transfers between devices  20.3 us (28%)
  waiting for transfers between devices  13.3 us (18%)
  other arithmetic  1.71 us (2%)
  local copies, waits for them, and re-layouts  1.37 us (2%)
  between operations  0.84 us (1%)
    pallas_call x5, Pallas kernels, call(): pl.pallas_call(kernel, in_specs=[IN_SMEM if n == scalar else IN_VMEM for...  35.3 us
    ppermute x15, starting transfers between devices, exchange(): return lax.ppermute(value, axis, [(i, i ^ distance) for i in range(size)])  20.3 us
    ppermute x15, waiting for transfers between devices, exchange(): return lax.ppermute(value, axis, [(i, i ^ distance) for i in range(size)])  13.3 us
  transfers between devices with their start and end apart: 15, of which 7 were waited for; matrix products, arithmetic and copies ran while one was open for 2% of the time, Pallas kernels for 28%

profile of v3, /device:TPU:0, one launch (start us, length us, event | category | flops | bytes accessed | tf_op | source)
XLA Modules:
  0.0 72.8 jit_solution(7808083246767820102)
XLA Ops:
  0.0 0.5 collective-permute-start
  0.5 1.1 %collective-permute-done = bf16[25,8,128]{2,1,0:T(8,128)(2,1)S(1)} collective-permute-done((bf16[25,8,128]{2,1,0:T(8,128)(2,1)}, bf16[25,8,128]{2,1,0:T(8,128)(2,1)S(1)}, u32[]{:S(2)}, u32[]{:S(2)}) %collective-permute-start) | collective-permute-done | bytes 51232 | tf_op jit(solution)/shard_map/ppermute | solution.py:442
  1.6 0.8 %fusion.6 = (bf16[1,2,25,8,128]{4,3,2,1,0:T(8,128)(2,1)S(1)}, bf16[2,25,8,128]{3,2,1,0:T(8,128)(2,1)S(1)}, bf16[2,25,8,128]{3,2,1,0:T(8,128)(2,1)S(1)}) fusion(bf16[1,25,8,128]{3,2,1,0:T(8,128)(2,1)} %bitcast.64, bf16[1,25,8,128]{3,2,1,0:T(8,128)(2,1)} %bitcast.66, bf16[1,25,8,128]{3,2,1,0:T(8,128)(2,1)S(1)} %bitcast.67), kind=kLoop, calls=%fused_computation.16 | loop fusion | flops 102400 | bytes 460800 | tf_op jit(solution)/shard_map/stack | solution.py:453
  2.4 4.0 %collective-permute-start.2 = (bf16[2,25,8,128]{3,2,1,0:T(8,128)(2,1)S(1)}, bf16[2,25,8,128]{3,2,1,0:T(8,128)(2,1)S(1)}, u32[]{:S(2)}, u32[]{:S(2)}) collective-permute-start(bf16[2,25,8,128]{3,2,1,0:T(8,128)(2,1)S(1)} %get-tuple-element.28), channel_id=1, source_target_pairs={{0,8},{1,9},{2,10},{3,11},{4,12},{5,13},{6,14},{7,15},{8,0},{9,1},... | collective-permute-start | bytes 307208 | tf_op jit(solution)/shard_map/ppermute | solution.py:442
  6.4 1.6 %collective-permute-start.1 = (bf16[2,25,8,128]{3,2,1,0:T(8,128)(2,1)S(1)}, bf16[2,25,8,128]{3,2,1,0:T(8,128)(2,1)S(1)}, u32[]{:S(2)}, u32[]{:S(2)}) collective-permute-start(bf16[2,25,8,128]{3,2,1,0:T(8,128)(2,1)S(1)} %get-tuple-element.28), channel_id=1, source_target_pairs={{0,4},{1,5},{2,6},{3,7},{4,0},{5,1},{6,2},{7,3},{8,12},{9,13},{10,... | collective-permute-start | bytes 307208 | tf_op jit(solution)/shard_map/ppermute | solution.py:442
  8.0 0.0 collective-permute-start.3
  8.7 1.2 %copy.10 = bf16[1,1,512,475]{3,2,1,0:T(8,128)(2,1)S(1)} copy(bf16[1,1,512,475]{2,3,1,0:T(8,128)(2,1)} %param.14) | data formatting | bytes 972800 | tf_op args[5]
  9.9 2.7 %collective-permute-done.2 = bf16[2,25,8,128]{3,2,1,0:T(8,128)(2,1)S(1)} collective-permute-done((bf16[2,25,8,128]{3,2,1,0:T(8,128)(2,1)S(1)}, bf16[2,25,8,128]{3,2,1,0:T(8,128)(2,1)S(1)}, u32[]{:S(2)}, u32[]{:S(2)}) %collective-permute-start.2) | collective-permute-done | bytes 102432 | tf_op jit(solution)/shard_map/ppermute | solution.py:442
  12.6 0.0 collective-permute-done.1
  12.6 2.6 %collective-permute-done.3 = bf16[2,25,8,128]{3,2,1,0:T(8,128)(2,1)S(1)} collective-permute-done((bf16[2,25,8,128]{3,2,1,0:T(8,128)(2,1)S(1)}, bf16[2,25,8,128]{3,2,1,0:T(8,128)(2,1)S(1)}, u32[]{:S(2)}, u32[]{:S(2)}) %collective-permute-start.3) | collective-permute-done | bytes 102432 | tf_op jit(solution)/shard_map/ppermute | solution.py:442
  15.2 0.1 pad_maximum_fusion.refs_10_
  15.3 1.6 %collective-permute-start.5 = (bf16[4,2,25,8,128]{4,3,2,1,0:T(8,128)(2,1)S(1)}, bf16[4,2,25,8,128]{4,3,2,1,0:T(8,128)(2,1)S(1)}, u32[]{:S(2)}, u32[]{:S(2)}) collective-permute-start(bf16[4,2,25,8,128]{4,3,2,1,0:T(8,128)(2,1)S(1)} %pad_maximum_fusion.refs_10_), channel_id=1, source_target_pairs={{0,2},{1,3},{2,0},{3,1},{4,6},{5,7},{6,4},{7,5},{8,10},{9,11},{10,... | collective-permute-start | bytes 1228808 | tf_op jit(solution)/shard_map/ppermute | solution.py:442
  16.9 1.5 %collective-permute-start.4 = (bf16[4,2,25,8,128]{4,3,2,1,0:T(8,128)(2,1)S(1)}, bf16[4,2,25,8,128]{4,3,2,1,0:T(8,128)(2,1)S(1)}, u32[]{:S(2)}, u32[]{:S(2)}) collective-permute-start(bf16[4,2,25,8,128]{4,3,2,1,0:T(8,128)(2,1)S(1)} %pad_maximum_fusion.refs_10_), channel_id=1, source_target_pairs={{0,1},{1,0},{2,3},{3,2},{4,5},{5,4},{6,7},{7,6},{8,9},{9,8},{10,11... | collective-permute-start | bytes 1228808 | tf_op jit(solution)/shard_map/ppermute | solution.py:442
  18.4 3.2 %shard_map.91.refs_2_ = bf16[64,160,256]{2,1,0:T(8,128)(2,1)S(1)} custom-call(bf16[512,475]{1,0:T(8,128)(2,1)S(1)} %bitcast.47), custom_call_target="tpu_custom_call" | custom-call | flops 2684354560 | bytes 5729280 | tf_op jit(solution)/shard_map/pallas_call | solution.py:353
  21.6 0.0 copy-start
  21.6 0.0 copy-start.1
  21.6 0.0 copy-start.2
  21.7 0.0 copy-start.4
  21.7 5.8 %shard_map.92.refs_3_.refs_2_ = bf16[64,208,256]{2,1,0:T(8,128)(2,1)S(1)} custom-call(bf16[512,475]{1,0:T(8,128)(2,1)S(1)} %bitcast.48), custom_call_target="tpu_custom_call" | custom-call | flops 2684354560 | bytes 7302144 | tf_op jit(solution)/shard_map/pallas_call | solution.py:353
  27.5 0.0 collective-permute-done.5.refs_12_
  27.6 0.6 collective-permute-start.7
  28.2 0.0 collective-permute-done.4.refs_11_
  28.2 0.9 %collective-permute-start.6 = (bf16[2,2,25,8,128]{4,3,2,1,0:T(8,128)(2,1)S(1)}, bf16[2,2,25,8,128]{4,3,2,1,0:T(8,128)(2,1)S(1)}, u32[]{:S(2)}, u32[]{:S(2)}) collective-permute-start(bf16[2,2,25,8,128]{4,3,2,1,0:T(8,128)(2,1)S(1)} %slice.52), channel_id=1, source_target_pairs={{0,2},{1,3},{2,0},{3,1},{4,6},{5,7},{6,4},{7,5},{8,10},{9,11},{10,... | collective-permute-start | bytes 614408 | tf_op jit(solution)/shard_map/ppermute | solution.py:442
  29.1 0.0 copy-done
  29.1 0.0 copy-done.1
  29.1 0.0 copy-done.2
  29.1 0.0 copy-start.3
  29.1 5.6 %shard_map.93 = (f32[512,640]{1,0:T(8,128)S(1)}, f32[1024,512]{1,0:T(8,128)S(1)}, f32[1024,384]{1,0:T(8,128)S(1)}) custom-call(s32[1,512]{1,0:T(1,128)S(1)} %bitcast.59, bf16[2,25,8,128]{3,2,1,0:T(8,128)(2,1)S(1)} %get-tuple-element.29.refs_1_, bf16[64,160,256]{2,1,0:T(8,128)(2,1)S(1)} %shard_map.91.refs_2_, bf16[5,2,128,640]{3,2,1,0:T(8,128)(2,1)S(1)} %bitcast.52, ...), custom_call_target="tpu_custom_call" | custom-call | flops 4294967296 | bytes 15243264 | tf_op jit(solution)/shard_map/pallas_call | solution.py:353
  34.7 0.0 collective-permute-done.7.refs_14_
  34.7 0.0 collective-permute-done.6.refs_13_
  34.8 14.6 %shard_map.94 = (bf16[512,640]{1,0:T(8,128)(2,1)S(1)}, bf16[1024,1024]{1,0:T(8,128)(2,1)S(1)}, bf16[1024,768]{1,0:T(8,128)(2,1)S(1)}, bf16[16,25,8,128]{3,2,1,0:T(8,128)(2,1)S(1)}) custom-call(s32[1,512]{1,0:T(1,128)S(1)} %bitcast.58, s32[1,1]{1,0:T(1,128)S(6)} %copy.11.refs_1_, bf16[64,160,256]{2,1,0:T(8,128)(2,1)S(1)} %shard_map.91.refs_2_, ...), custom_call_target="tpu_custom_call" | custom-call | flops 10737418240 | bytes 28739588 | tf_op jit(solution)/shard_map/pallas_call | solution.py:353
  49.4 1.2 %collective-permute-start.8 = (bf16[4,25,8,128]{3,2,1,0:T(8,128)(2,1)S(1)}, bf16[4,25,8,128]{3,2,1,0:T(8,128)(2,1)S(1)}, u32[]{:S(2)}, u32[]{:S(2)}) collective-permute-start(bf16[4,25,8,128]{3,2,1,0:T(8,128)(2,1)S(1)} %get-tuple-element.21), channel_id=1, source_target_pairs={{0,1},{1,0},{2,3},{3,2},{4,5},{5,4},{6,7},{7,6},{8,9},{9,8},{10,11... | collective-permute-start | bytes 614408 | tf_op jit(solution)/shard_map/ppermute | solution.py:442
  50.6 1.5 %collective-permute-start.10 = (bf16[4,25,8,128]{3,2,1,0:T(8,128)(2,1)S(1)}, bf16[4,25,8,128]{3,2,1,0:T(8,128)(2,1)S(1)}, u32[]{:S(2)}, u32[]{:S(2)}) collective-permute-start(bf16[4,25,8,128]{3,2,1,0:T(8,128)(2,1)S(1)} %get-tuple-element.22), channel_id=1, source_target_pairs={{0,3},{1,2},{2,1},{3,0},{4,7},{5,6},{6,5},{7,4},{8,11},{9,10},{10,... | collective-permute-start | bytes 614408 | tf_op jit(solution)/shard_map/ppermute | solution.py:442
  52.1 0.9 %collective-permute-start.9 = (bf16[4,25,8,128]{3,2,1,0:T(8,128)(2,1)S(1)}, bf16[4,25,8,128]{3,2,1,0:T(8,128)(2,1)S(1)}, u32[]{:S(2)}, u32[]{:S(2)}) collective-permute-start(bf16[4,25,8,128]{3,2,1,0:T(8,128)(2,1)S(1)} %get-tuple-element.23), channel_id=1, source_target_pairs={{0,2},{1,3},{2,0},{3,1},{4,6},{5,7},{6,4},{7,5},{8,10},{9,11},{10,... | collective-permute-start | bytes 614408 | tf_op jit(solution)/shard_map/ppermute | solution.py:442
  53.0 6.1 %shard_map.95 = bf16[2,25,8,128]{3,2,1,0:T(8,128)(2,1)S(1)} custom-call(s32[1,512]{1,0:T(1,128)S(1)} %bitcast.60, s32[1,1]{1,0:T(1,128)S(6)} %copy.11.refs_1_, bf16[64,208,256]{2,1,0:T(8,128)(2,1)S(1)} %shard_map.92.refs_3_.refs_2_, bf16[5,2,128,640]{3,2,1,0:T(8,128)(2,1)S(1)} %bitcast.54, bf16[2,4,2,128,512]{4,3,2,1,0:T(8,128)(2,1)S(1)} %bitcast.51, ...), custom_call_target="tpu_custom_call" | custom-call | flops 4697620480 | bytes 16160772 | tf_op jit(solution)/shard_map/pallas_call | solution.py:353
  59.0 0.1 collective-permute-start.14
  59.1 0.0 collective-permute-done.8
  59.1 0.5 collective-permute-done.10
  59.6 1.4 %collective-permute-done.9 = bf16[4,25,8,128]{3,2,1,0:T(8,128)(2,1)S(1)} collective-permute-done((bf16[4,25,8,128]{3,2,1,0:T(8,128)(2,1)S(1)}, bf16[4,25,8,128]{3,2,1,0:T(8,128)(2,1)S(1)}, u32[]{:S(2)}, u32[]{:S(2)}) %collective-permute-start.9) | collective-permute-done | bytes 204832 | tf_op jit(solution)/shard_map/ppermute | solution.py:442
  61.0 0.1 fusion.7
  61.1 2.6 %collective-permute-start.11 = (bf16[25,8,128]{2,1,0:T(8,128)(2,1)S(1)}, bf16[25,8,128]{2,1,0:T(8,128)(2,1)S(1)}, u32[]{:S(2)}, u32[]{:S(2)}) collective-permute-start(bf16[25,8,128]{2,1,0:T(8,128)(2,1)S(1)} %get-tuple-element.24), channel_id=1, source_target_pairs={{0,4},{1,5},{2,6},{3,7},{4,0},{5,1},{6,2},{7,3},{8,12},{9,13},{10,... | collective-permute-start | bytes 153608 | tf_op jit(solution)/shard_map/ppermute | solution.py:442
  63.7 3.4 %collective-permute-start.13 = (bf16[25,8,128]{2,1,0:T(8,128)(2,1)S(1)}, bf16[25,8,128]{2,1,0:T(8,128)(2,1)S(1)}, u32[]{:S(2)}, u32[]{:S(2)}) collective-permute-start(bf16[25,8,128]{2,1,0:T(8,128)(2,1)S(1)} %get-tuple-element.25), channel_id=1, source_target_pairs={{0,12},{1,13},{2,14},{3,15},{4,8},{5,9},{6,10},{7,11},{8,4},{9,5},... | collective-permute-start | bytes 153608 | tf_op jit(solution)/shard_map/ppermute | solution.py:442
  67.1 0.0 collective-permute-start.12
  67.1 0.0 collective-permute-done.14
  67.1 0.0 collective-permute-done.11
  67.1 2.7 %collective-permute-done.13 = bf16[25,8,128]{2,1,0:T(8,128)(2,1)S(1)} collective-permute-done((bf16[25,8,128]{2,1,0:T(8,128)(2,1)S(1)}, bf16[25,8,128]{2,1,0:T(8,128)(2,1)S(1)}, u32[]{:S(2)}, u32[]{:S(2)}) %collective-permute-start.13) | collective-permute-done | bytes 51232 | tf_op jit(solution)/shard_map/ppermute | solution.py:442
  69.8 2.3 %collective-permute-done.12 = bf16[25,8,128]{2,1,0:T(8,128)(2,1)S(1)} collective-permute-done((bf16[25,8,128]{2,1,0:T(8,128)(2,1)S(1)}, bf16[25,8,128]{2,1,0:T(8,128)(2,1)S(1)}, u32[]{:S(2)}, u32[]{:S(2)}) %collective-permute-start.12) | collective-permute-done | bytes 51232 | tf_op jit(solution)/shard_map/ppermute | solution.py:442
  72.1 0.7 fusion.5
  (7 shorter events, 0.1 us)
Async XLA Ops:
  0.0 1.6 %collective-permute-start = (bf16[25,8,128]{2,1,0:T(8,128)(2,1)}, bf16[25,8,128]{2,1,0:T(8,128)(2,1)S(1)}, u32[]{:S(2)}, u32[]{:S(2)}) collective-permute-start(bf16[25,8,128]{2,1,0:T(8,128)(2,1)} %bitcast.65), channel_id=1, source_target_pairs={{0,16},{16,0},{1,17},{17,1},{2,18},{18,2},{3,19},{19,3},{4,20},{20... | collective-permute-start | bytes 153608 | tf_op jit(solution)/shard_map/ppermute | solution.py:442
  2.4 10.1 %collective-permute-start.2 = (bf16[2,25,8,128]{3,2,1,0:T(8,128)(2,1)S(1)}, bf16[2,25,8,128]{3,2,1,0:T(8,128)(2,1)S(1)}, u32[]{:S(2)}, u32[]{:S(2)}) collective-permute-start(bf16[2,25,8,128]{3,2,1,0:T(8,128)(2,1)S(1)} %get-tuple-element.28), channel_id=1, source_target_pairs={{0,8},{1,9},{2,10},{3,11},{4,12},{5,13},{6,14},{7,15},{8,0},{9,1},... | collective-permute-start | bytes 307208 | tf_op jit(solution)/shard_map/ppermute | solution.py:442
  6.4 6.2 %collective-permute-start.1 = (bf16[2,25,8,128]{3,2,1,0:T(8,128)(2,1)S(1)}, bf16[2,25,8,128]{3,2,1,0:T(8,128)(2,1)S(1)}, u32[]{:S(2)}, u32[]{:S(2)}) collective-permute-start(bf16[2,25,8,128]{3,2,1,0:T(8,128)(2,1)S(1)} %get-tuple-element.28), channel_id=1, source_target_pairs={{0,4},{1,5},{2,6},{3,7},{4,0},{5,1},{6,2},{7,3},{8,12},{9,13},{10,... | collective-permute-start | bytes 307208 | tf_op jit(solution)/shard_map/ppermute | solution.py:442
  8.0 7.2 %collective-permute-start.3 = (bf16[2,25,8,128]{3,2,1,0:T(8,128)(2,1)S(1)}, bf16[2,25,8,128]{3,2,1,0:T(8,128)(2,1)S(1)}, u32[]{:S(2)}, u32[]{:S(2)}) collective-permute-start(bf16[2,25,8,128]{3,2,1,0:T(8,128)(2,1)S(1)} %get-tuple-element.28), channel_id=1, source_target_pairs={{0,12},{1,13},{2,14},{3,15},{4,8},{5,9},{6,10},{7,11},{8,4},{9,5},... | collective-permute-start | bytes 307208 | tf_op jit(solution)/shard_map/ppermute | solution.py:442
  15.3 12.2 %collective-permute-start.5 = (bf16[4,2,25,8,128]{4,3,2,1,0:T(8,128)(2,1)S(1)}, bf16[4,2,25,8,128]{4,3,2,1,0:T(8,128)(2,1)S(1)}, u32[]{:S(2)}, u32[]{:S(2)}) collective-permute-start(bf16[4,2,25,8,128]{4,3,2,1,0:T(8,128)(2,1)S(1)} %pad_maximum_fusion.refs_10_), channel_id=1, source_target_pairs={{0,2},{1,3},{2,0},{3,1},{4,6},{5,7},{6,4},{7,5},{8,10},{9,11},{10,... | collective-permute-start | bytes 1228808 | tf_op jit(solution)/shard_map/ppermute | solution.py:442
  16.9 11.3 %collective-permute-start.4 = (bf16[4,2,25,8,128]{4,3,2,1,0:T(8,128)(2,1)S(1)}, bf16[4,2,25,8,128]{4,3,2,1,0:T(8,128)(2,1)S(1)}, u32[]{:S(2)}, u32[]{:S(2)}) collective-permute-start(bf16[4,2,25,8,128]{4,3,2,1,0:T(8,128)(2,1)S(1)} %pad_maximum_fusion.refs_10_), channel_id=1, source_target_pairs={{0,1},{1,0},{2,3},{3,2},{4,5},{5,4},{6,7},{7,6},{8,9},{9,8},{10,11... | collective-permute-start | bytes 1228808 | tf_op jit(solution)/shard_map/ppermute | solution.py:442
  21.6 7.5 %copy-start = (bf16[2,1024,512]{2,1,0:T(8,128)(2,1)S(1)}, bf16[2,1024,512]{2,1,0:T(8,128)(2,1)}, u32[]{:S(2)}) copy-start(bf16[2,1024,512]{2,1,0:T(8,128)(2,1)} %param.16) | copy-start | bytes 6291460
  21.6 7.5 %copy-start.1 = (bf16[1280,640]{1,0:T(8,128)(2,1)S(1)}, bf16[1280,640]{1,0:T(8,128)(2,1)}, u32[]{:S(2)}) copy-start(bf16[1280,640]{1,0:T(8,128)(2,1)} %param.15) | copy-start | bytes 4915204
  21.6 7.5 %copy-start.2 = (bf16[2,768,384]{2,1,0:T(8,128)(2,1)S(1)}, bf16[2,768,384]{2,1,0:T(8,128)(2,1)}, u32[]{:S(2)}) copy-start(bf16[2,768,384]{2,1,0:T(8,128)(2,1)} %param.17) | copy-start | bytes 3538948
  21.7 7.5 %copy-start.4 = (s32[1,1,512]{2,1,0:T(1,128)S(1)}, s32[1,1,512]{2,1,0:T(1,128)}, u32[]{:S(2)}) copy-start(s32[1,1,512]{2,1,0:T(1,128)} %param.11) | copy-start | bytes 6148
  27.6 7.2 %collective-permute-start.7 = (bf16[2,2,25,8,128]{4,3,2,1,0:T(8,128)(2,1)S(1)}, bf16[2,2,25,8,128]{4,3,2,1,0:T(8,128)(2,1)S(1)}, u32[]{:S(2)}, u32[]{:S(2)}) collective-permute-start(bf16[2,2,25,8,128]{4,3,2,1,0:T(8,128)(2,1)S(1)} %slice.53), channel_id=1, source_target_pairs={{0,1},{1,0},{2,3},{3,2},{4,5},{5,4},{6,7},{7,6},{8,9},{9,8},{10,11... | collective-permute-start | bytes 614408 | tf_op jit(solution)/shard_map/ppermute | solution.py:442
  28.2 6.5 %collective-permute-start.6 = (bf16[2,2,25,8,128]{4,3,2,1,0:T(8,128)(2,1)S(1)}, bf16[2,2,25,8,128]{4,3,2,1,0:T(8,128)(2,1)S(1)}, u32[]{:S(2)}, u32[]{:S(2)}) collective-permute-start(bf16[2,2,25,8,128]{4,3,2,1,0:T(8,128)(2,1)S(1)} %slice.52), channel_id=1, source_target_pairs={{0,2},{1,3},{2,0},{3,1},{4,6},{5,7},{6,4},{7,5},{8,10},{9,11},{10,... | collective-permute-start | bytes 614408 | tf_op jit(solution)/shard_map/ppermute | solution.py:442
  29.1 5.6 %copy-start.3 = (s32[1,1,512]{2,1,0:T(1,128)S(1)}, s32[1,1,512]{2,1,0:T(1,128)}, u32[]{:S(2)}) copy-start(s32[1,1,512]{2,1,0:T(1,128)} %param.12) | copy-start | bytes 6148
  49.4 9.7 %collective-permute-start.8 = (bf16[4,25,8,128]{3,2,1,0:T(8,128)(2,1)S(1)}, bf16[4,25,8,128]{3,2,1,0:T(8,128)(2,1)S(1)}, u32[]{:S(2)}, u32[]{:S(2)}) collective-permute-start(bf16[4,25,8,128]{3,2,1,0:T(8,128)(2,1)S(1)} %get-tuple-element.21), channel_id=1, source_target_pairs={{0,1},{1,0},{2,3},{3,2},{4,5},{5,4},{6,7},{7,6},{8,9},{9,8},{10,11... | collective-permute-start | bytes 614408 | tf_op jit(solution)/shard_map/ppermute | solution.py:442
  50.6 9.0 %collective-permute-start.10 = (bf16[4,25,8,128]{3,2,1,0:T(8,128)(2,1)S(1)}, bf16[4,25,8,128]{3,2,1,0:T(8,128)(2,1)S(1)}, u32[]{:S(2)}, u32[]{:S(2)}) collective-permute-start(bf16[4,25,8,128]{3,2,1,0:T(8,128)(2,1)S(1)} %get-tuple-element.22), channel_id=1, source_target_pairs={{0,3},{1,2},{2,1},{3,0},{4,7},{5,6},{6,5},{7,4},{8,11},{9,10},{10,... | collective-permute-start | bytes 614408 | tf_op jit(solution)/shard_map/ppermute | solution.py:442
  52.1 8.9 %collective-permute-start.9 = (bf16[4,25,8,128]{3,2,1,0:T(8,128)(2,1)S(1)}, bf16[4,25,8,128]{3,2,1,0:T(8,128)(2,1)S(1)}, u32[]{:S(2)}, u32[]{:S(2)}) collective-permute-start(bf16[4,25,8,128]{3,2,1,0:T(8,128)(2,1)S(1)} %get-tuple-element.23), channel_id=1, source_target_pairs={{0,2},{1,3},{2,0},{3,1},{4,6},{5,7},{6,4},{7,5},{8,10},{9,11},{10,... | collective-permute-start | bytes 614408 | tf_op jit(solution)/shard_map/ppermute | solution.py:442
  59.0 8.1 %collective-permute-start.14 = (bf16[25,8,128]{2,1,0:T(8,128)(2,1)S(1)}, bf16[25,8,128]{2,1,0:T(8,128)(2,1)S(1)}, u32[]{:S(2)}, u32[]{:S(2)}) collective-permute-start(bf16[25,8,128]{2,1,0:T(8,128)(2,1)S(1)} %slice_bitcast_fusion.1), channel_id=1, source_target_pairs={{0,16},{16,0},{1,17},{17,1},{2,18},{18,2},{3,19},{19,3},{4,20},{20... | collective-permute-start | bytes 153608 | tf_op jit(solution)/shard_map/ppermute | solution.py:442
  61.1 6.0 %collective-permute-start.11 = (bf16[25,8,128]{2,1,0:T(8,128)(2,1)S(1)}, bf16[25,8,128]{2,1,0:T(8,128)(2,1)S(1)}, u32[]{:S(2)}, u32[]{:S(2)}) collective-permute-start(bf16[25,8,128]{2,1,0:T(8,128)(2,1)S(1)} %get-tuple-element.24), channel_id=1, source_target_pairs={{0,4},{1,5},{2,6},{3,7},{4,0},{5,1},{6,2},{7,3},{8,12},{9,13},{10,... | collective-permute-start | bytes 153608 | tf_op jit(solution)/shard_map/ppermute | solution.py:442
  63.7 6.0 %collective-permute-start.13 = (bf16[25,8,128]{2,1,0:T(8,128)(2,1)S(1)}, bf16[25,8,128]{2,1,0:T(8,128)(2,1)S(1)}, u32[]{:S(2)}, u32[]{:S(2)}) collective-permute-start(bf16[25,8,128]{2,1,0:T(8,128)(2,1)S(1)} %get-tuple-element.25), channel_id=1, source_target_pairs={{0,12},{1,13},{2,14},{3,15},{4,8},{5,9},{6,10},{7,11},{8,4},{9,5},... | collective-permute-start | bytes 153608 | tf_op jit(solution)/shard_map/ppermute | solution.py:442
  67.1 5.0 %collective-permute-start.12 = (bf16[25,8,128]{2,1,0:T(8,128)(2,1)S(1)}, bf16[25,8,128]{2,1,0:T(8,128)(2,1)S(1)}, u32[]{:S(2)}, u32[]{:S(2)}) collective-permute-start(bf16[25,8,128]{2,1,0:T(8,128)(2,1)S(1)} %get-tuple-element.26), channel_id=1, source_target_pairs={{0,8},{1,9},{2,10},{3,11},{4,12},{5,13},{6,14},{7,15},{8,0},{9,1},... | collective-permute-start | bytes 153608 | tf_op jit(solution)/shard_map/ppermute | solution.py:442

commit v4 on v3

--- a/solution.py
+++ b/solution.py
@@ -28,9 +28,12 @@
     return lax.broadcasted_iota(jnp.int32, shape, axis)
 
 
-def flatten(wig_ref, flat):
-    flat[:, 384:512] = jnp.zeros((wig_ref.shape[0], 128), BF16)
-    flat[:, 0 : wig_ref.shape[1]] = wig_ref[...]
+def flatten(wig_ref, tall, flat_ref):
+    width = wig_ref.shape[0]
+    tall[480:512, :] = jnp.zeros((32, tall.shape[1]), F32)
+    tall[width // 8 * 8 : 480, :] = jnp.zeros((480 - width // 8 * 8, tall.shape[1]), F32)
+    tall[0:width, :] = wig_ref[...].astype(F32)
+    flat_ref[...] = tall[...].T.astype(BF16)
 
 
 def picked(operand, wanted):
@@ -41,8 +44,8 @@
     return jnp.where(same_edge, spread, 0.0).reshape(edges // GROUP, GROUP, LANES)
 
 
-def expand_fwd_kernel(wig_ref, fwd_ref, flat):
-    flatten(wig_ref, flat)
+def expand_fwd_kernel(wig_ref, fwd_ref, flat, tall):
+    flatten(wig_ref, tall, flat)
     slot = iota((256, LANES), 1) // GROUP
 
     def fwd_step(pair, unused):
@@ -59,8 +62,11 @@
     lax.fori_loop(0, K_PAD // 16, fwd_step, 0)
 
 
-def expand_bwd_kernel(wig_ref, bwd_ref, flat):
-    flatten(wig_ref, flat)
+def expand_bwd_kernel(flat_ref, bwd_ref, flat):
+    dest = iota((512, 512), 1)
+    origin = jnp.where(dest < ROWS * COEF, dest % ROWS * COEF + dest // ROWS, -1)
+    move = jnp.where(iota((512, 512), 0) == origin, 1.0, 0.0).astype(BF16)
+    flat[...] = jnp.dot(flat_ref[...], move, preferred_element_type=F32).astype(BF16)
     slot = iota((1, LANES), 1) // GROUP
     row_of = jnp.full(slot.shape, -1, jnp.int32)
     for n, k in enumerate(SLOTS):
@@ -70,8 +76,9 @@
         parts = []
         for odd in range(2):
             j = pair * 2 + odd
-            wanted = jnp.where((row_of >= 0) & (j < COEF), row_of * COEF + j, -1)
-            parts.append(picked(flat[...], wanted))
+            base = jnp.minimum(j * ROWS // 128, 2) * 128
+            wanted = jnp.where((row_of >= 0) & (j < COEF), row_of + j * ROWS - base, -1)
+            parts.append(picked(flat[:, pl.ds(aligned(base, 128), 256)], wanted))
         start = aligned(pair * 16, 16)
         bwd_ref[:, pl.ds(start, 16), :] = jnp.concatenate(parts, axis=1).astype(BF16)
         return unused
@@ -92,19 +99,17 @@
             table[:, start : start + C] = column.astype(BF16)
 
 
-def source_hot(ids_ref, chunk, atoms):
-    ids = ids_ref[:, pl.ds(aligned(chunk * CHUNK, CHUNK), CHUNK)]
+def source_hot(ids, atoms):
     place = ids ^ (lax.axis_index("row") * 8)
-    return place == iota((atoms, CHUNK), 0)
-
-
-def target_hot(ids_ref, chunk, atoms):
-    ids = ids_ref[:, pl.ds(aligned(chunk * CHUNK, CHUNK), CHUNK)]
+    return place == iota((atoms, ids.shape[1]), 0)
+
+
+def target_hot(ids, atoms):
     place = ids ^ (lax.axis_index("col") * 8)
     block = place // 8
     outer = atoms // (8 * INNER)
     place = ((block % INNER) * outer + block // INNER) * 8 + place % 8
-    return place == iota((atoms, CHUNK), 0)
+    return place == iota((atoms, ids.shape[1]), 0)
 
 
 def store_pair(packed, slot, first, second):
@@ -164,31 +169,25 @@
     return w_ref[:, :, half].reshape(-1, width)
 
 
-def source_forward_kernel(*refs):
-    ids_ref, feats_ref, rot_ref = refs[:3]
-    w_refs, outs = refs[3:6], refs[6:9]
-    table, packed, lefts = refs[9], refs[10], refs[11:]
+def source_forward_kernel(count_pieces, *refs):
+    ids_ref, rot_ref = refs[:2]
+    w_refs, pieces = refs[2:5], refs[5 : 5 + count_pieces]
+    refs = refs[5 + count_pieces :]
+    outs, table, packed, lefts = refs[:3], refs[3], refs[4], refs[5:]
     edges = ids_ref.shape[1]
-    blocks = [lambda kind, j, b=b: feats_ref[b, j] for b in range(feats_ref.shape[0])]
+    blocks = [lambda kind, j, piece=piece: piece[j] for piece in pieces]
     fill_table(blocks, table, 1)
     clear_rows(packed, COEF + 1)
 
-    def chunk_step(chunk, unused):
-        gather_atoms(source_hot(ids_ref, chunk, table.shape[0]), table, packed)
-
-        for g in range(0, CHUNK // GROUP, 2):
-            at = chunk * (CHUNK // GROUP) + g
-            pair = [rotate_group(rot_ref, at + n, packed, g + n) for n in range(2)]
-            top, low = slice(g * 8, g * 8 + 16), slice(CHUNK + g * 8, CHUNK + g * 8 + 16)
-            store_forward(lambda k: pair_row(*pair, k), lefts, top, low)
-        for n in range(3):
-            rows = lefts[n].shape[0]
-            outs[n][pl.ds(aligned(chunk * rows, rows), rows), :] = jnp.dot(
-                lefts[n][...], half_weight(w_refs[n], n, 0), preferred_element_type=F32
-            )
-        return unused
-
-    lax.fori_loop(0, edges // CHUNK, chunk_step, 0)
+    gather_atoms(source_hot(ids_ref[...], table.shape[0]), table, packed)
+    for g in range(0, edges // GROUP, 2):
+        pair = [rotate_group(rot_ref, g + n, packed, g + n) for n in range(2)]
+        top, low = slice(g * 8, g * 8 + 16), slice(edges + g * 8, edges + g * 8 + 16)
+        store_forward(lambda k: pair_row(*pair, k), lefts, top, low)
+    for n in range(3):
+        outs[n][...] = jnp.dot(
+            lefts[n][...], half_weight(w_refs[n], n, 0), preferred_element_type=F32
+        )
 
 
 def y_slices(start):
@@ -199,48 +198,51 @@
     return out
 
 
-def back_half(half, chunk, lefts, w_refs, rot_ref, packed, edge_grad):
-    for n, count, slot in ((0, 5, 0), (1, 4, 6), (2, 3, 14)):
+def back_half(half, first, lefts, w_refs, rot_ref, packed, edge_grad):
+    groups = packed.shape[0]
+    count = groups * GROUP
+    edges = lefts[0].shape[0]
+    for n, terms, slot in ((0, 5, 0), (1, 4, 6), (2, 3, 14)):
         width = w_refs[n].shape[-1]
-        rows = CHUNK if n == 0 else 2 * CHUNK
-        here = pl.ds(aligned(chunk * rows, rows), rows)
-        for k in range(0, count, 2):
-            until = min(k + 2, count)
-            if n == 0:
-                weight = w_refs[n][k:until, half].reshape(-1, width)
-                value = lax.dot_general(lefts[n][here, :], weight, NT, preferred_element_type=F32)
-            else:
-                real = w_refs[n][0, k:until, half].reshape(-1, width)
-                imag = w_refs[n][1, k:until, half].reshape(-1, width)
-                value = lax.dot_general(
-                    lefts[n][here, :width], real, NT, preferred_element_type=F32
-                ) + lax.dot_general(lefts[n][here, width:], imag, NT, preferred_element_type=F32)
-            for sign in range(rows // CHUNK):
-                part = value[sign * CHUNK : (sign + 1) * CHUNK]
-                first = part[:, :C]
-                second = part[:, C:] if until - k == 2 else jnp.zeros_like(first)
-                store_pair(packed, slot + sign * (count + 1) // 2 * 2 + k, first, second)
-
-    at = chunk * (CHUNK // GROUP)
-    for g in range(0, CHUNK // GROUP, 2):
+        for k in range(0, terms, 2):
+            until = min(k + 2, terms)
+            for sign in range(1 if n == 0 else 2):
+                here = pl.ds(aligned(first + sign * edges, GROUP), count)
+                if n == 0:
+                    weight = w_refs[n][k:until, half].reshape(-1, width)
+                    value = lax.dot_general(
+                        lefts[n][here, :], weight, NT, preferred_element_type=F32
+                    )
+                else:
+                    real = w_refs[n][0, k:until, half].reshape(-1, width)
+                    imag = w_refs[n][1, k:until, half].reshape(-1, width)
+                    value = lax.dot_general(
+                        lefts[n][here, :width], real, NT, preferred_element_type=F32
+                    ) + lax.dot_general(
+                        lefts[n][here, width:], imag, NT, preferred_element_type=F32
+                    )
+                one = value[:, :C]
+                two = value[:, C:] if until - k == 2 else jnp.zeros_like(one)
+                store_pair(packed, slot + sign * (terms + 1) // 2 * 2 + k, one, two)
+
+    at = first // GROUP
+    for g in range(0, groups, 2):
         pair = [rotate_group(rot_ref, at + g + n, packed, g + n) for n in range(2)]
+        rows = pl.ds(aligned(first + g * 8, 16), 16)
         for j in range(COEF):
-            edge_grad[g * 8 : g * 8 + 16, j * C : (j + 1) * C] = pair_row(*pair, j).astype(BF16)
-
-
-def scatter_atoms(hot, count_ref, chunk, edge_grad, total):
-    valid = chunk * CHUNK + iota(hot.shape, 1) < count_ref[0, 0]
+            edge_grad[rows, j * C : (j + 1) * C] = pair_row(*pair, j).astype(BF16)
+
+
+def scatter_atoms(hot, count_ref, edge_grad, out_ref):
+    valid = iota(hot.shape, 1) < count_ref[0, 0]
     hot = jnp.where(hot & valid, 1.0, 0.0).astype(BF16)
-    step = total.shape[1] // 5
-    for n in range(5):
-        here = slice(n * step, (n + 1) * step)
-        total[:, here] += jnp.dot(hot, edge_grad[:, here], preferred_element_type=F32)
-
-
-def write_blocks(total, out_ref):
-    for j in range(COEF):
-        for b in range(out_ref.shape[0]):
-            out_ref[b, j] = total[b * 8 : b * 8 + 8, j * C : (j + 1) * C].astype(out_ref.dtype)
+    for j in range(0, COEF, 2):
+        until = min(j + 2, COEF)
+        total = jnp.dot(hot, edge_grad[:, j * C : until * C], preferred_element_type=F32)
+        for n in range(until - j):
+            for b in range(out_ref.shape[0]):
+                block = total[b * 8 : b * 8 + 8, n * C : (n + 1) * C]
+                out_ref[b, j + n] = block.astype(out_ref.dtype)
 
 
 def target_kernel(count_pieces, *refs):
@@ -251,7 +253,7 @@
     lefts, out_ref = refs[:3], refs[3]
     table, packed = refs[4], refs[5]
     forward_lefts, cots, ys, packed_back = refs[6:9], refs[9], refs[10:13], refs[13]
-    edge_grad, total = refs[14], refs[15]
+    edge_grad = refs[14]
     edges = ids_ref.shape[1]
     blocks = []
     for piece in pieces:
@@ -260,10 +262,10 @@
     fill_table(blocks, table, 2)
     clear_rows(packed, COEF + 1)
     clear_rows(packed_back, len(SLOTS))
-    total[...] = jnp.zeros_like(total)
 
     def chunk_step(chunk, unused):
-        hot = target_hot(ids_ref, chunk, table.shape[0])
+        first = aligned(chunk * CHUNK, CHUNK)
+        hot = target_hot(ids_ref[:, pl.ds(first, CHUNK)], table.shape[0])
         gather_atoms(hot, table, packed)
 
         for g in range(0, CHUNK // GROUP, 2):
@@ -274,10 +276,13 @@
             for k in range(ROWS):
                 cots[top, k * C : (k + 1) * C] = pair_row(*pair, k, 1).astype(BF16)
         for n in range(3):
-            rows = forward_lefts[n].shape[0]
-            ys[n][...] = sources[n][pl.ds(aligned(chunk * rows, rows), rows), :] + jnp.dot(
+            value = jnp.dot(
                 forward_lefts[n][...], half_weight(w_refs[n], n, 1), preferred_element_type=F32
             )
+            for sign in range(1 if n == 0 else 2):
+                here = slice(sign * CHUNK, (sign + 1) * CHUNK)
+                there = pl.ds(aligned(first + sign * edges, CHUNK), CHUNK)
+                ys[n][here, :] = sources[n][there, :] + value[here]
 
         def gate(i, unused):
             start = aligned(i * 16, 16)
@@ -297,26 +302,22 @@
                 dotted = dotted + cot[k] * y_at(k)
             grads = [cot[0] * (gating + y0 * slope) + dotted * slope]
             grads += [gating * cot[k] for k in range(1, ROWS)]
-            zero_row = aligned(chunk * CHUNK + start, 16)
-            top_row = aligned(chunk * 2 * CHUNK + start, 16)
-            low_row = aligned(chunk * 2 * CHUNK + CHUNK + start, 16)
-            store_backward(grads, lefts, zero_row, top_row, low_row)
+            store_backward(grads, lefts, first + start)
             return unused
 
-        lax.fori_loop(0, CHUNK // 16, gate, 0, unroll=4)
-        back_half(1, chunk, lefts, w_refs, bwd_ref, packed_back, edge_grad)
-        hot = target_hot(ids_ref, chunk, table.shape[0])
-        scatter_atoms(hot, count_ref, chunk, edge_grad, total)
+        lax.fori_loop(0, CHUNK // 16, gate, 0, unroll=True)
+        back_half(1, first, lefts, w_refs, bwd_ref, packed_back, edge_grad)
         return unused
 
     lax.fori_loop(0, edges // CHUNK, chunk_step, 0)
-    write_blocks(total, out_ref)
-
-
-def store_backward(value, lefts, zero_row, top_row, low_row):
+    scatter_atoms(target_hot(ids_ref[...], table.shape[0]), count_ref, edge_grad, out_ref)
+
+
+def store_backward(value, lefts, row):
+    top = pl.ds(aligned(row, 16), 16)
+    low = pl.ds(aligned(row + lefts[0].shape[0], 16), 16)
     for k in range(5):
-        lefts[0][pl.ds(zero_row, 16), k * C : (k + 1) * C] = value[k].astype(BF16)
-    top, low = pl.ds(top_row, 16), pl.ds(low_row, 16)
+        lefts[0][top, k * C : (k + 1) * C] = value[k].astype(BF16)
     for left, base, count in ((lefts[1], 5, 4), (lefts[2], 13, 3)):
         for n in range(count):
             a, b = value[base + n], value[base + count + n]
@@ -331,17 +332,10 @@
 def source_back_kernel(*refs):
     ids_ref, count_ref, bwd_ref = refs[:3]
     w_refs, lefts, out_ref = refs[3:6], refs[6:9], refs[9]
-    packed, edge_grad, total = refs[10:]
+    packed, edge_grad = refs[10:]
     clear_rows(packed, len(SLOTS))
-    total[...] = jnp.zeros_like(total)
-
-    def chunk_step(chunk, unused):
-        back_half(0, chunk, lefts, w_refs, bwd_ref, packed, edge_grad)
-        scatter_atoms(source_hot(ids_ref, chunk, total.shape[0]), count_ref, chunk, edge_grad, total)
-        return unused
-
-    lax.fori_loop(0, lefts[0].shape[0] // CHUNK, chunk_step, 0)
-    write_blocks(total, out_ref)
+    back_half(0, 0, lefts, w_refs, bwd_ref, packed, edge_grad)
+    scatter_atoms(source_hot(ids_ref[...], out_ref.shape[0] * 8), count_ref, edge_grad, out_ref)
 
 
 IN_VMEM = pl.BlockSpec(memory_space=pltpu.VMEM)
@@ -377,29 +371,36 @@
     return [(s, dtype) for s in shapes]
 
 
-def packed_shape(kinds):
-    return (CHUNK // GROUP, LANES, kinds * C)
+def packed_shape(edges, kinds):
+    return (edges // GROUP, LANES, kinds * C)
 
 
 PUSH = 2 * 65536
 
 
-def expand(kernel, rows, wig):
-    edges = wig.shape[0]
-    outs = arrays([(edges // GROUP, rows, LANES)], BF16)
-    return call(kernel, [wig], outs, [((edges, 512), BF16)], 6, PUSH * edges * 40)[0]
-
-
-def source_forward(ids, feats, rot, weights):
+def expand_fwd(tall):
+    edges = tall.shape[1]
+    outs = arrays([(edges // GROUP, K_PAD, LANES), (edges, 512)], BF16)
+    scratch = [((512, edges), F32)]
+    return call(expand_fwd_kernel, [tall], outs, scratch, 6, PUSH * edges * 20)
+
+
+def expand_bwd(flat):
+    edges = flat.shape[0]
+    outs = arrays([(edges // GROUP, J_PAD, LANES)], BF16)
+    return call(expand_bwd_kernel, [flat], outs, [((edges, 512), BF16)], 6, PUSH * edges * 30)[0]
+
+
+def source_forward(ids, pieces, rot, weights):
     edges = ids.shape[1]
-    scratch = [((feats.shape[0] * 8, COEF * C), BF16), (packed_shape(1), BF16)]
-    scratch += typed(left_shapes(CHUNK), BF16)
+    scratch = [((len(pieces) * 8, COEF * C), BF16), (packed_shape(edges, 1), BF16)]
+    scratch += typed(left_shapes(edges), BF16)
     return call(
-        source_forward_kernel,
-        [ids, feats, rot, *weights],
+        functools.partial(source_forward_kernel, len(pieces)),
+        [ids, rot, *weights, *pieces],
         arrays(y_shapes(edges), F32),
         scratch,
-        12,
+        14,
         PUSH * edges * 64,
     )
 
@@ -408,10 +409,10 @@
     edges = ids.shape[1]
     blocks = sum(p.shape[0] for p in pieces)
     outs = arrays(left_shapes(edges), BF16) + arrays([(blocks, COEF, 8, C)], BF16)
-    scratch = [((blocks * 8, 2 * COEF * C), BF16), (packed_shape(2), BF16)]
+    scratch = [((blocks * 8, 2 * COEF * C), BF16), (packed_shape(CHUNK, 2), BF16)]
     scratch += typed(left_shapes(CHUNK), BF16) + [((CHUNK, ROWS * C), BF16)]
-    scratch += typed(y_shapes(CHUNK), F32) + [(packed_shape(1), BF16)]
-    scratch += [((CHUNK, COEF * C), BF16), ((blocks * 8, COEF * C), F32)]
+    scratch += typed(y_shapes(CHUNK), F32) + [(packed_shape(CHUNK, 1), BF16)]
+    scratch += [((edges, COEF * C), BF16)]
     return call(
         functools.partial(target_kernel, len(pieces)),
         [ids, count, fwd, bwd, *weights, *sources, *pieces],
@@ -424,15 +425,15 @@
 
 
 def source_back(ids, count, bwd, weights, lefts, blocks):
-    scratch = [(packed_shape(1), BF16)]
-    scratch += [((CHUNK, COEF * C), BF16), ((blocks * 8, COEF * C), F32)]
+    edges = lefts[0].shape[0]
+    scratch = [(packed_shape(edges, 1), BF16), ((edges, COEF * C), BF16)]
     return call(
         source_back_kernel,
         [ids, count, bwd, *weights, *lefts],
         arrays([(blocks, COEF, 8, C)], BF16),
         scratch,
         12,
-        PUSH * lefts[0].shape[0] * 70,
+        PUSH * edges * 70,
         1,
     )[0]
 
@@ -447,17 +448,21 @@
     inner, outer = INNER, cols // INNER
     feats = node_feats.transpose(1, 0, 2)
     own = jnp.stack([feats, grad_out.transpose(1, 0, 2)])
-    line = [own]
+    line = []
     for d in range(1, outer):
         line.append(exchange(own, "col", inner * d))
+    own_first = exchange(own, "col", 1)
+    own_second = exchange(own, "col", 2)
+    source_feats = [feats] + [exchange(feats, "row", d) for d in range(1, rows)]
     line = jnp.stack(line)
-    source_feats = [feats] + [exchange(feats, "row", d) for d in range(1, rows)]
-    source_feats = jnp.stack(source_feats)
     first = exchange(line, "col", 1)
     second = exchange(line, "col", 2)
-    far_first = exchange(first[: outer // 2], "col", 2)
-    far_second = exchange(second[outer // 2 :], "col", 1)
-    pieces = [line, first, second, far_first, far_second]
+    cut = outer // 2
+    far_first = exchange(first[:cut], "col", 2)
+    rest = jnp.concatenate([own_second[None], second[cut:]])
+    far_second = exchange(rest, "col", 1)
+    pieces = [own[None], line, own_first[None], first, own_second[None], second]
+    pieces += [far_second[:1], far_first, far_second[1:]]
 
     weights = (
         w_zero.reshape(5, 2, C, 5 * C),
@@ -466,8 +471,8 @@
     )
     edges = edge_src.shape[-1]
     src, tgt = edge_src.reshape(1, edges), edge_tgt.reshape(1, edges)
-    fwd = expand(expand_fwd_kernel, K_PAD, wigner[0, 0])
-    bwd = expand(expand_bwd_kernel, J_PAD, wigner[0, 0])
+    fwd, flat = expand_fwd(wigner[0, 0].T)
+    bwd = expand_bwd(flat)
     sources = source_forward(src, source_feats, fwd, weights)
     *lefts, tile_tgt = target_work(tgt, count, fwd, bwd, weights, sources, pieces)
     tile_src = source_back(src, count, bwd, weights, lefts, rows)

time: 73 us -> 74.3 us (1.018)
  waiting for transfers between devices: 13.3 us -> 18 us
  Pallas kernels: 35.3 us -> 31.9 us
    ppermute x15 -> x17, waiting for transfers between devices: 13.3 us -> 18 us  [exchange(): return lax.ppermute(value, axis, [(i, i ^ distance) for i in range(size)])]
    pallas_call x5, Pallas kernels: 35.3 us -> 31.9 us  [call(): pl.pallas_call(kernel, in_specs=[IN_SMEM if n == scalar else IN_VMEM for...]
    another operation x2 -> x1, other arithmetic: 0.9 us -> 0.04 us  [step(): line = jnp.stack(line)]
    another operation x0 -> x1, other arithmetic: none -> 0.84 us  [step(): own = jnp.stack([feats, grad_out.transpose(1, 0, 2)])]
    ppermute x15 -> x17, starting transfers between devices: 20.3 us -> 20.5 us  [exchange(): return lax.ppermute(value, axis, [(i, i ^ distance) for i in range(size)])]
  transfers between devices with their start and end apart: 15 -> 17, of which waited for: 7 -> 8; matrix products, arithmetic and copies ran while one was open for 2% -> 0% of each run, Pallas kernels for 28% -> 25%
where the time goes in v4:
time: 74.3 us; the launch traced here: 74.1 us
  Pallas kernels  31.9 us (43%)
  starting transfers between devices  20.5 us (28%)
  waiting for transfers between devices  18 us (24%)
  other arithmetic  1.69 us (2%)
  local copies, waits for them, and re-layouts  1.17 us (2%)
  between operations  0.88 us (1%)
    pallas_call x5, Pallas kernels, call(): pl.pallas_call(kernel, in_specs=[IN_SMEM if n == scalar else IN_VMEM for...  31.9 us
    ppermute x17, starting transfers between devices, exchange(): return lax.ppermute(value, axis, [(i, i ^ distance) for i in range(size)])  20.5 us
    ppermute x17, waiting for transfers between devices, exchange(): return lax.ppermute(value, axis, [(i, i ^ distance) for i in range(size)])  18 us
  transfers between devices with their start and end apart: 17, of which 8 were waited for; matrix products, arithmetic and copies ran while one was open for 0% of the time, Pallas kernels for 25%

profile of v4, /device:TPU:0, one launch (start us, length us, event | category | flops | bytes accessed | tf_op | source)
XLA Modules:
  0.0 74.1 jit_solution(11275613526569846655)
XLA Ops:
  0.0 0.8 %pad_maximum_fusion.2 = (bf16[2,25,8,128]{3,2,1,0:T(8,128)(2,1)S(1)}, bf16[1,2,25,8,128]{4,3,2,1,0:T(8,128)(2,1)S(1)}) fusion(bf16[1,25,8,128]{3,2,1,0:T(8,128)(2,1)} %bitcast.72, bf16[1,25,8,128]{3,2,1,0:T(8,128)(2,1)} %bitcast.52), kind=kLoop, calls=%fused_computation.10 | loop fusion | flops 51200 | bytes 307200 | tf_op jit(solution)/shard_map/stack | solution.py:450
  0.8 5.1 %collective-permute-start.3 = (bf16[2,25,8,128]{3,2,1,0:T(8,128)(2,1)S(1)}, bf16[2,25,8,128]{3,2,1,0:T(8,128)(2,1)S(1)}, u32[]{:S(2)}, u32[]{:S(2)}) collective-permute-start(bf16[2,25,8,128]{3,2,1,0:T(8,128)(2,1)S(1)} %get-tuple-element.33), channel_id=1, source_target_pairs={{0,12},{1,13},{2,14},{3,15},{4,8},{5,9},{6,10},{7,11},{8,4},{9,5},... | collective-permute-start | bytes 307208 | tf_op jit(solution)/shard_map/ppermute | solution.py:443
  6.0 0.0 collective-permute-start.2
  6.0 0.6 collective-permute-start.1
  6.6 1.6 %collective-permute-start.4 = (bf16[2,25,8,128]{3,2,1,0:T(8,128)(2,1)S(1)}, bf16[2,25,8,128]{3,2,1,0:T(8,128)(2,1)S(1)}, u32[]{:S(2)}, u32[]{:S(2)}) collective-permute-start(bf16[2,25,8,128]{3,2,1,0:T(8,128)(2,1)S(1)} %get-tuple-element.33), channel_id=1, source_target_pairs={{0,1},{1,0},{2,3},{3,2},{4,5},{5,4},{6,7},{7,6},{8,9},{9,8},{10,11... | collective-permute-start | bytes 307208 | tf_op jit(solution)/shard_map/ppermute | solution.py:443
  8.3 1.5 %collective-permute-start.6 = (bf16[2,25,8,128]{3,2,1,0:T(8,128)(2,1)S(1)}, bf16[2,25,8,128]{3,2,1,0:T(8,128)(2,1)S(1)}, u32[]{:S(2)}, u32[]{:S(2)}) collective-permute-start(bf16[2,25,8,128]{3,2,1,0:T(8,128)(2,1)S(1)} %get-tuple-element.33), channel_id=1, source_target_pairs={{0,2},{1,3},{2,0},{3,1},{4,6},{5,7},{6,4},{7,5},{8,10},{9,11},{10,... | collective-permute-start | bytes 307208 | tf_op jit(solution)/shard_map/ppermute | solution.py:443
  10.4 0.0 collective-permute-done.3
  10.5 0.1 collective-permute-start
  10.5 4.1 %collective-permute-done.2 = bf16[2,25,8,128]{3,2,1,0:T(8,128)(2,1)S(1)} collective-permute-done((bf16[2,25,8,128]{3,2,1,0:T(8,128)(2,1)S(1)}, bf16[2,25,8,128]{3,2,1,0:T(8,128)(2,1)S(1)}, u32[]{:S(2)}, u32[]{:S(2)}) %collective-permute-start.2) | collective-permute-done | bytes 102432 | tf_op jit(solution)/shard_map/ppermute | solution.py:443
  14.6 0.0 collective-permute-done.1
  14.7 1.6 %collective-permute-start.7 = (bf16[3,2,25,8,128]{4,3,2,1,0:T(8,128)(2,1)S(1)}, bf16[3,2,25,8,128]{4,3,2,1,0:T(8,128)(2,1)S(1)}, u32[]{:S(2)}, u32[]{:S(2)}) collective-permute-start(bf16[3,2,25,8,128]{4,3,2,1,0:T(8,128)(2,1)S(1)} %pad_maximum_fusion.refs_11_), channel_id=1, source_target_pairs={{0,2},{1,3},{2,0},{3,1},{4,6},{5,7},{6,4},{7,5},{8,10},{9,11},{10,... | collective-permute-start | bytes 921608 | tf_op jit(solution)/shard_map/ppermute | solution.py:443
  16.2 1.0 %copy-done.4 = bf16[1,1,512,475]{2,3,1,0:T(8,128)(2,1)S(1)} copy-done((bf16[1,1,512,475]{2,3,1,0:T(8,128)(2,1)S(1)}, bf16[1,1,512,475]{2,3,1,0:T(8,128)(2,1)}, u32[]{:S(2)}) %copy-start.4) | copy-done | bytes 486424
  17.3 3.4 %shard_map.91 = (bf16[64,160,256]{2,1,0:T(8,128)(2,1)S(1)}, bf16[512,512]{1,0:T(8,128)(2,1)S(1)}) custom-call(bf16[475,512]{1,0:T(8,128)(2,1)S(1)} %bitcast.64), custom_call_target="tpu_custom_call" | custom-call | flops 1342177280 | bytes 6253568 | tf_op jit(solution)/shard_map/pallas_call | solution.py:347
  20.7 0.0 copy-start
  20.7 0.0 copy-start.1
  20.7 0.0 copy-start.2
  20.7 0.0 copy-start.3
  20.7 0.0 copy-start.6
  20.7 4.6 %shard_map.92.refs_3_.refs_2_ = bf16[64,208,256]{2,1,0:T(8,128)(2,1)S(1)} custom-call(bf16[512,512]{1,0:T(8,128)(2,1)S(1)} %get-tuple-element.15.flat_ref), custom_call_target="tpu_custom_call" | custom-call | flops 2013265920 | bytes 7340032 | tf_op jit(solution)/shard_map/pallas_call | solution.py:347
  25.3 1.6 %collective-permute-start.5 = (bf16[3,2,25,8,128]{4,3,2,1,0:T(8,128)(2,1)S(1)}, bf16[3,2,25,8,128]{4,3,2,1,0:T(8,128)(2,1)S(1)}, u32[]{:S(2)}, u32[]{:S(2)}) collective-permute-start(bf16[3,2,25,8,128]{4,3,2,1,0:T(8,128)(2,1)S(1)} %pad_maximum_fusion.refs_11_), channel_id=1, source_target_pairs={{0,1},{1,0},{2,3},{3,2},{4,5},{5,4},{6,7},{7,6},{8,9},{9,8},{10,11... | collective-permute-start | bytes 921608 | tf_op jit(solution)/shard_map/ppermute | solution.py:443
  26.9 0.0 collective-permute-done.7.refs_15_
  26.9 0.0 collective-permute-done.6
  26.9 0.6 collective-permute-start.8
  27.5 0.0 collective-permute-done.refs_6_
  27.6 0.0 copy-start.5
  27.6 5.1 %shard_map.93 = (f32[512,640]{1,0:T(8,128)S(1)}, f32[1024,512]{1,0:T(8,128)S(1)}, f32[1024,384]{1,0:T(8,128)S(1)}) custom-call(s32[1,512]{1,0:T(1,128)S(1)} %bitcast.67, bf16[64,160,256]{2,1,0:T(8,128)(2,1)S(1)} %get-tuple-element.14.refs_1_.refs_2_, bf16[5,2,128,640]{3,2,1,0:T(8,128)(2,1)S(1)} %bitcast.58, bf16[2,4,2,128,512]{4,3,2,1,0:T(8,128)(2,1)S(1)} %bitcast.55, ...), custom_call_target="tpu_custom_call" | custom-call | flops 4294967296 | bytes 15243264 | tf_op jit(solution)/shard_map/pallas_call | solution.py:347
  32.7 2.9 %collective-permute-done.5.refs_13_ = bf16[3,2,25,8,128]{4,3,2,1,0:T(8,128)(2,1)S(1)} collective-permute-done((bf16[3,2,25,8,128]{4,3,2,1,0:T(8,128)(2,1)S(1)}, bf16[3,2,25,8,128]{4,3,2,1,0:T(8,128)(2,1)S(1)}, u32[]{:S(2)}, u32[]{:S(2)}) %collective-permute-start.5) | collective-permute-done | bytes 307232 | tf_op jit(solution)/shard_map/ppermute | solution.py:443
  35.5 0.6 collective-permute-start.9
  36.1 1.7 %collective-permute-done.8 = bf16[2,2,25,8,128]{4,3,2,1,0:T(8,128)(2,1)S(1)} collective-permute-done((bf16[2,2,25,8,128]{4,3,2,1,0:T(8,128)(2,1)S(1)}, bf16[2,2,25,8,128]{4,3,2,1,0:T(8,128)(2,1)S(1)}, u32[]{:S(2)}, u32[]{:S(2)}) %collective-permute-start.8) | collective-permute-done | bytes 204832 | tf_op jit(solution)/shard_map/ppermute | solution.py:443
  37.8 0.0 collective-permute-done.4
  37.8 3.5 %collective-permute-done.9.refs_17_ = bf16[2,2,25,8,128]{4,3,2,1,0:T(8,128)(2,1)S(1)} collective-permute-done((bf16[2,2,25,8,128]{4,3,2,1,0:T(8,128)(2,1)S(1)}, bf16[2,2,25,8,128]{4,3,2,1,0:T(8,128)(2,1)S(1)}, u32[]{:S(2)}, u32[]{:S(2)}) %collective-permute-start.9) | collective-permute-done | bytes 204832 | tf_op jit(solution)/shard_map/ppermute | solution.py:443
  41.4 13.5 %shard_map.94 = (bf16[512,640]{1,0:T(8,128)(2,1)S(1)}, bf16[1024,1024]{1,0:T(8,128)(2,1)S(1)}, bf16[1024,768]{1,0:T(8,128)(2,1)S(1)}, bf16[16,25,8,128]{3,2,1,0:T(8,128)(2,1)S(1)}) custom-call(s32[1,512]{1,0:T(1,128)S(1)} %bitcast.66, s32[1,1]{1,0:T(1,128)S(6)} %copy.10.refs_1_, bf16[64,160,256]{2,1,0:T(8,128)(2,1)S(1)} %get-tuple-element.14.refs_1_.refs_2_, ...), custom_call_target="tpu_custom_call" | custom-call | flops 10737418240 | bytes 28739588 | tf_op jit(solution)/shard_map/pallas_call | solution.py:347
  54.9 1.6 %collective-permute-start.10 = (bf16[4,25,8,128]{3,2,1,0:T(8,128)(2,1)S(1)}, bf16[4,25,8,128]{3,2,1,0:T(8,128)(2,1)S(1)}, u32[]{:S(2)}, u32[]{:S(2)}) collective-permute-start(bf16[4,25,8,128]{3,2,1,0:T(8,128)(2,1)S(1)} %get-tuple-element.25), channel_id=1, source_target_pairs={{0,1},{1,0},{2,3},{3,2},{4,5},{5,4},{6,7},{7,6},{8,9},{9,8},{10,11... | collective-permute-start | bytes 614408 | tf_op jit(solution)/shard_map/ppermute | solution.py:443
  56.5 0.5 collective-permute-start.12
  57.0 1.5 %collective-permute-start.11 = (bf16[4,25,8,128]{3,2,1,0:T(8,128)(2,1)S(1)}, bf16[4,25,8,128]{3,2,1,0:T(8,128)(2,1)S(1)}, u32[]{:S(2)}, u32[]{:S(2)}) collective-permute-start(bf16[4,25,8,128]{3,2,1,0:T(8,128)(2,1)S(1)} %get-tuple-element.27), channel_id=1, source_target_pairs={{0,2},{1,3},{2,0},{3,1},{4,6},{5,7},{6,4},{7,5},{8,10},{9,11},{10,... | collective-permute-start | bytes 614408 | tf_op jit(solution)/shard_map/ppermute | solution.py:443
  58.5 5.3 %shard_map.95 = bf16[2,25,8,128]{3,2,1,0:T(8,128)(2,1)S(1)} custom-call(s32[1,512]{1,0:T(1,128)S(1)} %bitcast.68, s32[1,1]{1,0:T(1,128)S(6)} %copy.10.refs_1_, bf16[64,208,256]{2,1,0:T(8,128)(2,1)S(1)} %shard_map.92.refs_3_.refs_2_, bf16[5,2,128,640]{3,2,1,0:T(8,128)(2,1)S(1)} %bitcast.60, bf16[2,4,2,128,512]{4,3,2,1,0:T(8,128)(2,1)S(1)} %bitcast.57, ...), custom_call_target="tpu_custom_call" | custom-call | flops 4697620480 | bytes 16160772 | tf_op jit(solution)/shard_map/pallas_call | solution.py:347
  63.8 0.1 collective-permute-start.16
  63.9 0.0 collective-permute-done.10
  63.9 0.0 collective-permute-done.12
  63.9 1.0 %collective-permute-done.11 = bf16[4,25,8,128]{3,2,1,0:T(8,128)(2,1)S(1)} collective-permute-done((bf16[4,25,8,128]{3,2,1,0:T(8,128)(2,1)S(1)}, bf16[4,25,8,128]{3,2,1,0:T(8,128)(2,1)S(1)}, u32[]{:S(2)}, u32[]{:S(2)}) %collective-permute-start.11) | collective-permute-done | bytes 204832 | tf_op jit(solution)/shard_map/ppermute | solution.py:443
  64.9 0.1 fusion.7
  65.0 0.5 collective-permute-start.13
  65.5 2.1 %collective-permute-start.15 = (bf16[25,8,128]{2,1,0:T(8,128)(2,1)S(1)}, bf16[25,8,128]{2,1,0:T(8,128)(2,1)S(1)}, u32[]{:S(2)}, u32[]{:S(2)}) collective-permute-start(bf16[25,8,128]{2,1,0:T(8,128)(2,1)S(1)} %get-tuple-element.29), channel_id=1, source_target_pairs={{0,12},{1,13},{2,14},{3,15},{4,8},{5,9},{6,10},{7,11},{8,4},{9,5},... | collective-permute-start | bytes 153608 | tf_op jit(solution)/shard_map/ppermute | solution.py:443
  67.7 0.9 %collective-permute-start.14 = (bf16[25,8,128]{2,1,0:T(8,128)(2,1)S(1)}, bf16[25,8,128]{2,1,0:T(8,128)(2,1)S(1)}, u32[]{:S(2)}, u32[]{:S(2)}) collective-permute-start(bf16[25,8,128]{2,1,0:T(8,128)(2,1)S(1)} %get-tuple-element.30), channel_id=1, source_target_pairs={{0,8},{1,9},{2,10},{3,11},{4,12},{5,13},{6,14},{7,15},{8,0},{9,1},... | collective-permute-start | bytes 153608 | tf_op jit(solution)/shard_map/ppermute | solution.py:443
  68.6 0.6 collective-permute-done.13
  69.2 2.2 %collective-permute-done.15 = bf16[25,8,128]{2,1,0:T(8,128)(2,1)S(1)} collective-permute-done((bf16[25,8,128]{2,1,0:T(8,128)(2,1)S(1)}, bf16[25,8,128]{2,1,0:T(8,128)(2,1)S(1)}, u32[]{:S(2)}, u32[]{:S(2)}) %collective-permute-start.15) | collective-permute-done | bytes 51232 | tf_op jit(solution)/shard_map/ppermute | solution.py:443
  71.5 1.9 %collective-permute-done.14 = bf16[25,8,128]{2,1,0:T(8,128)(2,1)S(1)} collective-permute-done((bf16[25,8,128]{2,1,0:T(8,128)(2,1)S(1)}, bf16[25,8,128]{2,1,0:T(8,128)(2,1)S(1)}, u32[]{:S(2)}, u32[]{:S(2)}) %collective-permute-start.14) | collective-permute-done | bytes 51232 | tf_op jit(solution)/shard_map/ppermute | solution.py:443
  73.4 0.7 fusion.5
  (16 shorter events, 0.2 us)
Async XLA Ops:
  0.8 9.6 %collective-permute-start.3 = (bf16[2,25,8,128]{3,2,1,0:T(8,128)(2,1)S(1)}, bf16[2,25,8,128]{3,2,1,0:T(8,128)(2,1)S(1)}, u32[]{:S(2)}, u32[]{:S(2)}) collective-permute-start(bf16[2,25,8,128]{3,2,1,0:T(8,128)(2,1)S(1)} %get-tuple-element.33), channel_id=1, source_target_pairs={{0,12},{1,13},{2,14},{3,15},{4,8},{5,9},{6,10},{7,11},{8,4},{9,5},... | collective-permute-start | bytes 307208 | tf_op jit(solution)/shard_map/ppermute | solution.py:443
  6.0 8.6 %collective-permute-start.2 = (bf16[2,25,8,128]{3,2,1,0:T(8,128)(2,1)S(1)}, bf16[2,25,8,128]{3,2,1,0:T(8,128)(2,1)S(1)}, u32[]{:S(2)}, u32[]{:S(2)}) collective-permute-start(bf16[2,25,8,128]{3,2,1,0:T(8,128)(2,1)S(1)} %get-tuple-element.33), channel_id=1, source_target_pairs={{0,8},{1,9},{2,10},{3,11},{4,12},{5,13},{6,14},{7,15},{8,0},{9,1},... | collective-permute-start | bytes 307208 | tf_op jit(solution)/shard_map/ppermute | solution.py:443
  6.0 8.6 %collective-permute-start.1 = (bf16[2,25,8,128]{3,2,1,0:T(8,128)(2,1)S(1)}, bf16[2,25,8,128]{3,2,1,0:T(8,128)(2,1)S(1)}, u32[]{:S(2)}, u32[]{:S(2)}) collective-permute-start(bf16[2,25,8,128]{3,2,1,0:T(8,128)(2,1)S(1)} %get-tuple-element.33), channel_id=1, source_target_pairs={{0,4},{1,5},{2,6},{3,7},{4,0},{5,1},{6,2},{7,3},{8,12},{9,13},{10,... | collective-permute-start | bytes 307208 | tf_op jit(solution)/shard_map/ppermute | solution.py:443
  6.6 31.2 %collective-permute-start.4 = (bf16[2,25,8,128]{3,2,1,0:T(8,128)(2,1)S(1)}, bf16[2,25,8,128]{3,2,1,0:T(8,128)(2,1)S(1)}, u32[]{:S(2)}, u32[]{:S(2)}) collective-permute-start(bf16[2,25,8,128]{3,2,1,0:T(8,128)(2,1)S(1)} %get-tuple-element.33), channel_id=1, source_target_pairs={{0,1},{1,0},{2,3},{3,2},{4,5},{5,4},{6,7},{7,6},{8,9},{9,8},{10,11... | collective-permute-start | bytes 307208 | tf_op jit(solution)/shard_map/ppermute | solution.py:443
  8.3 18.6 %collective-permute-start.6 = (bf16[2,25,8,128]{3,2,1,0:T(8,128)(2,1)S(1)}, bf16[2,25,8,128]{3,2,1,0:T(8,128)(2,1)S(1)}, u32[]{:S(2)}, u32[]{:S(2)}) collective-permute-start(bf16[2,25,8,128]{3,2,1,0:T(8,128)(2,1)S(1)} %get-tuple-element.33), channel_id=1, source_target_pairs={{0,2},{1,3},{2,0},{3,1},{4,6},{5,7},{6,4},{7,5},{8,10},{9,11},{10,... | collective-permute-start | bytes 307208 | tf_op jit(solution)/shard_map/ppermute | solution.py:443
  10.5 17.1 %collective-permute-start = (bf16[25,8,128]{2,1,0:T(8,128)(2,1)}, bf16[25,8,128]{2,1,0:T(8,128)(2,1)S(1)}, u32[]{:S(2)}, u32[]{:S(2)}) collective-permute-start(bf16[25,8,128]{2,1,0:T(8,128)(2,1)} %bitcast.53), channel_id=1, source_target_pairs={{0,16},{16,0},{1,17},{17,1},{2,18},{18,2},{3,19},{19,3},{4,20},{20... | collective-permute-start | bytes 153608 | tf_op jit(solution)/shard_map/ppermute | solution.py:443
  14.7 12.2 %collective-permute-start.7 = (bf16[3,2,25,8,128]{4,3,2,1,0:T(8,128)(2,1)S(1)}, bf16[3,2,25,8,128]{4,3,2,1,0:T(8,128)(2,1)S(1)}, u32[]{:S(2)}, u32[]{:S(2)}) collective-permute-start(bf16[3,2,25,8,128]{4,3,2,1,0:T(8,128)(2,1)S(1)} %pad_maximum_fusion.refs_11_), channel_id=1, source_target_pairs={{0,2},{1,3},{2,0},{3,1},{4,6},{5,7},{6,4},{7,5},{8,10},{9,11},{10,... | collective-permute-start | bytes 921608 | tf_op jit(solution)/shard_map/ppermute | solution.py:443
  16.2 1.0 %copy-start.4 = (bf16[1,1,512,475]{2,3,1,0:T(8,128)(2,1)S(1)}, bf16[1,1,512,475]{2,3,1,0:T(8,128)(2,1)}, u32[]{:S(2)}) copy-start(bf16[1,1,512,475]{2,3,1,0:T(8,128)(2,1)} %param.14) | copy-start | bytes 1459204
  20.7 6.8 %copy-start = (bf16[8,25,128]{2,0,1:T(8,128)(2,1)S(1)}, bf16[8,25,128]{2,0,1:T(8,128)(2,1)}, u32[]{:S(2)}) copy-start(bf16[8,25,128]{2,0,1:T(8,128)(2,1)} %param.9) | copy-start | bytes 153604
  20.7 6.8 %copy-start.1 = (bf16[2,1024,512]{2,1,0:T(8,128)(2,1)S(1)}, bf16[2,1024,512]{2,1,0:T(8,128)(2,1)}, u32[]{:S(2)}) copy-start(bf16[2,1024,512]{2,1,0:T(8,128)(2,1)} %param.16) | copy-start | bytes 6291460
  20.7 6.8 %copy-start.2 = (bf16[1280,640]{1,0:T(8,128)(2,1)S(1)}, bf16[1280,640]{1,0:T(8,128)(2,1)}, u32[]{:S(2)}) copy-start(bf16[1280,640]{1,0:T(8,128)(2,1)} %param.15) | copy-start | bytes 4915204
  20.7 6.8 %copy-start.3 = (bf16[2,768,384]{2,1,0:T(8,128)(2,1)S(1)}, bf16[2,768,384]{2,1,0:T(8,128)(2,1)}, u32[]{:S(2)}) copy-start(bf16[2,768,384]{2,1,0:T(8,128)(2,1)} %param.17) | copy-start | bytes 3538948
  20.7 6.8 %copy-start.6 = (s32[1,1,512]{2,1,0:T(1,128)S(1)}, s32[1,1,512]{2,1,0:T(1,128)}, u32[]{:S(2)}) copy-start(s32[1,1,512]{2,1,0:T(1,128)} %param.11) | copy-start | bytes 6148
  25.3 10.2 %collective-permute-start.5 = (bf16[3,2,25,8,128]{4,3,2,1,0:T(8,128)(2,1)S(1)}, bf16[3,2,25,8,128]{4,3,2,1,0:T(8,128)(2,1)S(1)}, u32[]{:S(2)}, u32[]{:S(2)}) collective-permute-start(bf16[3,2,25,8,128]{4,3,2,1,0:T(8,128)(2,1)S(1)} %pad_maximum_fusion.refs_11_), channel_id=1, source_target_pairs={{0,1},{1,0},{2,3},{3,2},{4,5},{5,4},{6,7},{7,6},{8,9},{9,8},{10,11... | collective-permute-start | bytes 921608 | tf_op jit(solution)/shard_map/ppermute | solution.py:443
  26.9 10.9 %collective-permute-start.8 = (bf16[2,2,25,8,128]{4,3,2,1,0:T(8,128)(2,1)S(1)}, bf16[2,2,25,8,128]{4,3,2,1,0:T(8,128)(2,1)S(1)}, u32[]{:S(2)}, u32[]{:S(2)}) collective-permute-start(bf16[2,2,25,8,128]{4,3,2,1,0:T(8,128)(2,1)S(1)} %pad_maximum_fusion.1), channel_id=1, source_target_pairs={{0,1},{1,0},{2,3},{3,2},{4,5},{5,4},{6,7},{7,6},{8,9},{9,8},{10,11... | collective-permute-start | bytes 614408 | tf_op jit(solution)/shard_map/ppermute | solution.py:443
  27.6 13.8 %copy-start.5 = (s32[1,1,512]{2,1,0:T(1,128)S(1)}, s32[1,1,512]{2,1,0:T(1,128)}, u32[]{:S(2)}) copy-start(s32[1,1,512]{2,1,0:T(1,128)} %param.12) | copy-start | bytes 6148
  35.5 5.8 %collective-permute-start.9 = (bf16[2,2,25,8,128]{4,3,2,1,0:T(8,128)(2,1)S(1)}, bf16[2,2,25,8,128]{4,3,2,1,0:T(8,128)(2,1)S(1)}, u32[]{:S(2)}, u32[]{:S(2)}) collective-permute-start(bf16[2,2,25,8,128]{4,3,2,1,0:T(8,128)(2,1)S(1)} %slice.62), channel_id=1, source_target_pairs={{0,2},{1,3},{2,0},{3,1},{4,6},{5,7},{6,4},{7,5},{8,10},{9,11},{10,... | collective-permute-start | bytes 614408 | tf_op jit(solution)/shard_map/ppermute | solution.py:443
  54.9 9.0 %collective-permute-start.10 = (bf16[4,25,8,128]{3,2,1,0:T(8,128)(2,1)S(1)}, bf16[4,25,8,128]{3,2,1,0:T(8,128)(2,1)S(1)}, u32[]{:S(2)}, u32[]{:S(2)}) collective-permute-start(bf16[4,25,8,128]{3,2,1,0:T(8,128)(2,1)S(1)} %get-tuple-element.25), channel_id=1, source_target_pairs={{0,1},{1,0},{2,3},{3,2},{4,5},{5,4},{6,7},{7,6},{8,9},{9,8},{10,11... | collective-permute-start | bytes 614408 | tf_op jit(solution)/shard_map/ppermute | solution.py:443
  56.5 7.4 %collective-permute-start.12 = (bf16[4,25,8,128]{3,2,1,0:T(8,128)(2,1)S(1)}, bf16[4,25,8,128]{3,2,1,0:T(8,128)(2,1)S(1)}, u32[]{:S(2)}, u32[]{:S(2)}) collective-permute-start(bf16[4,25,8,128]{3,2,1,0:T(8,128)(2,1)S(1)} %get-tuple-element.26), channel_id=1, source_target_pairs={{0,3},{1,2},{2,1},{3,0},{4,7},{5,6},{6,5},{7,4},{8,11},{9,10},{10,... | collective-permute-start | bytes 614408 | tf_op jit(solution)/shard_map/ppermute | solution.py:443
  57.0 8.0 %collective-permute-start.11 = (bf16[4,25,8,128]{3,2,1,0:T(8,128)(2,1)S(1)}, bf16[4,25,8,128]{3,2,1,0:T(8,128)(2,1)S(1)}, u32[]{:S(2)}, u32[]{:S(2)}) collective-permute-start(bf16[4,25,8,128]{3,2,1,0:T(8,128)(2,1)S(1)} %get-tuple-element.27), channel_id=1, source_target_pairs={{0,2},{1,3},{2,0},{3,1},{4,6},{5,7},{6,4},{7,5},{8,10},{9,11},{10,... | collective-permute-start | bytes 614408 | tf_op jit(solution)/shard_map/ppermute | solution.py:443
  63.8 4.8 %collective-permute-start.16 = (bf16[25,8,128]{2,1,0:T(8,128)(2,1)S(1)}, bf16[25,8,128]{2,1,0:T(8,128)(2,1)S(1)}, u32[]{:S(2)}, u32[]{:S(2)}) collective-permute-start(bf16[25,8,128]{2,1,0:T(8,128)(2,1)S(1)} %slice_bitcast_fusion.1), channel_id=1, source_target_pairs={{0,16},{16,0},{1,17},{17,1},{2,18},{18,2},{3,19},{19,3},{4,20},{20... | collective-permute-start | bytes 153608 | tf_op jit(solution)/shard_map/ppermute | solution.py:443
  65.0 4.2 %collective-permute-start.13 = (bf16[25,8,128]{2,1,0:T(8,128)(2,1)S(1)}, bf16[25,8,128]{2,1,0:T(8,128)(2,1)S(1)}, u32[]{:S(2)}, u32[]{:S(2)}) collective-permute-start(bf16[25,8,128]{2,1,0:T(8,128)(2,1)S(1)} %get-tuple-element.28), channel_id=1, source_target_pairs={{0,4},{1,5},{2,6},{3,7},{4,0},{5,1},{6,2},{7,3},{8,12},{9,13},{10,... | collective-permute-start | bytes 153608 | tf_op jit(solution)/shard_map/ppermute | solution.py:443
  65.5 5.9 %collective-permute-start.15 = (bf16[25,8,128]{2,1,0:T(8,128)(2,1)S(1)}, bf16[25,8,128]{2,1,0:T(8,128)(2,1)S(1)}, u32[]{:S(2)}, u32[]{:S(2)}) collective-permute-start(bf16[25,8,128]{2,1,0:T(8,128)(2,1)S(1)} %get-tuple-element.29), channel_id=1, source_target_pairs={{0,12},{1,13},{2,14},{3,15},{4,8},{5,9},{6,10},{7,11},{8,4},{9,5},... | collective-permute-start | bytes 153608 | tf_op jit(solution)/shard_map/ppermute | solution.py:443
  67.7 5.7 %collective-permute-start.14 = (bf16[25,8,128]{2,1,0:T(8,128)(2,1)S(1)}, bf16[25,8,128]{2,1,0:T(8,128)(2,1)S(1)}, u32[]{:S(2)}, u32[]{:S(2)}) collective-permute-start(bf16[25,8,128]{2,1,0:T(8,128)(2,1)S(1)} %get-tuple-element.30), channel_id=1, source_target_pairs={{0,8},{1,9},{2,10},{3,11},{4,12},{5,13},{6,14},{7,15},{8,0},{9,1},... | collective-permute-start | bytes 153608 | tf_op jit(solution)/shard_map/ppermute | solution.py:443

commit v5 on v4

--- a/solution.py
+++ b/solution.py
@@ -59,7 +59,7 @@
         fwd_ref[:, pl.ds(start, 16), :] = jnp.concatenate(parts, axis=1).astype(BF16)
         return unused
 
-    lax.fori_loop(0, K_PAD // 16, fwd_step, 0)
+    lax.fori_loop(0, K_PAD // 16, fwd_step, 0, unroll=True)
 
 
 def expand_bwd_kernel(flat_ref, bwd_ref, flat):
@@ -83,7 +83,7 @@
         bwd_ref[:, pl.ds(start, 16), :] = jnp.concatenate(parts, axis=1).astype(BF16)
         return unused
 
-    lax.fori_loop(0, J_PAD // 16, bwd_step, 0)
+    lax.fori_loop(0, J_PAD // 16, bwd_step, 0, unroll=True)
 
 
 def aligned(value, by):
@@ -309,7 +309,7 @@
         back_half(1, first, lefts, w_refs, bwd_ref, packed_back, edge_grad)
         return unused
 
-    lax.fori_loop(0, edges // CHUNK, chunk_step, 0)
+    lax.fori_loop(0, edges // CHUNK, chunk_step, 0, unroll=True)
     scatter_atoms(target_hot(ids_ref[...], table.shape[0]), count_ref, edge_grad, out_ref)
 
 

time: 74.3 us -> 70.6 us (0.950)
  Pallas kernels: 31.9 us -> 27.3 us
  starting transfers between devices: 20.5 us -> 22.1 us
    pallas_call x5, Pallas kernels: 31.9 us -> 27.3 us  [call(): pl.pallas_call(kernel, in_specs=[IN_SMEM if n == scalar else IN_VMEM for...]
    ppermute x17, starting transfers between devices: 20.5 us -> 22.1 us  [exchange(): return lax.ppermute(value, axis, [(i, i ^ distance) for i in range(size)])]
  transfers between devices with their start and end apart: 17 -> 17, of which waited for: 8 -> 7; matrix products, arithmetic and copies ran while one was open for 0% -> 0% of each run, Pallas kernels for 25% -> 21%
where the time goes in v5:
time: 70.6 us; the launch traced here: 70.4 us
  Pallas kernels  27.3 us (39%)
  starting transfers between devices  22.1 us (31%)
  waiting for transfers between devices  17.3 us (25%)
  other arithmetic  1.69 us (2%)
  local copies, waits for them, and re-layouts  1.17 us (2%)
  between operations  0.88 us (1%)
    pallas_call x5, Pallas kernels, call(): pl.pallas_call(kernel, in_specs=[IN_SMEM if n == scalar else IN_VMEM for...  27.3 us
    ppermute x17, starting transfers between devices, exchange(): return lax.ppermute(value, axis, [(i, i ^ distance) for i in range(size)])  22.1 us
    ppermute x17, waiting for transfers between devices, exchange(): return lax.ppermute(value, axis, [(i, i ^ distance) for i in range(size)])  17.3 us
  transfers between devices with their start and end apart: 17, of which 7 were waited for; matrix products, arithmetic and copies ran while one was open for 0% of the time, Pallas kernels for 21%

profile of v5, /device:TPU:0, one launch (start us, length us, event | category | flops | bytes accessed | tf_op | source)
XLA Modules:
  0.0 70.4 jit_solution(7467006325881129143)
XLA Ops:
  0.0 0.8 %pad_maximum_fusion.2 = (bf16[2,25,8,128]{3,2,1,0:T(8,128)(2,1)S(1)}, bf16[1,2,25,8,128]{4,3,2,1,0:T(8,128)(2,1)S(1)}) fusion(bf16[1,25,8,128]{3,2,1,0:T(8,128)(2,1)} %bitcast.72, bf16[1,25,8,128]{3,2,1,0:T(8,128)(2,1)} %bitcast.52), kind=kLoop, calls=%fused_computation.10 | loop fusion | flops 51200 | bytes 307200 | tf_op jit(solution)/shard_map/stack | solution.py:450
  0.8 5.1 %collective-permute-start.3 = (bf16[2,25,8,128]{3,2,1,0:T(8,128)(2,1)S(1)}, bf16[2,25,8,128]{3,2,1,0:T(8,128)(2,1)S(1)}, u32[]{:S(2)}, u32[]{:S(2)}) collective-permute-start(bf16[2,25,8,128]{3,2,1,0:T(8,128)(2,1)S(1)} %get-tuple-element.33), channel_id=1, source_target_pairs={{0,12},{1,13},{2,14},{3,15},{4,8},{5,9},{6,10},{7,11},{8,4},{9,5},... | collective-permute-start | bytes 307208 | tf_op jit(solution)/shard_map/ppermute | solution.py:443
  6.0 0.0 collective-permute-start.2
  6.0 0.6 collective-permute-start.1
  6.6 1.6 %collective-permute-start.4 = (bf16[2,25,8,128]{3,2,1,0:T(8,128)(2,1)S(1)}, bf16[2,25,8,128]{3,2,1,0:T(8,128)(2,1)S(1)}, u32[]{:S(2)}, u32[]{:S(2)}) collective-permute-start(bf16[2,25,8,128]{3,2,1,0:T(8,128)(2,1)S(1)} %get-tuple-element.33), channel_id=1, source_target_pairs={{0,1},{1,0},{2,3},{3,2},{4,5},{5,4},{6,7},{7,6},{8,9},{9,8},{10,11... | collective-permute-start | bytes 307208 | tf_op jit(solution)/shard_map/ppermute | solution.py:443
  8.3 1.5 %collective-permute-start.6 = (bf16[2,25,8,128]{3,2,1,0:T(8,128)(2,1)S(1)}, bf16[2,25,8,128]{3,2,1,0:T(8,128)(2,1)S(1)}, u32[]{:S(2)}, u32[]{:S(2)}) collective-permute-start(bf16[2,25,8,128]{3,2,1,0:T(8,128)(2,1)S(1)} %get-tuple-element.33), channel_id=1, source_target_pairs={{0,2},{1,3},{2,0},{3,1},{4,6},{5,7},{6,4},{7,5},{8,10},{9,11},{10,... | collective-permute-start | bytes 307208 | tf_op jit(solution)/shard_map/ppermute | solution.py:443
  10.4 0.0 collective-permute-done.3
  10.5 0.1 collective-permute-start
  10.5 4.1 %collective-permute-done.2 = bf16[2,25,8,128]{3,2,1,0:T(8,128)(2,1)S(1)} collective-permute-done((bf16[2,25,8,128]{3,2,1,0:T(8,128)(2,1)S(1)}, bf16[2,25,8,128]{3,2,1,0:T(8,128)(2,1)S(1)}, u32[]{:S(2)}, u32[]{:S(2)}) %collective-permute-start.2) | collective-permute-done | bytes 102432 | tf_op jit(solution)/shard_map/ppermute | solution.py:443
  14.6 0.0 collective-permute-done.1
  14.7 1.6 %collective-permute-start.7 = (bf16[3,2,25,8,128]{4,3,2,1,0:T(8,128)(2,1)S(1)}, bf16[3,2,25,8,128]{4,3,2,1,0:T(8,128)(2,1)S(1)}, u32[]{:S(2)}, u32[]{:S(2)}) collective-permute-start(bf16[3,2,25,8,128]{4,3,2,1,0:T(8,128)(2,1)S(1)} %pad_maximum_fusion.refs_11_), channel_id=1, source_target_pairs={{0,2},{1,3},{2,0},{3,1},{4,6},{5,7},{6,4},{7,5},{8,10},{9,11},{10,... | collective-permute-start | bytes 921608 | tf_op jit(solution)/shard_map/ppermute | solution.py:443
  16.2 1.0 %copy-done.4 = bf16[1,1,512,475]{2,3,1,0:T(8,128)(2,1)S(1)} copy-done((bf16[1,1,512,475]{2,3,1,0:T(8,128)(2,1)S(1)}, bf16[1,1,512,475]{2,3,1,0:T(8,128)(2,1)}, u32[]{:S(2)}) %copy-start.4) | copy-done | bytes 486424
  17.3 1.9 %shard_map.91 = (bf16[64,160,256]{2,1,0:T(8,128)(2,1)S(1)}, bf16[512,512]{1,0:T(8,128)(2,1)S(1)}) custom-call(bf16[475,512]{1,0:T(8,128)(2,1)S(1)} %bitcast.64), custom_call_target="tpu_custom_call" | custom-call | flops 1342177280 | bytes 6253568 | tf_op jit(solution)/shard_map/pallas_call | solution.py:347
  19.1 0.0 copy-start
  19.1 0.0 copy-start.1
  19.1 0.0 copy-start.2
  19.2 0.0 copy-start.3
  19.2 0.0 copy-start.6
  19.2 2.4 %shard_map.92.refs_3_.refs_2_ = bf16[64,208,256]{2,1,0:T(8,128)(2,1)S(1)} custom-call(bf16[512,512]{1,0:T(8,128)(2,1)S(1)} %get-tuple-element.15.flat_ref), custom_call_target="tpu_custom_call" | custom-call | flops 2013265920 | bytes 7340032 | tf_op jit(solution)/shard_map/pallas_call | solution.py:347
  21.6 1.6 %collective-permute-start.5 = (bf16[3,2,25,8,128]{4,3,2,1,0:T(8,128)(2,1)S(1)}, bf16[3,2,25,8,128]{4,3,2,1,0:T(8,128)(2,1)S(1)}, u32[]{:S(2)}, u32[]{:S(2)}) collective-permute-start(bf16[3,2,25,8,128]{4,3,2,1,0:T(8,128)(2,1)S(1)} %pad_maximum_fusion.refs_11_), channel_id=1, source_target_pairs={{0,1},{1,0},{2,3},{3,2},{4,5},{5,4},{6,7},{7,6},{8,9},{9,8},{10,11... | collective-permute-start | bytes 921608 | tf_op jit(solution)/shard_map/ppermute | solution.py:443
  23.2 0.0 collective-permute-done.7.refs_15_
  23.2 0.0 collective-permute-done.6
  23.2 1.4 %collective-permute-start.8 = (bf16[2,2,25,8,128]{4,3,2,1,0:T(8,128)(2,1)S(1)}, bf16[2,2,25,8,128]{4,3,2,1,0:T(8,128)(2,1)S(1)}, u32[]{:S(2)}, u32[]{:S(2)}) collective-permute-start(bf16[2,2,25,8,128]{4,3,2,1,0:T(8,128)(2,1)S(1)} %pad_maximum_fusion.1), channel_id=1, source_target_pairs={{0,1},{1,0},{2,3},{3,2},{4,5},{5,4},{6,7},{7,6},{8,9},{9,8},{10,11... | collective-permute-start | bytes 614408 | tf_op jit(solution)/shard_map/ppermute | solution.py:443
  24.7 0.0 collective-permute-done.refs_6_
  24.7 0.0 copy-start.5
  24.7 5.1 %shard_map.93 = (f32[512,640]{1,0:T(8,128)S(1)}, f32[1024,512]{1,0:T(8,128)S(1)}, f32[1024,384]{1,0:T(8,128)S(1)}) custom-call(s32[1,512]{1,0:T(1,128)S(1)} %bitcast.67, bf16[64,160,256]{2,1,0:T(8,128)(2,1)S(1)} %get-tuple-element.14.refs_1_.refs_2_, bf16[5,2,128,640]{3,2,1,0:T(8,128)(2,1)S(1)} %bitcast.58, bf16[2,4,2,128,512]{4,3,2,1,0:T(8,128)(2,1)S(1)} %bitcast.55, ...), custom_call_target="tpu_custom_call" | custom-call | flops 4294967296 | bytes 15243264 | tf_op jit(solution)/shard_map/pallas_call | solution.py:347
  29.8 2.0 %collective-permute-done.5.refs_13_ = bf16[3,2,25,8,128]{4,3,2,1,0:T(8,128)(2,1)S(1)} collective-permute-done((bf16[3,2,25,8,128]{4,3,2,1,0:T(8,128)(2,1)S(1)}, bf16[3,2,25,8,128]{4,3,2,1,0:T(8,128)(2,1)S(1)}, u32[]{:S(2)}, u32[]{:S(2)}) %collective-permute-start.5) | collective-permute-done | bytes 307232 | tf_op jit(solution)/shard_map/ppermute | solution.py:443
  31.8 0.6 collective-permute-start.9
  32.4 1.7 %collective-permute-done.8 = bf16[2,2,25,8,128]{4,3,2,1,0:T(8,128)(2,1)S(1)} collective-permute-done((bf16[2,2,25,8,128]{4,3,2,1,0:T(8,128)(2,1)S(1)}, bf16[2,2,25,8,128]{4,3,2,1,0:T(8,128)(2,1)S(1)}, u32[]{:S(2)}, u32[]{:S(2)}) %collective-permute-start.8) | collective-permute-done | bytes 204832 | tf_op jit(solution)/shard_map/ppermute | solution.py:443
  34.1 0.0 collective-permute-done.4
  34.2 3.5 %collective-permute-done.9.refs_17_ = bf16[2,2,25,8,128]{4,3,2,1,0:T(8,128)(2,1)S(1)} collective-permute-done((bf16[2,2,25,8,128]{4,3,2,1,0:T(8,128)(2,1)S(1)}, bf16[2,2,25,8,128]{4,3,2,1,0:T(8,128)(2,1)S(1)}, u32[]{:S(2)}, u32[]{:S(2)}) %collective-permute-start.9) | collective-permute-done | bytes 204832 | tf_op jit(solution)/shard_map/ppermute | solution.py:443
  37.7 12.6 %shard_map.94 = (bf16[512,640]{1,0:T(8,128)(2,1)S(1)}, bf16[1024,1024]{1,0:T(8,128)(2,1)S(1)}, bf16[1024,768]{1,0:T(8,128)(2,1)S(1)}, bf16[16,25,8,128]{3,2,1,0:T(8,128)(2,1)S(1)}) custom-call(s32[1,512]{1,0:T(1,128)S(1)} %bitcast.66, s32[1,1]{1,0:T(1,128)S(6)} %copy.10.refs_1_, bf16[64,160,256]{2,1,0:T(8,128)(2,1)S(1)} %get-tuple-element.14.refs_1_.refs_2_, ...), custom_call_target="tpu_custom_call" | custom-call | flops 10737418240 | bytes 28739588 | tf_op jit(solution)/shard_map/pallas_call | solution.py:347
  50.3 1.6 %collective-permute-start.10 = (bf16[4,25,8,128]{3,2,1,0:T(8,128)(2,1)S(1)}, bf16[4,25,8,128]{3,2,1,0:T(8,128)(2,1)S(1)}, u32[]{:S(2)}, u32[]{:S(2)}) collective-permute-start(bf16[4,25,8,128]{3,2,1,0:T(8,128)(2,1)S(1)} %get-tuple-element.25), channel_id=1, source_target_pairs={{0,1},{1,0},{2,3},{3,2},{4,5},{5,4},{6,7},{7,6},{8,9},{9,8},{10,11... | collective-permute-start | bytes 614408 | tf_op jit(solution)/shard_map/ppermute | solution.py:443
  51.9 0.5 collective-permute-start.12
  52.3 1.5 %collective-permute-start.11 = (bf16[4,25,8,128]{3,2,1,0:T(8,128)(2,1)S(1)}, bf16[4,25,8,128]{3,2,1,0:T(8,128)(2,1)S(1)}, u32[]{:S(2)}, u32[]{:S(2)}) collective-permute-start(bf16[4,25,8,128]{3,2,1,0:T(8,128)(2,1)S(1)} %get-tuple-element.27), channel_id=1, source_target_pairs={{0,2},{1,3},{2,0},{3,1},{4,6},{5,7},{6,4},{7,5},{8,10},{9,11},{10,... | collective-permute-start | bytes 614408 | tf_op jit(solution)/shard_map/ppermute | solution.py:443
  53.8 5.3 %shard_map.95 = bf16[2,25,8,128]{3,2,1,0:T(8,128)(2,1)S(1)} custom-call(s32[1,512]{1,0:T(1,128)S(1)} %bitcast.68, s32[1,1]{1,0:T(1,128)S(6)} %copy.10.refs_1_, bf16[64,208,256]{2,1,0:T(8,128)(2,1)S(1)} %shard_map.92.refs_3_.refs_2_, bf16[5,2,128,640]{3,2,1,0:T(8,128)(2,1)S(1)} %bitcast.60, bf16[2,4,2,128,512]{4,3,2,1,0:T(8,128)(2,1)S(1)} %bitcast.57, ...), custom_call_target="tpu_custom_call" | custom-call | flops 4697620480 | bytes 16160772 | tf_op jit(solution)/shard_map/pallas_call | solution.py:347
  59.2 0.1 collective-permute-start.16
  59.3 0.0 collective-permute-done.10
  59.3 0.0 collective-permute-done.12
  59.3 1.0 %collective-permute-done.11 = bf16[4,25,8,128]{3,2,1,0:T(8,128)(2,1)S(1)} collective-permute-done((bf16[4,25,8,128]{3,2,1,0:T(8,128)(2,1)S(1)}, bf16[4,25,8,128]{3,2,1,0:T(8,128)(2,1)S(1)}, u32[]{:S(2)}, u32[]{:S(2)}) %collective-permute-start.11) | collective-permute-done | bytes 204832 | tf_op jit(solution)/shard_map/ppermute | solution.py:443
  60.3 0.1 fusion.7
  60.4 0.5 collective-permute-start.13
  60.9 3.8 %collective-permute-start.15 = (bf16[25,8,128]{2,1,0:T(8,128)(2,1)S(1)}, bf16[25,8,128]{2,1,0:T(8,128)(2,1)S(1)}, u32[]{:S(2)}, u32[]{:S(2)}) collective-permute-start(bf16[25,8,128]{2,1,0:T(8,128)(2,1)S(1)} %get-tuple-element.29), channel_id=1, source_target_pairs={{0,12},{1,13},{2,14},{3,15},{4,8},{5,9},{6,10},{7,11},{8,4},{9,5},... | collective-permute-start | bytes 153608 | tf_op jit(solution)/shard_map/ppermute | solution.py:443
  64.7 0.0 collective-permute-start.14
  64.7 0.0 collective-permute-done.13
  64.7 2.7 %collective-permute-done.15 = bf16[25,8,128]{2,1,0:T(8,128)(2,1)S(1)} collective-permute-done((bf16[25,8,128]{2,1,0:T(8,128)(2,1)S(1)}, bf16[25,8,128]{2,1,0:T(8,128)(2,1)S(1)}, u32[]{:S(2)}, u32[]{:S(2)}) %collective-permute-start.15) | collective-permute-done | bytes 51232 | tf_op jit(solution)/shard_map/ppermute | solution.py:443
  67.5 2.3 %collective-permute-done.14 = bf16[25,8,128]{2,1,0:T(8,128)(2,1)S(1)} collective-permute-done((bf16[25,8,128]{2,1,0:T(8,128)(2,1)S(1)}, bf16[25,8,128]{2,1,0:T(8,128)(2,1)S(1)}, u32[]{:S(2)}, u32[]{:S(2)}) %collective-permute-start.14) | collective-permute-done | bytes 51232 | tf_op jit(solution)/shard_map/ppermute | solution.py:443
  69.7 0.7 fusion.5
  (16 shorter events, 0.2 us)
Async XLA Ops:
  0.8 9.6 %collective-permute-start.3 = (bf16[2,25,8,128]{3,2,1,0:T(8,128)(2,1)S(1)}, bf16[2,25,8,128]{3,2,1,0:T(8,128)(2,1)S(1)}, u32[]{:S(2)}, u32[]{:S(2)}) collective-permute-start(bf16[2,25,8,128]{3,2,1,0:T(8,128)(2,1)S(1)} %get-tuple-element.33), channel_id=1, source_target_pairs={{0,12},{1,13},{2,14},{3,15},{4,8},{5,9},{6,10},{7,11},{8,4},{9,5},... | collective-permute-start | bytes 307208 | tf_op jit(solution)/shard_map/ppermute | solution.py:443
  6.0 8.6 %collective-permute-start.2 = (bf16[2,25,8,128]{3,2,1,0:T(8,128)(2,1)S(1)}, bf16[2,25,8,128]{3,2,1,0:T(8,128)(2,1)S(1)}, u32[]{:S(2)}, u32[]{:S(2)}) collective-permute-start(bf16[2,25,8,128]{3,2,1,0:T(8,128)(2,1)S(1)} %get-tuple-element.33), channel_id=1, source_target_pairs={{0,8},{1,9},{2,10},{3,11},{4,12},{5,13},{6,14},{7,15},{8,0},{9,1},... | collective-permute-start | bytes 307208 | tf_op jit(solution)/shard_map/ppermute | solution.py:443
  6.0 8.6 %collective-permute-start.1 = (bf16[2,25,8,128]{3,2,1,0:T(8,128)(2,1)S(1)}, bf16[2,25,8,128]{3,2,1,0:T(8,128)(2,1)S(1)}, u32[]{:S(2)}, u32[]{:S(2)}) collective-permute-start(bf16[2,25,8,128]{3,2,1,0:T(8,128)(2,1)S(1)} %get-tuple-element.33), channel_id=1, source_target_pairs={{0,4},{1,5},{2,6},{3,7},{4,0},{5,1},{6,2},{7,3},{8,12},{9,13},{10,... | collective-permute-start | bytes 307208 | tf_op jit(solution)/shard_map/ppermute | solution.py:443
  6.6 27.5 %collective-permute-start.4 = (bf16[2,25,8,128]{3,2,1,0:T(8,128)(2,1)S(1)}, bf16[2,25,8,128]{3,2,1,0:T(8,128)(2,1)S(1)}, u32[]{:S(2)}, u32[]{:S(2)}) collective-permute-start(bf16[2,25,8,128]{3,2,1,0:T(8,128)(2,1)S(1)} %get-tuple-element.33), channel_id=1, source_target_pairs={{0,1},{1,0},{2,3},{3,2},{4,5},{5,4},{6,7},{7,6},{8,9},{9,8},{10,11... | collective-permute-start | bytes 307208 | tf_op jit(solution)/shard_map/ppermute | solution.py:443
  8.3 14.9 %collective-permute-start.6 = (bf16[2,25,8,128]{3,2,1,0:T(8,128)(2,1)S(1)}, bf16[2,25,8,128]{3,2,1,0:T(8,128)(2,1)S(1)}, u32[]{:S(2)}, u32[]{:S(2)}) collective-permute-start(bf16[2,25,8,128]{3,2,1,0:T(8,128)(2,1)S(1)} %get-tuple-element.33), channel_id=1, source_target_pairs={{0,2},{1,3},{2,0},{3,1},{4,6},{5,7},{6,4},{7,5},{8,10},{9,11},{10,... | collective-permute-start | bytes 307208 | tf_op jit(solution)/shard_map/ppermute | solution.py:443
  10.5 14.2 %collective-permute-start = (bf16[25,8,128]{2,1,0:T(8,128)(2,1)}, bf16[25,8,128]{2,1,0:T(8,128)(2,1)S(1)}, u32[]{:S(2)}, u32[]{:S(2)}) collective-permute-start(bf16[25,8,128]{2,1,0:T(8,128)(2,1)} %bitcast.53), channel_id=1, source_target_pairs={{0,16},{16,0},{1,17},{17,1},{2,18},{18,2},{3,19},{19,3},{4,20},{20... | collective-permute-start | bytes 153608 | tf_op jit(solution)/shard_map/ppermute | solution.py:443
  14.7 8.5 %collective-permute-start.7 = (bf16[3,2,25,8,128]{4,3,2,1,0:T(8,128)(2,1)S(1)}, bf16[3,2,25,8,128]{4,3,2,1,0:T(8,128)(2,1)S(1)}, u32[]{:S(2)}, u32[]{:S(2)}) collective-permute-start(bf16[3,2,25,8,128]{4,3,2,1,0:T(8,128)(2,1)S(1)} %pad_maximum_fusion.refs_11_), channel_id=1, source_target_pairs={{0,2},{1,3},{2,0},{3,1},{4,6},{5,7},{6,4},{7,5},{8,10},{9,11},{10,... | collective-permute-start | bytes 921608 | tf_op jit(solution)/shard_map/ppermute | solution.py:443
  16.2 1.0 %copy-start.4 = (bf16[1,1,512,475]{2,3,1,0:T(8,128)(2,1)S(1)}, bf16[1,1,512,475]{2,3,1,0:T(8,128)(2,1)}, u32[]{:S(2)}) copy-start(bf16[1,1,512,475]{2,3,1,0:T(8,128)(2,1)} %param.14) | copy-start | bytes 1459204
  19.1 5.5 %copy-start = (bf16[8,25,128]{2,0,1:T(8,128)(2,1)S(1)}, bf16[8,25,128]{2,0,1:T(8,128)(2,1)}, u32[]{:S(2)}) copy-start(bf16[8,25,128]{2,0,1:T(8,128)(2,1)} %param.9) | copy-start | bytes 153604
  19.1 5.5 %copy-start.1 = (bf16[2,1024,512]{2,1,0:T(8,128)(2,1)S(1)}, bf16[2,1024,512]{2,1,0:T(8,128)(2,1)}, u32[]{:S(2)}) copy-start(bf16[2,1024,512]{2,1,0:T(8,128)(2,1)} %param.16) | copy-start | bytes 6291460
  19.1 5.5 %copy-start.2 = (bf16[1280,640]{1,0:T(8,128)(2,1)S(1)}, bf16[1280,640]{1,0:T(8,128)(2,1)}, u32[]{:S(2)}) copy-start(bf16[1280,640]{1,0:T(8,128)(2,1)} %param.15) | copy-start | bytes 4915204
  19.2 5.5 %copy-start.3 = (bf16[2,768,384]{2,1,0:T(8,128)(2,1)S(1)}, bf16[2,768,384]{2,1,0:T(8,128)(2,1)}, u32[]{:S(2)}) copy-start(bf16[2,768,384]{2,1,0:T(8,128)(2,1)} %param.17) | copy-start | bytes 3538948
  19.2 5.5 %copy-start.6 = (s32[1,1,512]{2,1,0:T(1,128)S(1)}, s32[1,1,512]{2,1,0:T(1,128)}, u32[]{:S(2)}) copy-start(s32[1,1,512]{2,1,0:T(1,128)} %param.11) | copy-start | bytes 6148
  21.6 10.2 %collective-permute-start.5 = (bf16[3,2,25,8,128]{4,3,2,1,0:T(8,128)(2,1)S(1)}, bf16[3,2,25,8,128]{4,3,2,1,0:T(8,128)(2,1)S(1)}, u32[]{:S(2)}, u32[]{:S(2)}) collective-permute-start(bf16[3,2,25,8,128]{4,3,2,1,0:T(8,128)(2,1)S(1)} %pad_maximum_fusion.refs_11_), channel_id=1, source_target_pairs={{0,1},{1,0},{2,3},{3,2},{4,5},{5,4},{6,7},{7,6},{8,9},{9,8},{10,11... | collective-permute-start | bytes 921608 | tf_op jit(solution)/shard_map/ppermute | solution.py:443
  23.2 10.9 %collective-permute-start.8 = (bf16[2,2,25,8,128]{4,3,2,1,0:T(8,128)(2,1)S(1)}, bf16[2,2,25,8,128]{4,3,2,1,0:T(8,128)(2,1)S(1)}, u32[]{:S(2)}, u32[]{:S(2)}) collective-permute-start(bf16[2,2,25,8,128]{4,3,2,1,0:T(8,128)(2,1)S(1)} %pad_maximum_fusion.1), channel_id=1, source_target_pairs={{0,1},{1,0},{2,3},{3,2},{4,5},{5,4},{6,7},{7,6},{8,9},{9,8},{10,11... | collective-permute-start | bytes 614408 | tf_op jit(solution)/shard_map/ppermute | solution.py:443
  24.7 12.9 %copy-start.5 = (s32[1,1,512]{2,1,0:T(1,128)S(1)}, s32[1,1,512]{2,1,0:T(1,128)}, u32[]{:S(2)}) copy-start(s32[1,1,512]{2,1,0:T(1,128)} %param.12) | copy-start | bytes 6148
  31.8 5.8 %collective-permute-start.9 = (bf16[2,2,25,8,128]{4,3,2,1,0:T(8,128)(2,1)S(1)}, bf16[2,2,25,8,128]{4,3,2,1,0:T(8,128)(2,1)S(1)}, u32[]{:S(2)}, u32[]{:S(2)}) collective-permute-start(bf16[2,2,25,8,128]{4,3,2,1,0:T(8,128)(2,1)S(1)} %slice.62), channel_id=1, source_target_pairs={{0,2},{1,3},{2,0},{3,1},{4,6},{5,7},{6,4},{7,5},{8,10},{9,11},{10,... | collective-permute-start | bytes 614408 | tf_op jit(solution)/shard_map/ppermute | solution.py:443
  50.3 9.0 %collective-permute-start.10 = (bf16[4,25,8,128]{3,2,1,0:T(8,128)(2,1)S(1)}, bf16[4,25,8,128]{3,2,1,0:T(8,128)(2,1)S(1)}, u32[]{:S(2)}, u32[]{:S(2)}) collective-permute-start(bf16[4,25,8,128]{3,2,1,0:T(8,128)(2,1)S(1)} %get-tuple-element.25), channel_id=1, source_target_pairs={{0,1},{1,0},{2,3},{3,2},{4,5},{5,4},{6,7},{7,6},{8,9},{9,8},{10,11... | collective-permute-start | bytes 614408 | tf_op jit(solution)/shard_map/ppermute | solution.py:443
  51.9 7.4 %collective-permute-start.12 = (bf16[4,25,8,128]{3,2,1,0:T(8,128)(2,1)S(1)}, bf16[4,25,8,128]{3,2,1,0:T(8,128)(2,1)S(1)}, u32[]{:S(2)}, u32[]{:S(2)}) collective-permute-start(bf16[4,25,8,128]{3,2,1,0:T(8,128)(2,1)S(1)} %get-tuple-element.26), channel_id=1, source_target_pairs={{0,3},{1,2},{2,1},{3,0},{4,7},{5,6},{6,5},{7,4},{8,11},{9,10},{10,... | collective-permute-start | bytes 614408 | tf_op jit(solution)/shard_map/ppermute | solution.py:443
  52.3 8.0 %collective-permute-start.11 = (bf16[4,25,8,128]{3,2,1,0:T(8,128)(2,1)S(1)}, bf16[4,25,8,128]{3,2,1,0:T(8,128)(2,1)S(1)}, u32[]{:S(2)}, u32[]{:S(2)}) collective-permute-start(bf16[4,25,8,128]{3,2,1,0:T(8,128)(2,1)S(1)} %get-tuple-element.27), channel_id=1, source_target_pairs={{0,2},{1,3},{2,0},{3,1},{4,6},{5,7},{6,4},{7,5},{8,10},{9,11},{10,... | collective-permute-start | bytes 614408 | tf_op jit(solution)/shard_map/ppermute | solution.py:443
  59.2 5.5 %collective-permute-start.16 = (bf16[25,8,128]{2,1,0:T(8,128)(2,1)S(1)}, bf16[25,8,128]{2,1,0:T(8,128)(2,1)S(1)}, u32[]{:S(2)}, u32[]{:S(2)}) collective-permute-start(bf16[25,8,128]{2,1,0:T(8,128)(2,1)S(1)} %slice_bitcast_fusion.1), channel_id=1, source_target_pairs={{0,16},{16,0},{1,17},{17,1},{2,18},{18,2},{3,19},{19,3},{4,20},{20... | collective-permute-start | bytes 153608 | tf_op jit(solution)/shard_map/ppermute | solution.py:443
  60.4 4.3 %collective-permute-start.13 = (bf16[25,8,128]{2,1,0:T(8,128)(2,1)S(1)}, bf16[25,8,128]{2,1,0:T(8,128)(2,1)S(1)}, u32[]{:S(2)}, u32[]{:S(2)}) collective-permute-start(bf16[25,8,128]{2,1,0:T(8,128)(2,1)S(1)} %get-tuple-element.28), channel_id=1, source_target_pairs={{0,4},{1,5},{2,6},{3,7},{4,0},{5,1},{6,2},{7,3},{8,12},{9,13},{10,... | collective-permute-start | bytes 153608 | tf_op jit(solution)/shard_map/ppermute | solution.py:443
  60.9 6.6 %collective-permute-start.15 = (bf16[25,8,128]{2,1,0:T(8,128)(2,1)S(1)}, bf16[25,8,128]{2,1,0:T(8,128)(2,1)S(1)}, u32[]{:S(2)}, u32[]{:S(2)}) collective-permute-start(bf16[25,8,128]{2,1,0:T(8,128)(2,1)S(1)} %get-tuple-element.29), channel_id=1, source_target_pairs={{0,12},{1,13},{2,14},{3,15},{4,8},{5,9},{6,10},{7,11},{8,4},{9,5},... | collective-permute-start | bytes 153608 | tf_op jit(solution)/shard_map/ppermute | solution.py:443
  64.7 5.0 %collective-permute-start.14 = (bf16[25,8,128]{2,1,0:T(8,128)(2,1)S(1)}, bf16[25,8,128]{2,1,0:T(8,128)(2,1)S(1)}, u32[]{:S(2)}, u32[]{:S(2)}) collective-permute-start(bf16[25,8,128]{2,1,0:T(8,128)(2,1)S(1)} %get-tuple-element.30), channel_id=1, source_target_pairs={{0,8},{1,9},{2,10},{3,11},{4,12},{5,13},{6,14},{7,15},{8,0},{9,1},... | collective-permute-start | bytes 153608 | tf_op jit(solution)/shard_map/ppermute | solution.py:443
